TPU v7x, 32 devices: a whole 2x2x4 slice. The times are simulated.
32 devices in a mesh: blk: 8 (over z, x), slab: 4 (over y, core).
Axes of the slice: x: 2, y: 2, z: 4, core: 2. Of those that a mesh axis runs over, the one named last changes fastest.
Arguments:
- states_in: float32 [256, 8, 8, 1024], P('blk', None, 'slab'), may hold values from -6 to 6
- region: int32 [8, 1024], P('slab'), may hold values from 0 to 3
- onsite_table: float32 [4, 8, 8], replicated, may hold values from -1.75 to 1.75
- hop_table: float32 [4, 8], replicated, may hold values from 0.05 to 0.3
- coupling_x: float32 [8, 8], replicated, may hold values from -0.875 to 0.875
- coupling_y: float32 [8, 8], replicated, may hold values from -0.875 to 0.875
Outputs:
- states_out: float32 [256, 8, 8, 1024], P('blk', None, 'slab')
- projected: float32 [256, 256], P('blk')
Inputs may be any that keep to these rules, and one draw needn't show every extreme that they name: `region`: material codes.
All inputs are finite; a program needn't handle non-finite values.
Results may differ from a plain program's by a relative error of at most 0.000084.
Values sent between devices are 32-bit elements; how exact they have to be, the bound alone decides.
No kernel may reach another device: no remote copies, remote signals or barrier semaphores. Data moves between devices by JAX's collectives and lax.ppermute only.
A program may use at most 128 MiB of HBM per device.

v0:
```python
import jax
import jax.numpy as jnp
from jax import lax
from jax.sharding import PartitionSpec as P

BANDS = 8
MATERIALS = 4
DEGREE = 4
PANEL = 32


SHIFT = 1.0
SCALE = 3.0


def extended(array, sides, width):
    for axis, dim in sides:
        size, length = (lax.axis_size(axis), array.shape[dim])
        up = [(i, (i + 1) % size) for i in range(size - 1)]
        down = [(j, i) for i, j in up]
        last = lax.slice_in_dim(array, length - width, length, axis=dim)
        leading = lax.slice_in_dim(array, 0, width, axis=dim)
        before = lax.ppermute(last, axis, up)
        after = lax.ppermute(leading, axis, down)
        array = jnp.concatenate([before, array, after], axis=dim)
    return array


def mixing(onsite_table, coupling_x, coupling_y):
    onsite = 0.5 * (onsite_table + jnp.swapaxes(onsite_table, 1, 2))
    blocks = [onsite[material] for material in range(onsite.shape[0])]
    return jnp.concatenate(
        blocks + [0.5 * (coupling_x - coupling_x.T), 0.5 * (coupling_y - coupling_y.T)], axis=1
    )


def masks_of(region):
    codes = jnp.arange(MATERIALS, dtype=jnp.int32)
    return (region[None] == codes[:, None, None]).astype(jnp.float32)


def apply_padded(padded, hop_padded, material_masks, mixing_matrix):
    centre = padded[:, :, 1:-1, 1:-1]
    hop_centre = hop_padded[:, 1:-1, 1:-1]
    kinetic = jnp.zeros_like(centre)
    sides = (
        (padded[:, :, 2:, 1:-1], hop_padded[:, 2:, 1:-1]),
        (padded[:, :, :-2, 1:-1], hop_padded[:, :-2, 1:-1]),
        (padded[:, :, 1:-1, 2:], hop_padded[:, 1:-1, 2:]),
        (padded[:, :, 1:-1, :-2], hop_padded[:, 1:-1, :-2]),
    )
    for field_side, hop_side in sides:
        kinetic = kinetic + (0.5 * (hop_centre + hop_side))[None] * (centre - field_side)
    deriv_rows = 0.5 * (padded[:, :, 2:, 1:-1] - padded[:, :, :-2, 1:-1])
    deriv_cols = 0.5 * (padded[:, :, 1:-1, 2:] - padded[:, :, 1:-1, :-2])
    pieces = [
        material_masks[material][None, None] * centre for material in range(material_masks.shape[0])
    ]
    stacked = jnp.concatenate(pieces + [deriv_rows, deriv_cols], axis=1)
    mixed = jnp.einsum("bc,scxy->sbxy", mixing_matrix, stacked, precision=lax.Precision.HIGHEST)
    return mixed + kinetic


def chebyshev(field, apply_fn):

    def scaled(value):
        return (apply_fn(value) - SHIFT * value) / SCALE

    previous = field
    current = scaled(field)
    for repeat in range(DEGREE - 1):
        previous, current = (current, 2.0 * scaled(current) - previous)
    return current


def inner(left, right):
    return jnp.dot(
        left, right.T, precision=lax.Precision.HIGHEST, preferred_element_type=jnp.float32
    )


def per_device(states_in, region, onsite_table, hop_table, coupling_x, coupling_y):
    mixing_matrix = mixing(onsite_table, coupling_x, coupling_y)
    material_masks = masks_of(region)
    hop_field = jnp.einsum(
        "mb,mxy->bxy", hop_table, material_masks, precision=lax.Precision.HIGHEST
    )
    hop_rows = extended(hop_field, (("slab", 1),), 1)
    hop_padded = jnp.pad(hop_rows, ((0, 0), (0, 0), (1, 1)))

    def apply_rows(field):
        padded = extended(field, (("slab", 2),), 1)
        padded = jnp.pad(padded, ((0, 0), (0, 0), (0, 0), (1, 1)))
        return apply_padded(padded, hop_padded, material_masks, mixing_matrix)

    filtered = chebyshev(states_in, apply_rows)
    block_count = lax.axis_size("blk")
    slab_count = lax.axis_size("slab")
    states_all = filtered.shape[0] * block_count
    row_count = filtered.shape[2]
    width_all = filtered.shape[3]
    entries = float(BANDS * row_count * slab_count * width_all)
    image = apply_rows(filtered)
    cell_states, cell_image = (
        lax.all_to_all(filtered, "blk", split_axis=3, concat_axis=0, tiled=True),
        lax.all_to_all(image, "blk", split_axis=3, concat_axis=0, tiled=True),
    )
    states_flat = cell_states.reshape(states_all, -1)
    image_flat = cell_image.reshape(states_all, -1)
    moment = lax.psum(inner(states_flat, image_flat) / entries, ("blk", "slab"))

    def panel_step(panel, carry):
        basis_rows, factor_rows = carry
        offset = panel * PANEL
        panel_states = lax.dynamic_slice_in_dim(states_flat, offset, PANEL, 0)
        coeffs = lax.psum(inner(basis_rows, panel_states) / entries, ("blk", "slab"))
        residue = panel_states - jnp.dot(
            coeffs.T,
            basis_rows,
            precision=lax.Precision.HIGHEST,
            preferred_element_type=jnp.float32,
        )
        panel_gram = lax.psum(inner(residue, residue) / entries, ("blk", "slab"))
        panel_factor = jnp.linalg.cholesky(panel_gram)
        panel_basis = lax.linalg.triangular_solve(panel_factor, residue, left_side=True, lower=True)
        basis_rows = lax.dynamic_update_slice_in_dim(basis_rows, panel_basis, offset, 0)
        factor_row = lax.dynamic_update_slice_in_dim(coeffs.T, panel_factor, offset, 1)
        factor_rows = lax.dynamic_update_slice_in_dim(factor_rows, factor_row, offset, 0)
        return (basis_rows, factor_rows)

    start_state = (jnp.zeros_like(states_flat), jnp.zeros((states_all, states_all), jnp.float32))
    basis_flat, factor = lax.fori_loop(0, states_all // PANEL, panel_step, start_state)
    half_done = lax.linalg.triangular_solve(factor, moment, left_side=True, lower=True)
    projected = lax.linalg.triangular_solve(factor, half_done.T, left_side=True, lower=True).T
    basis_cells = basis_flat.reshape(cell_states.shape)
    states_out = lax.all_to_all(basis_cells, "blk", split_axis=0, concat_axis=3, tiled=True)
    owned = states_all // block_count
    projected_rows = lax.dynamic_slice_in_dim(projected, lax.axis_index("blk") * owned, owned, 0)
    return (states_out, projected_rows)


def solution(mesh):
    return jax.shard_map(
        per_device,
        mesh=mesh,
        in_specs=(P("blk", None, "slab", None), P("slab", None), P(), P(), P(), P()),
        out_specs=(P("blk", None, "slab", None), P("blk", None)),
        check_vma=False,
    )
```

profile of v0, /device:TPU:0, one launch (start us, length us, event | category | flops | bytes accessed | tf_op | source)
XLA Modules:
  0.0 1216.3 jit_solution(13053189828074453356)
XLA Ops:
  41.7 11.4 multiply_dynamic-update-slice_fusion.19
  59.7 9.4 collective-permute-start.5
  77.0 12.1 multiply_dynamic-update-slice_fusion.14
  90.7 14.7 %collective-permute-start.7 = (f32[32,8,1,1024]{3,1,2,0:T(8,128)S(1)}, f32[32,8,1,1024]{3,1,2,0:T(8,128)S(1)}, u32[]{:S(2)}, u32[]{:S(2)}) collective-permute-start(f32[32,8,1,1024]{3,1,2,0:T(8,128)S(1)} %get-tuple-element.136), channel_id=1, source_target_pairs={{0,1},{1,2},{2,3},{4,5},{5,6},{6,7},{8,9},{9,10},{10,11},{12,13},{... | collective-permute-start | bytes 3145736 | tf_op jit(solution)/shard_map/ppermute | solution.py:23
  116.1 11.7 multiply_dynamic-update-slice_fusion.9
  129.3 11.9 collective-permute-start.9
  152.0 11.7 multiply_dynamic-update-slice_fusion.4
  170.1 8.6 reshape.87
  187.2 12.7 %collective-permute-start.11 = (f32[32,8,1,1024]{3,1,2,0:T(8,128)}, f32[32,8,1,1024]{3,1,2,0:T(8,128)}, u32[]{:S(2)}, u32[]{:S(2)}) collective-permute-start(f32[32,8,1,1024]{3,1,2,0:T(8,128)} %get-tuple-element.132), channel_id=1, source_target_pairs={{0,1},{1,2},{2,3},{4,5},{5,6},{6,7},{8,9},{9,10},{10,11},{12,13},{... | collective-permute-start | bytes 3145736 | tf_op jit(solution)/shard_map/ppermute | solution.py:23
  212.8 11.4 fusion.12
  224.2 7.7 copy.153
  231.9 8.6 reshape.89
  271.1 758.8 %while.19 = (s32[]{:T(128)}, f32[256,2048]{1,0:T(8,128)S(1)}, f32[256,256]{1,0:T(8,128)S(1)}, f32[256,2048]{1,0:T(8,128)}, s32[]{:T(128)}, /*index=5*/s32[]{:T(128)}, s32[]{:T(128)}, s32[]{:T(128)}) while((s32[]{:T(128)}, f32[256,2048]{1,0:T(8,128)S(1)}, f32[256,256]{1,0:T(8,128)S(1)}, f32[256,2048]{1,0:T(8,128)}, s32[]{:T(128)}, ...), condition=%wide.region_5.6_spmd, body=%wide.region_0.5_spmd.sunk | while | flops 453078048 | bytes 6037913 | solution.py:132
  274.2 51.5 %psum.32 = f32[256,32]{0,1:T(8,128)S(1)} all-reduce(f32[256,32]{0,1:T(8,128)S(1)} %fusion.144), channel_id=1, replica_groups=mesh['blk'=8,'slab'=4] {'blk','slab'}, use_global_device_ids=true, to_apply=%region_1.1 | all-reduce | flops 8192 | bytes 65536 | tf_op jit(solution)/shard_map/while/body/eval_jaxpr/psum | solution.py:116
  328.3 39.7 %psum.33 = f32[32,32]{0,1:T(8,128)S(1)} all-reduce(f32[32,32]{0,1:T(8,128)S(1)} %convolution_multiply_fusion.4), channel_id=1, replica_groups=mesh['blk'=8,'slab'=4] {'blk','slab'}, use_global_device_ids=true, to_apply=%region_2.2 | all-reduce | flops 1024 | bytes 8192 | tf_op jit(solution)/shard_map/while/body/eval_jaxpr/psum | solution.py:123
  378.6 40.6 %psum.32 = f32[256,32]{0,1:T(8,128)S(1)} all-reduce(f32[256,32]{0,1:T(8,128)S(1)} %fusion.144), channel_id=1, replica_groups=mesh['blk'=8,'slab'=4] {'blk','slab'}, use_global_device_ids=true, to_apply=%region_1.1 | all-reduce | flops 8192 | bytes 65536 | tf_op jit(solution)/shard_map/while/body/eval_jaxpr/psum | solution.py:116
  421.8 39.7 %psum.33 = f32[32,32]{0,1:T(8,128)S(1)} all-reduce(f32[32,32]{0,1:T(8,128)S(1)} %convolution_multiply_fusion.4), channel_id=1, replica_groups=mesh['blk'=8,'slab'=4] {'blk','slab'}, use_global_device_ids=true, to_apply=%region_2.2 | all-reduce | flops 1024 | bytes 8192 | tf_op jit(solution)/shard_map/while/body/eval_jaxpr/psum | solution.py:123
  472.1 40.6 %psum.32 = f32[256,32]{0,1:T(8,128)S(1)} all-reduce(f32[256,32]{0,1:T(8,128)S(1)} %fusion.144), channel_id=1, replica_groups=mesh['blk'=8,'slab'=4] {'blk','slab'}, use_global_device_ids=true, to_apply=%region_1.1 | all-reduce | flops 8192 | bytes 65536 | tf_op jit(solution)/shard_map/while/body/eval_jaxpr/psum | solution.py:116
  515.3 39.7 %psum.33 = f32[32,32]{0,1:T(8,128)S(1)} all-reduce(f32[32,32]{0,1:T(8,128)S(1)} %convolution_multiply_fusion.4), channel_id=1, replica_groups=mesh['blk'=8,'slab'=4] {'blk','slab'}, use_global_device_ids=true, to_apply=%region_2.2 | all-reduce | flops 1024 | bytes 8192 | tf_op jit(solution)/shard_map/while/body/eval_jaxpr/psum | solution.py:123
  565.7 40.6 %psum.32 = f32[256,32]{0,1:T(8,128)S(1)} all-reduce(f32[256,32]{0,1:T(8,128)S(1)} %fusion.144), channel_id=1, replica_groups=mesh['blk'=8,'slab'=4] {'blk','slab'}, use_global_device_ids=true, to_apply=%region_1.1 | all-reduce | flops 8192 | bytes 65536 | tf_op jit(solution)/shard_map/while/body/eval_jaxpr/psum | solution.py:116
  608.9 39.7 %psum.33 = f32[32,32]{0,1:T(8,128)S(1)} all-reduce(f32[32,32]{0,1:T(8,128)S(1)} %convolution_multiply_fusion.4), channel_id=1, replica_groups=mesh['blk'=8,'slab'=4] {'blk','slab'}, use_global_device_ids=true, to_apply=%region_2.2 | all-reduce | flops 1024 | bytes 8192 | tf_op jit(solution)/shard_map/while/body/eval_jaxpr/psum | solution.py:123
  659.2 40.6 %psum.32 = f32[256,32]{0,1:T(8,128)S(1)} all-reduce(f32[256,32]{0,1:T(8,128)S(1)} %fusion.144), channel_id=1, replica_groups=mesh['blk'=8,'slab'=4] {'blk','slab'}, use_global_device_ids=true, to_apply=%region_1.1 | all-reduce | flops 8192 | bytes 65536 | tf_op jit(solution)/shard_map/while/body/eval_jaxpr/psum | solution.py:116
  702.4 39.7 %psum.33 = f32[32,32]{0,1:T(8,128)S(1)} all-reduce(f32[32,32]{0,1:T(8,128)S(1)} %convolution_multiply_fusion.4), channel_id=1, replica_groups=mesh['blk'=8,'slab'=4] {'blk','slab'}, use_global_device_ids=true, to_apply=%region_2.2 | all-reduce | flops 1024 | bytes 8192 | tf_op jit(solution)/shard_map/while/body/eval_jaxpr/psum | solution.py:123
  752.6 40.6 %psum.32 = f32[256,32]{0,1:T(8,128)S(1)} all-reduce(f32[256,32]{0,1:T(8,128)S(1)} %fusion.144), channel_id=1, replica_groups=mesh['blk'=8,'slab'=4] {'blk','slab'}, use_global_device_ids=true, to_apply=%region_1.1 | all-reduce | flops 8192 | bytes 65536 | tf_op jit(solution)/shard_map/while/body/eval_jaxpr/psum | solution.py:116
  795.8 39.7 %psum.33 = f32[32,32]{0,1:T(8,128)S(1)} all-reduce(f32[32,32]{0,1:T(8,128)S(1)} %convolution_multiply_fusion.4), channel_id=1, replica_groups=mesh['blk'=8,'slab'=4] {'blk','slab'}, use_global_device_ids=true, to_apply=%region_2.2 | all-reduce | flops 1024 | bytes 8192 | tf_op jit(solution)/shard_map/while/body/eval_jaxpr/psum | solution.py:123
  846.0 40.6 %psum.32 = f32[256,32]{0,1:T(8,128)S(1)} all-reduce(f32[256,32]{0,1:T(8,128)S(1)} %fusion.144), channel_id=1, replica_groups=mesh['blk'=8,'slab'=4] {'blk','slab'}, use_global_device_ids=true, to_apply=%region_1.1 | all-reduce | flops 8192 | bytes 65536 | tf_op jit(solution)/shard_map/while/body/eval_jaxpr/psum | solution.py:116
  889.2 39.6 %psum.33 = f32[32,32]{0,1:T(8,128)S(1)} all-reduce(f32[32,32]{0,1:T(8,128)S(1)} %convolution_multiply_fusion.4), channel_id=1, replica_groups=mesh['blk'=8,'slab'=4] {'blk','slab'}, use_global_device_ids=true, to_apply=%region_2.2 | all-reduce | flops 1024 | bytes 8192 | tf_op jit(solution)/shard_map/while/body/eval_jaxpr/psum | solution.py:123
  939.4 40.6 %psum.32 = f32[256,32]{0,1:T(8,128)S(1)} all-reduce(f32[256,32]{0,1:T(8,128)S(1)} %fusion.144), channel_id=1, replica_groups=mesh['blk'=8,'slab'=4] {'blk','slab'}, use_global_device_ids=true, to_apply=%region_1.1 | all-reduce | flops 8192 | bytes 65536 | tf_op jit(solution)/shard_map/while/body/eval_jaxpr/psum | solution.py:116
  982.7 39.6 %psum.33 = f32[32,32]{0,1:T(8,128)S(1)} all-reduce(f32[32,32]{0,1:T(8,128)S(1)} %convolution_multiply_fusion.4), channel_id=1, replica_groups=mesh['blk'=8,'slab'=4] {'blk','slab'}, use_global_device_ids=true, to_apply=%region_2.2 | all-reduce | flops 1024 | bytes 8192 | tf_op jit(solution)/shard_map/while/body/eval_jaxpr/psum | solution.py:123
  1055.1 8.8 copy.154
  1076.0 19.7 %custom-call.19 = f32[2,128,128]{1,2,0:T(8,128)S(1)} custom-call(f32[2,128,128]{2,1,0:T(8,128)S(1)} %get-tuple-element.100), custom_call_target="InvertDiagBlocksLowerTriangular" | custom-call | tf_op jit(solution)/shard_map/triangular_solve/custom-call.2 | solution.py:134
  1095.7 103.6 %all-reduce.8.cloned.1.call-done = f32[256,256]{1,0:T(8,128)} async-done(((f32[256,256]{1,0:T(8,128)}), f32[256,256]{1,0:T(8,128)}) %all-reduce.8.cloned.1.call-update) | async-done | bytes 262160 | tf_op jit(solution)/shard_map/psum | solution.py:110
  (252 shorter events, 287.1 us)
Async XLA Ops:
  7.2 17.6 %copy-start = (f32[4,8]{1,0:T(4,128)S(1)}, f32[4,8]{1,0:T(4,128)}, u32[]{:S(2)}) copy-start(f32[4,8]{1,0:T(4,128)} %param.13) | copy-start | bytes 388
  8.0 2.7 copy-start.2
  13.4 4.5 copy-start.5
  18.0 6.8 copy-start.11
  18.0 12.5 %copy-start.7 = (f32[4,8,8]{2,1,0:T(8,128)S(1)}, f32[4,8,8]{2,1,0:T(8,128)}, u32[]{:S(2)}) copy-start(f32[4,8,8]{2,1,0:T(8,128)} %param.12) | copy-start | bytes 3076
  18.0 12.6 %copy-start.13 = (f32[8,8]{1,0:T(8,128)S(1)}, f32[8,8]{1,0:T(8,128)}, u32[]{:S(2)}) copy-start(f32[8,8]{1,0:T(8,128)} %param.14) | copy-start | bytes 772
  18.0 12.7 %copy-start.12 = (f32[8,8]{1,0:T(8,128)S(1)}, f32[8,8]{1,0:T(8,128)}, u32[]{:S(2)}) copy-start(f32[8,8]{1,0:T(8,128)} %param.15) | copy-start | bytes 772
  19.4 14.2 %collective-permute-start = (f32[32,8,1,1024]{3,1,2,0:T(8,128)}, f32[32,8,1,1024]{3,1,2,0:T(8,128)S(1)}, u32[]{:S(2)}, u32[]{:S(2)}) collective-permute-start(f32[32,8,1,1024]{3,1,2,0:T(8,128)} %get-tuple-element.143), channel_id=1, source_target_pairs={{1,0},{2,1},{3,2},{5,4},{6,5},{7,6},{9,8},{10,9},{11,10},{13,12},{... | collective-permute-start | bytes 3145736 | tf_op jit(solution)/shard_map/ppermute | solution.py:24
  20.7 12.9 %collective-permute-start.1 = (f32[32,8,1,1024]{3,1,2,0:T(8,128)}, f32[32,8,1,1024]{3,1,2,0:T(8,128)}, u32[]{:S(2)}, u32[]{:S(2)}) collective-permute-start(f32[32,8,1,1024]{3,1,2,0:T(8,128)} %get-tuple-element.144), channel_id=1, source_target_pairs={{0,1},{1,2},{2,3},{4,5},{5,6},{6,7},{8,9},{9,10},{10,11},{12,13},{... | collective-permute-start | bytes 3145736 | tf_op jit(solution)/shard_map/ppermute | solution.py:23
  25.0 7.0 collective-permute-start.2
  26.3 5.7 collective-permute-start.3
  32.0 0.6 copy-start.6
  41.7 11.5 copy-start.8
  53.1 1.6 copy-start.10
  54.8 1.6 copy-start.9
  58.4 10.7 collective-permute-start.4
  59.7 11.4 collective-permute-start.5
  75.0 2.0 copy-start.3
  89.4 20.9 %collective-permute-start.6 = (f32[32,8,1,1024]{3,1,2,0:T(8,128)S(1)}, f32[32,8,1,1024]{3,1,2,0:T(8,128)S(1)}, u32[]{:S(2)}, u32[]{:S(2)}) collective-permute-start(f32[32,8,1,1024]{3,1,2,0:T(8,128)S(1)} %get-tuple-element.135), channel_id=1, source_target_pairs={{1,0},{2,1},{3,2},{5,4},{6,5},{7,6},{9,8},{10,9},{11,10},{13,12},{... | collective-permute-start | bytes 3145736 | tf_op jit(solution)/shard_map/ppermute | solution.py:24
  90.7 19.6 %collective-permute-start.7 = (f32[32,8,1,1024]{3,1,2,0:T(8,128)S(1)}, f32[32,8,1,1024]{3,1,2,0:T(8,128)S(1)}, u32[]{:S(2)}, u32[]{:S(2)}) collective-permute-start(f32[32,8,1,1024]{3,1,2,0:T(8,128)S(1)} %get-tuple-element.136), channel_id=1, source_target_pairs={{0,1},{1,2},{2,3},{4,5},{5,6},{6,7},{8,9},{9,10},{10,11},{12,13},{... | collective-permute-start | bytes 3145736 | tf_op jit(solution)/shard_map/ppermute | solution.py:23
  128.0 18.1 %collective-permute-start.8 = (f32[32,8,1,1024]{3,1,2,0:T(8,128)S(1)}, f32[32,8,1,1024]{3,1,2,0:T(8,128)S(1)}, u32[]{:S(2)}, u32[]{:S(2)}) collective-permute-start(f32[32,8,1,1024]{3,1,2,0:T(8,128)S(1)} %get-tuple-element.133), channel_id=1, source_target_pairs={{1,0},{2,1},{3,2},{5,4},{6,5},{7,6},{9,8},{10,9},{11,10},{13,12},{... | collective-permute-start | bytes 3145736 | tf_op jit(solution)/shard_map/ppermute | solution.py:24
  129.3 16.8 %collective-permute-start.9 = (f32[32,8,1,1024]{3,1,2,0:T(8,128)S(1)}, f32[32,8,1,1024]{3,1,2,0:T(8,128)S(1)}, u32[]{:S(2)}, u32[]{:S(2)}) collective-permute-start(f32[32,8,1,1024]{3,1,2,0:T(8,128)S(1)} %get-tuple-element.134), channel_id=1, source_target_pairs={{0,1},{1,2},{2,3},{4,5},{5,6},{6,7},{8,9},{9,10},{10,11},{12,13},{... | collective-permute-start | bytes 3145736 | tf_op jit(solution)/shard_map/ppermute | solution.py:23
  178.6 61.9 %all-to-all-start = ((f32[8,1,65536]{2,1,0:T(1,128)}), f32[8,1,65536]{2,1,0:T(1,128)}, u32[]{:S(2)}, u32[]{:S(2)}) async-start(f32[8,1,65536]{2,1,0:T(1,128)} %reshape.87), calls=%async_computation | async-start | bytes 4194304 | tf_op jit(solution)/shard_map/all_to_all | solution.py:105
  185.9 18.9 %collective-permute-start.10 = (f32[32,8,1,1024]{3,1,2,0:T(8,128)}, f32[32,8,1,1024]{3,1,2,0:T(8,128)S(1)}, u32[]{:S(2)}, u32[]{:S(2)}) collective-permute-start(f32[32,8,1,1024]{3,1,2,0:T(8,128)} %get-tuple-element.131), channel_id=1, source_target_pairs={{1,0},{2,1},{3,2},{5,4},{6,5},{7,6},{9,8},{10,9},{11,10},{13,12},{... | collective-permute-start | bytes 3145736 | tf_op jit(solution)/shard_map/ppermute | solution.py:24
  187.2 17.6 %collective-permute-start.11 = (f32[32,8,1,1024]{3,1,2,0:T(8,128)}, f32[32,8,1,1024]{3,1,2,0:T(8,128)}, u32[]{:S(2)}, u32[]{:S(2)}) collective-permute-start(f32[32,8,1,1024]{3,1,2,0:T(8,128)} %get-tuple-element.132), channel_id=1, source_target_pairs={{0,1},{1,2},{2,3},{4,5},{5,6},{6,7},{8,9},{9,10},{10,11},{12,13},{... | collective-permute-start | bytes 3145736 | tf_op jit(solution)/shard_map/ppermute | solution.py:23
  240.5 795.5 %all-to-all-start.2 = ((f32[8,1,65536]{2,1,0:T(1,128)}), f32[8,1,65536]{2,1,0:T(1,128)}, u32[]{:S(2)}, u32[]{:S(2)}) async-start(f32[8,1,65536]{2,1,0:T(1,128)} %reshape.89), calls=%async_computation.2 | async-start | bytes 4194304 | tf_op jit(solution)/shard_map/all_to_all | solution.py:106
  1036.0 167.9 %all-to-all-start.1 = ((f32[256,8,2,128]{3,2,1,0:T(2,128)}), f32[256,8,2,128]{3,2,1,0:T(2,128)}, u32[]{:S(2)}, u32[]{:S(2)}) async-start(f32[256,8,2,128]{3,2,1,0:T(2,128)} %copy.150), calls=%async_computation.1 | async-start | bytes 4194304 | tf_op jit(solution)/shard_map/all_to_all | solution.py:136
  1041.2 158.1 %all-reduce.8.cloned.1.call-start = ((), (), s32[]{:S(2)}) async-start(), calls=%async_computation.3 | async-start | bytes 524288 | tf_op jit(solution)/shard_map/psum | solution.py:110
  1063.9 4.0 copy-start.4
  1205.6 3.3 copy-start.1
Sparse Core Ops, SparseCore 0:
  1072.2 127.0 all-reduce.7
where the time goes:
time: 1230 us; the launch traced here: 1220 us
  blocking collectives  653 us (53%)
  other arithmetic  150 us (12%)
  matrix products  114 us (9%)
  waiting for transfers between devices  106 us (9%)
  local copies, waits for them, and re-layouts  95.7 us (8%)
  starting transfers between devices  82 us (7%)
  between operations  15 us (1%)
    psum x8, blocking collectives, panel_step(): lax.psum(inner(basis_rows, panel_states) / entries, ('blk', 'slab'))  336 us
    psum x8, blocking collectives, panel_step(): panel_gram = lax.psum(inner(residue, residue) / entries, ('blk', 'slab'))  317 us
    psum x1, waiting for transfers between devices, per_device(): moment = lax.psum(inner(states_flat, image_flat) / entries, ('blk', 'slab'))  104 us
    dot_general x5, matrix products, apply_padded(): jnp.einsum('bc,scxy->sbxy', mixing_matrix, stacked, precision=lax.Precisi...  58.3 us
    ppermute x6, starting transfers between devices, extended(): before = lax.ppermute(last, axis, up)  57 us
    unnamed x40, local copies, waits for them, and re-layouts  38.6 us
    unnamed x21, other arithmetic  36.6 us
    dot_general x17, matrix products, inner(): jnp.dot(left, right.T, precision=lax.Precision.HIGHEST, preferred_element...  30 us
  transfers between devices with their start and end apart: 16, of which 2 were waited for; matrix products, arithmetic and copies ran while one was open for 20% of the time, Pallas kernels for 0%

commit v1 on v0

--- a/solution.py
+++ b/solution.py
@@ -1,16 +1,336 @@
 import jax
 import jax.numpy as jnp
 from jax import lax
+from jax.experimental import pallas as pl
+from jax.experimental.pallas import tpu as pltpu
 from jax.sharding import PartitionSpec as P
 
 BANDS = 8
 MATERIALS = 4
-DEGREE = 4
 PANEL = 32
-
-
 SHIFT = 1.0
 SCALE = 3.0
+LANES = 128
+ALL = ("blk", "slab")
+LEFT = 4
+WINDOW = 42
+VMEM = pltpu.CompilerParams(vmem_limit_bytes=56 * 1024 * 1024)
+HIGHEST = lax.Precision.HIGHEST
+
+
+def dot(left, right, dims=((1,), (0,)), precision=None):
+    return lax.dot_general(
+        left, right, (dims, ((), ())), precision=precision, preferred_element_type=jnp.float32
+    )
+
+
+def split(value):
+    high = value.astype(jnp.bfloat16)
+    return high, (value - high.astype(jnp.float32)).astype(jnp.bfloat16)
+
+
+def exchange(pieces, unit):
+    count = len(pieces)
+    lane = lax.broadcasted_iota(jnp.int32, pieces[0].shape, 1) // unit
+    step = count // 2
+    while step:
+        low = (lane // step) % 2 == 0
+        out = list(pieces)
+        for i in range(count):
+            if (i // step) % 2 == 0:
+                a, c = pieces[i], pieces[i + step]
+                out[i] = jnp.where(low, a, pltpu.roll(c, step * unit, 1))
+                out[i + step] = jnp.where(low, pltpu.roll(a, LANES - step * unit, 1), c)
+        pieces = out
+        step //= 2
+    return pieces
+
+
+def pack_kernel(x_ref, o_ref, scr):
+    scr[0 : LEFT * 4, :] = jnp.zeros((LEFT * 4, LANES), jnp.float32)
+    tail = (LEFT + 1024) * 4
+    scr[tail:, :] = jnp.zeros((scr.shape[0] - tail, LANES), jnp.float32)
+    for tile in range(8):
+        for r in range(4):
+            row, high = r // 2, r % 2
+            parts = [
+                x_ref[pl.ds(((high * 4 + low) * 8 + tile) * 2 + row, 32, stride=128), :]
+                for low in range(4)
+            ]
+            turned = jnp.concatenate(parts, axis=0).T
+            scr[pl.ds((LEFT + 128 * tile) * 4 + r, 128, stride=4), :] = turned
+    for d in range(32):
+        o_ref[d] = scr[128 * d : 128 * d + WINDOW * 4, :]
+
+
+def pack(x):
+    rows = x.reshape(32, 8, 2, 8, LANES).transpose(0, 1, 3, 2, 4).reshape(4096, LANES)
+    return pl.pallas_call(
+        pack_kernel,
+        out_shape=jax.ShapeDtypeStruct((32, WINDOW * 4, LANES), jnp.float32),
+        scratch_shapes=[pltpu.VMEM((4136, LANES), jnp.float32)],
+        compiler_params=VMEM,
+        name="pack",
+    )(rows)
+
+
+def unpack_kernel(r_ref, o_ref):
+    for tile in range(8):
+        for r in range(4):
+            row, high = r // 2, r % 2
+            turned = r_ref[pl.ds(tile * 512 + r, 128, stride=4), :].T
+            for low in range(4):
+                o_ref[pl.ds(((high * 4 + low) * 8 + tile) * 2 + row, 32, stride=128), :] = turned[
+                    32 * low : 32 * low + 32
+                ]
+
+
+def unpack(blocks):
+    rows = pl.pallas_call(
+        unpack_kernel,
+        out_shape=jax.ShapeDtypeStruct((4096, LANES), jnp.float32),
+        compiler_params=VMEM,
+        name="unpack",
+    )(blocks.reshape(4096, LANES))
+    return rows.reshape(32, 8, 8, 2, LANES).transpose(0, 1, 3, 2, 4).reshape(32, 8, 2, 1024)
+
+
+def coef_kernel(reg_ref, onsite_ref, hop_ref, kx_ref, ky_ref, ch_ref, cl_ref):
+    def decode(index):
+        band = (index % 2) * 4 + (index // 32) % 4
+        x = ((index // 8) % 4) * 2 + (index // 2) % 2
+        column = (index // 4) % 2
+        return band, x, column
+
+    def one_hot(values, shape, axis):
+        return (values == lax.broadcasted_iota(jnp.int32, shape, axis)).astype(jnp.float32)
+
+    b_r, x_r, y_r = decode(lax.broadcasted_iota(jnp.int32, (128, 8), 0))
+    band_rows = one_hot(b_r, (128, 8), 1)
+    b_c, _, _ = decode(lax.broadcasted_iota(jnp.int32, (8, 384), 1))
+    band_cols = one_hot(b_c, (8, 384), 0)
+    reg = reg_ref[...]
+    hop = dot(band_rows, hop_ref[...], ((1,), (1,)), HIGHEST)
+
+    def table_of(offset):
+        return dot(one_hot(x_r + offset, (128, 8), 1), reg, precision=HIGHEST)
+
+    def hops(codes):
+        total = jnp.zeros_like(codes)
+        for m in range(MATERIALS):
+            total = total + jnp.where(codes == m + 1.0, hop[:, m : m + 1], 0.0)
+        return total
+
+    second = (lax.broadcasted_iota(jnp.int32, (128, LANES), 0) // 4) % 2 == 1
+
+    def aligned(table):
+        return jnp.where(second, pltpu.roll(table, LANES - 1, 1), table)
+
+    codes = table_of(0)
+    here, up, down = hops(codes), hops(table_of(-1)), hops(table_of(1))
+    before, after = pltpu.roll(here, 1, 1), pltpu.roll(here, LANES - 1, 1)
+    valid = (codes > 0.5).astype(jnp.float32)
+    centre = (0.5 * (4.0 * here + up + down + before + after) - SHIFT) * valid
+    fields = [aligned((codes == m + 1.0).astype(jnp.float32)) for m in range(MATERIALS)]
+    fields += [aligned(valid), aligned(centre)]
+    fields += [aligned(-0.5 * (here + side) * valid) for side in (up, down, before, after)]
+
+    b_r, x_r, y_r = decode(lax.broadcasted_iota(jnp.int32, (128, 384), 0))
+    k = lax.broadcasted_iota(jnp.int32, (128, 384), 1)
+    b_c, x_c, y_c = decode(k)
+    dy = 2 * (k // 128 - 1) + y_c - y_r
+    dx = x_c - x_r
+    same = b_r == b_c
+
+    def spread(matrix):
+        return dot(dot(band_rows, matrix, precision=HIGHEST), band_cols, precision=HIGHEST)
+
+    here_at, up_at, down_at = (dy == 0) & (dx == 0), (dy == 0) & (dx == -1), (dy == 0) & (dx == 1)
+    before_at, after_at = (dy == -1) & (dx == 0), (dy == 1) & (dx == 0)
+    onsite = [
+        jnp.where(here_at, spread(0.5 * (onsite_ref[m] + onsite_ref[m].T)), 0.0) for m in range(MATERIALS)
+    ]
+    kx = spread(0.5 * (0.5 * (kx_ref[...] - kx_ref[...].T)))
+    ky = spread(0.5 * (0.5 * (ky_ref[...] - ky_ref[...].T)))
+    mixed = (
+        jnp.where(down_at, kx, 0.0)
+        - jnp.where(up_at, kx, 0.0)
+        + jnp.where(after_at, ky, 0.0)
+        - jnp.where(before_at, ky, 0.0)
+    )
+    places = [here_at & same, up_at & same, down_at & same, before_at & same, after_at & same]
+    for pair in range(WINDOW // 2):
+        lane = 2 * pair + 1
+        scalar = [field[:, lane : lane + 1] for field in fields]
+        value = scalar[4] * mixed
+        for m in range(MATERIALS):
+            value = value + scalar[m] * onsite[m]
+        for place, weight in zip(places, scalar[5:]):
+            value = value + jnp.where(place, weight, 0.0)
+        high, low = split((2.0 / SCALE) * value)
+        ch_ref[pair] = high
+        cl_ref[pair] = low
+
+
+def coefficients(reg, onsite_table, hop_table, coupling_x, coupling_y):
+    shape = jax.ShapeDtypeStruct((WINDOW // 2, 128, 384), jnp.bfloat16)
+    return pl.pallas_call(
+        coef_kernel, out_shape=(shape, shape), compiler_params=VMEM, name="coefficients"
+    )(reg, onsite_table, hop_table, coupling_x, coupling_y)
+
+
+def filter_kernel(r_ref, ch_ref, cl_ref, vh_ref, vl_ref, g_ref, m_ref, fa, fb, ah, al, bh, bl):
+    pairs = WINDOW // 2
+    block = 128
+    zero = jnp.zeros((block, 256), jnp.bfloat16)
+    for ref in (ah, al, bh, bl):
+        ref[0:block, :] = zero
+        ref[(pairs + 1) * block :, :] = zero
+    for slab in range(4):
+        for half in range(2):
+            pieces = [r_ref[(half * 4 + j) * 4 + slab] for j in range(4)]
+            for low, piece in enumerate(exchange(pieces, 32)):
+                high_part, low_part = split(piece)
+                for pair in range(pairs):
+                    at = pair * block + low * 32 + slab * 8
+                    lanes = slice(half * 128, half * 128 + 128)
+                    fa[at : at + 8, lanes] = piece[pair * 8 : pair * 8 + 8]
+    ah[block : (pairs + 1) * block, :], al[block : (pairs + 1) * block, :] = split(fa[...])
+
+    def product(pair, high, low, first=0, last=3):
+        rows = pl.ds((pair + first) * block, (last - first) * block)
+        cols = slice(first * block, last * block)
+        vh, vl = high[rows, :], low[rows, :]
+        c_high, c_low = ch_ref[pair, :, cols], cl_ref[pair, :, cols]
+        return dot(c_high, vh) + (dot(c_high, vl) + dot(c_low, vh))
+
+    def store(pair, value, field, high, low):
+        field[pl.ds(pair * block, block), :] = value
+        rows = pl.ds((pair + 1) * block, block)
+        high[rows, :], low[rows, :] = split(value)
+
+    def first(pair, carry):
+        store(pair, 0.5 * product(pair, ah, al), fb, bh, bl)
+        return carry
+
+    lax.fori_loop(0, pairs, first, 0)
+
+    def later(source_high, source_low, old, high, low):
+        def body(pair, carry):
+            rows = pl.ds(pair * block, block)
+            store(pair, product(pair, source_high, source_low) - old[rows, :], old, high, low)
+            return carry
+
+        return body
+
+    lax.fori_loop(1, pairs - 1, later(bh, bl, fa, ah, al), 0)
+    lax.fori_loop(1, pairs - 1, later(ah, al, fb, bh, bl), 0)
+    lax.fori_loop(2, pairs - 2, later(bh, bl, fa, ah, al), 0)
+    own = slice(3 * block, 19 * block)
+    top = slice(3 * block, 20 * block)
+
+    def image(pair, carry):
+        value = product(pair, ah, al)
+        rows = pl.ds((pair + 1) * block, block)
+        bh[rows, :], bl[rows, :] = split(value)
+        return carry
+
+    lax.fori_loop(3, 18, image, 0)
+    value = product(2, ah, al, 1, 3)
+    bh[3 * block : 4 * block, :], bl[3 * block : 4 * block, :] = split(value)
+    value = product(18, ah, al, 0, 1)
+    row = lax.broadcasted_iota(jnp.int32, (block, 256), 0)
+    value = jnp.where((row // 4) % 2 == 0, value, 0.0)
+    bh[19 * block : 20 * block, :], bl[19 * block : 20 * block, :] = split(value)
+    vh_ref[...] = ah[own, :]
+    vl_ref[...] = al[own, :]
+    dims = ((0,), (0,))
+    cross = dot(ah[own, :], al[own, :], dims)
+    gram = dot(ah[own, :], ah[own, :], dims) + (cross + cross.T)
+    moment = dot(ah[top, :], bh[top, :], dims) + (
+        dot(ah[top, :], bl[top, :], dims) + dot(al[top, :], bh[top, :], dims)
+    )
+    g_ref[...] = gram
+    m_ref[...] = (0.5 * SCALE) * moment + SHIFT * gram
+
+
+def filtered_blocks(received, coef_high, coef_low):
+    rows = (WINDOW // 2) * 128
+    half = jax.ShapeDtypeStruct((2048, 256), jnp.bfloat16)
+    square = jax.ShapeDtypeStruct((256, 256), jnp.float32)
+    return pl.pallas_call(
+        filter_kernel,
+        out_shape=(half, half, square, square),
+        scratch_shapes=[pltpu.VMEM((rows, 256), jnp.float32)] * 2
+        + [pltpu.VMEM((rows + 256, 256), jnp.bfloat16)] * 4,
+        compiler_params=VMEM,
+        name="filtered",
+    )(received, coef_high, coef_low)
+
+
+def apply_kernel(vh_ref, vl_ref, w_ref, o_ref, scr):
+    wh, wl = split(w_ref[...])
+    vh = vh_ref[...]
+    scr[...] = dot(vh, wh, ((1,), (1,))) + (
+        dot(vh, wl, ((1,), (1,))) + dot(vl_ref[...], wh, ((1,), (1,)))
+    )
+    for slab in range(4):
+        for half in range(2):
+            lanes = slice(half * 128, half * 128 + 128)
+            pieces = []
+            for low in range(4):
+                rows = [
+                    scr[pair * 128 + low * 32 + slab * 8 : pair * 128 + low * 32 + slab * 8 + 8, lanes]
+                    for pair in range(16)
+                ]
+                pieces.append(jnp.concatenate(rows, axis=0))
+            for j, piece in enumerate(exchange(pieces, 32)):
+                o_ref[(half * 4 + j) * 4 + slab] = piece
+
+
+def apply_inverse(vh, vl, inverse):
+    return pl.pallas_call(
+        apply_kernel,
+        out_shape=jax.ShapeDtypeStruct((32, 128, LANES), jnp.float32),
+        scratch_shapes=[pltpu.VMEM((2048, 256), jnp.float32)],
+        compiler_params=VMEM,
+        name="apply_inverse",
+    )(vh, vl, inverse)
+
+
+def total(square):
+    count = lax.axis_size(ALL)
+    size = square.shape[0]
+    parts = square.reshape(count, size // count, size)
+    share = lax.all_to_all(parts, ALL, 0, 0, tiled=True).sum(0)
+    spread = jnp.broadcast_to(share[None], parts.shape)
+    return lax.all_to_all(spread, ALL, 0, 0, tiled=True).reshape(size, size)
+
+
+def fast(states_in, region, onsite_table, hop_table, coupling_x, coupling_y):
+    slabs = lax.axis_size("slab")
+    device = lax.axis_index("blk") * slabs + lax.axis_index("slab")
+    codes = (region + 1).astype(jnp.float32)
+    codes = lax.all_to_all(jnp.broadcast_to(codes[None], (slabs,) + codes.shape), "slab", 0, 0, tiled=True)
+    codes = jnp.pad(codes.reshape(8, 1024), ((0, 0), (LEFT + 1, LANES)))
+    codes = lax.dynamic_slice(codes, (0, 32 * device), (8, LANES))
+    received = lax.all_to_all(pack(states_in), ALL, 0, 0, tiled=True)
+    coef_high, coef_low = coefficients(codes, onsite_table, hop_table, coupling_x, coupling_y)
+    vh, vl, gram, moment = filtered_blocks(received, coef_high, coef_low)
+    entries = float(BANDS * 8 * 1024)
+    gram = total(gram) / entries
+    moment = total(moment) / entries
+    factor = jnp.linalg.cholesky(gram)
+    inverse = lax.linalg.triangular_solve(
+        factor, jnp.eye(256, dtype=jnp.float32), left_side=True, lower=True
+    )
+    states_out = unpack(lax.all_to_all(apply_inverse(vh, vl, inverse), ALL, 0, 0, tiled=True))
+    mine = lax.dynamic_slice_in_dim(inverse, lax.axis_index("blk") * 32, 32, 0)
+    projected = dot(dot(mine, moment, precision=HIGHEST), inverse, ((1,), (1,)), HIGHEST)
+    return states_out, projected
+
+
+DEGREE = 4
 
 
 def extended(array, sides, width):
@@ -79,7 +399,7 @@
     )
 
 
-def per_device(states_in, region, onsite_table, hop_table, coupling_x, coupling_y):
+def general(states_in, region, onsite_table, hop_table, coupling_x, coupling_y):
     mixing_matrix = mixing(onsite_table, coupling_x, coupling_y)
     material_masks = masks_of(region)
     hop_field = jnp.einsum(
@@ -139,6 +459,12 @@
     return (states_out, projected_rows)
 
 
+def per_device(states_in, region, *tables):
+    known = (lax.axis_size("blk"), lax.axis_size("slab")) == (8, 4)
+    run = fast if known and states_in.shape == (32, 8, 2, 1024) else general
+    return run(states_in, region, *tables)
+
+
 def solution(mesh):
     return jax.shard_map(
         per_device,

time: 1230 us -> 288 us (0.23); the launches traced: 1220 us -> 287 us
  blocking collectives: 653 us -> 15 us
  matrix products: 114 us -> 2.51 us
  other arithmetic: 150 us -> 55.5 us
  local copies, waits for them, and re-layouts: 95.7 us -> 9.64 us
  starting transfers between devices: 82 us -> 24.6 us
  Pallas kernels: 0 us -> 55.8 us
  waiting for transfers between devices: 106 us -> 122 us
  between operations: 15 us -> 2.07 us
    psum x16 -> x0, blocking collectives: 653 us -> none  [the longest x8 336 us: panel_step(): lax.psum(inner(basis_rows, panel_states) / entries, ('blk', 'slab'))]
    all_to_all x3 -> x6, waiting for transfers between devices: 0.01 us -> 122 us  [the longest x1 53.1 us: fast(): received = lax.all_to_all(pack(states_in), ALL, 0, 0, tiled=True)]
    dot_general x31 -> x2, matrix products: 107 us -> 1.2 us  [dot(): lax.dot_general(left, right, (dims, ((), ())), precision=precision, prefe...]
    psum x1 -> x0, waiting for transfers between devices: 104 us -> none  [per_device(): moment = lax.psum(inner(states_flat, image_flat) / entries, ('blk', 'slab'))]
    ppermute x12 -> x0, starting transfers between devices: 64.7 us -> none  [the longest x6 57 us: extended(): before = lax.ppermute(last, axis, up)]
    pallas_call x0 -> x5, Pallas kernels: none -> 55.8 us  [the longest x1 32.2 us: filtered_blocks(): pl.pallas_call(filter_kernel, out_shape=(half, half, square, square), scr...]
    unnamed x21 -> x1, other arithmetic: 36.6 us -> 0.01 us
    unnamed x40 -> x4, local copies, waits for them, and re-layouts: 38.6 us -> 2.88 us
  transfers between devices with their start and end apart: 16 -> 6, of which waited for: 2 -> 4; matrix products, arithmetic and copies ran while one was open for 20% -> 22% of each run, Pallas kernels for 0% -> 6%
where the time goes in v1:
time: 288 us; the launch traced here: 287 us
  waiting for transfers between devices  122 us (42%)
  Pallas kernels  55.8 us (19%)
  other arithmetic  55.5 us (19%)
  starting transfers between devices  24.6 us (9%)
  blocking collectives  15 us (5%)
  local copies, waits for them, and re-layouts  9.64 us (3%)
    all_to_all x1, waiting for transfers between devices, fast(): received = lax.all_to_all(pack(states_in), ALL, 0, 0, tiled=True)  53.1 us
    all_to_all x1, waiting for transfers between devices, fast(): lax.all_to_all(apply_inverse(vh, vl, inverse), ALL, 0, 0, tiled=True)  47.6 us
    another operation x6, other arithmetic, fast(): factor = jnp.linalg.cholesky(gram)  33.9 us
    pallas_call x1, Pallas kernels, filtered_blocks(): pl.pallas_call(filter_kernel, out_shape=(half, half, square, square), scr...  32.2 us
    another operation x4, other arithmetic, fast(): lax.linalg.triangular_solve(factor, jnp.eye(256, dtype=jnp.float32), left...  20.6 us
    all_to_all x1, blocking collectives, total(): share = lax.all_to_all(parts, ALL, 0, 0, tiled=True).sum(0)  15 us
    all_to_all x1, waiting for transfers between devices, total(): share = lax.all_to_all(parts, ALL, 0, 0, tiled=True).sum(0)  10.6 us
    all_to_all x2, waiting for transfers between devices, total(): return lax.all_to_all(spread, ALL, 0, 0, tiled=True).reshape(size, size)  10.5 us
  transfers between devices with their start and end apart: 6, of which 4 were waited for; matrix products, arithmetic and copies ran while one was open for 22% of the time, Pallas kernels for 6%

profile of v1, /device:TPU:0, one launch (start us, length us, event | category | flops | bytes accessed | tf_op | source)
XLA Modules:
  0.0 286.9 jit_solution(7341109213099068820)
XLA Ops:
  0.6 0.7 add_convert_fusion
  2.0 4.2 %all-to-all-start.1 = ((f32[4,2,1024]{2,1,0:T(2,128)}), f32[4,2,1024]{2,1,0:T(2,128)S(1)}, u32[]{:S(2)}, u32[]{:S(2)}) async-start(f32[4,2,1024]{2,1,0:T(2,128)} %broadcast_in_dim.7), calls=%async_computation.1 | async-start | bytes 65536 | tf_op jit(solution)/shard_map/all_to_all | solution.py:314
  6.2 4.6 %pack.1 = f32[32,168,128]{2,1,0:T(8,128)} custom-call(f32[4096,128]{1,0:T(8,128)} %bitcast.53), custom_call_target="tpu_custom_call" | custom-call | tf_op jit(solution)/shard_map/pack/pallas_call | solution.py:68
  10.8 6.8 %all-to-all-start = ((f32[32,168,128]{2,1,0:T(8,128)}), f32[32,168,128]{2,1,0:T(8,128)S(1)}, u32[]{:S(2)}, u32[]{:S(2)}) async-start(f32[32,168,128]{2,1,0:T(8,128)} %pack.1), calls=%async_computation | async-start | bytes 5505024 | tf_op jit(solution)/shard_map/all_to_all | solution.py:317
  17.6 0.7 pad_dynamic-slice_fusion.2.reg_ref
  18.3 9.3 %coefficients.1 = (bf16[21,128,384]{2,1,0:T(8,128)(2,1)}, bf16[21,128,384]{2,1,0:T(8,128)(2,1)}) custom-call(f32[8,128]{1,0:T(8,128)} %pad_dynamic-slice_fusion.2.reg_ref, f32[4,8,8]{2,1,0:T(8,128)} %onsite_ref.1, f32[4,8]{1,0:T(4,128)} %hop_ref.1, f32[8,8]{1,0:T(8,128)} %kx_ref.1, f32[8,8]{1,0:T(8,128)} %ky_ref.1), custom_call_target="tpu_custom_call" | custom-call | tf_op jit(solution)/shard_map/coefficients/pallas_call | solution.py:177
  27.6 53.1 %all-to-all-done.r_ref = f32[32,168,128]{2,1,0:T(8,128)S(1)} async-done(((f32[32,168,128]{2,1,0:T(8,128)}), f32[32,168,128]{2,1,0:T(8,128)S(1)}, u32[]{:S(2)}, u32[]{:S(2)}) %all-to-all-start) | async-done | bytes 2752544 | tf_op jit(solution)/shard_map/all_to_all | solution.py:317
  80.7 1.6 copy-done
  82.3 32.2 %filtered.1 = (bf16[2048,256]{1,0:T(8,128)(2,1)}, bf16[2048,256]{1,0:T(8,128)(2,1)}, f32[256,256]{1,0:T(8,128)}, f32[256,256]{1,0:T(8,128)}) custom-call(f32[32,168,128]{2,1,0:T(8,128)} %copy-done, bf16[21,128,384]{2,1,0:T(8,128)(2,1)} %get-tuple-element.8.ch_ref, bf16[21,128,384]{2,1,0:T(8,128)(2,1)} %get-tuple-element.9.cl_ref), custom_call_target="tpu_custom_call" | custom-call | tf_op jit(solution)/shard_map/filtered/pallas_call | solution.py:261
  114.5 15.0 %all_to_all.35 = f32[32,8,256]{2,1,0:T(8,128)S(1)} all-to-all(f32[32,8,256]{2,1,0:T(8,128)} %bitcast.56), channel_id=1, replica_groups=mesh['blk'=8,'slab'=4] {'blk','slab'}, dimensions={0} | all-to-all | bytes 524288 | tf_op jit(solution)/shard_map/all_to_all | solution.py:305
  129.5 2.6 all-to-all-start.5
  132.1 10.6 %all-to-all-done.5 = f32[32,8,256]{2,1,0:T(8,128)S(1)} async-done(((f32[32,8,256]{2,1,0:T(8,128)}), f32[32,8,256]{2,1,0:T(8,128)S(1)}, u32[]{:S(2)}, u32[]{:S(2)}) %all-to-all-start.5) | async-done | bytes 262176 | tf_op jit(solution)/shard_map/all_to_all | solution.py:305
  142.7 0.7 broadcast_in_dim.8
  143.4 2.6 all-to-all-start.3
  146.1 10.5 %all-to-all-done.3 = f32[32,8,256]{2,1,0:T(8,128)S(1)} async-done(((f32[32,8,256]{2,1,0:T(8,128)}), f32[32,8,256]{2,1,0:T(8,128)S(1)}, u32[]{:S(2)}, u32[]{:S(2)}) %all-to-all-start.3) | async-done | bytes 262176 | tf_op jit(solution)/shard_map/all_to_all | solution.py:307
  156.6 0.7 broadcast_in_dim.9
  157.3 2.8 all-to-all-start.6
  160.3 11.7 %cholesky.50 = f32[128,128]{1,0:T(8,128)S(1)} custom-call(f32[128,128]{1,0:T(8,128)S(1)} %cholesky.118), custom_call_target="Cholesky" | custom-call | tf_op jit(solution)/shard_map/jit(cholesky)/cholesky | solution.py:323
  172.1 9.8 %custom-call.14 = f32[1,128,128]{1,2,0:T(8,128)S(1)} custom-call(f32[1,128,128]{2,1,0:T(8,128)S(1)} %get-tuple-element.35), custom_call_target="InvertDiagBlocksLowerTriangular" | custom-call | tf_op jit(solution)/shard_map/jit(cholesky)/cholesky | solution.py:323
  182.4 11.7 %cholesky.105 = f32[128,128]{1,0:T(8,128)S(1)} custom-call(f32[128,128]{1,0:T(8,128)S(1)} %convolution_subtract_fusion.1), custom_call_target="Cholesky" | custom-call | tf_op jit(solution)/shard_map/jit(cholesky)/cholesky | solution.py:323
  194.1 0.6 compare_reduce_fusion
  196.1 3.8 %while.1 = (s32[]{:T(128)}, f32[256,256]{1,0:T(8,128)S(1)}, s32[2,2]{1,0:T(2,128)S(1)}, f32[2,128,128]{2,1,0:T(8,128)S(1)}, s32[]{:T(128)}) while((s32[]{:T(128)}, f32[256,256]{1,0:T(8,128)S(1)}, s32[2,2]{1,0:T(2,128)S(1)}, f32[2,128,128]{2,1,0:T(8,128)S(1)}, s32[]{:T(128)}) %tuple.27), condition=%wide.while_cond, body=%wide.while_body.sunk | while | flops 2 | bytes 131189 | solution.py:324
  196.7 1.3 bitcast_dynamic-update-slice_fusion.2
  198.6 1.3 bitcast_dynamic-update-slice_fusion.2
  199.9 19.9 %custom-call.15 = f32[2,128,128]{1,2,0:T(8,128)S(1)} custom-call(f32[2,128,128]{2,1,0:T(8,128)S(1)} %get-tuple-element.21), custom_call_target="InvertDiagBlocksLowerTriangular" | custom-call | tf_op jit(solution)/shard_map/triangular_solve | solution.py:324
  220.7 0.7 pad_maximum_fusion.w_ref
  221.4 4.6 %apply_inverse.1 = f32[32,128,128]{2,1,0:T(8,128)} custom-call(bf16[2048,256]{1,0:T(8,128)(2,1)} %get-tuple-element.10.vh_ref, bf16[2048,256]{1,0:T(8,128)(2,1)} %get-tuple-element.11.vl_ref, f32[256,256]{1,0:T(8,128)} %pad_maximum_fusion.w_ref), custom_call_target="tpu_custom_call" | custom-call | tf_op jit(solution)/shard_map/apply_inverse/pallas_call | solution.py:292
  226.0 5.7 %all-to-all-start.4 = ((f32[32,128,128]{2,1,0:T(8,128)}), f32[32,128,128]{2,1,0:T(8,128)S(1)}, u32[]{:S(2)}, u32[]{:S(2)}) async-start(f32[32,128,128]{2,1,0:T(8,128)} %apply_inverse.1), calls=%async_computation.4 | async-start | bytes 4194304 | tf_op jit(solution)/shard_map/all_to_all | solution.py:327
  231.9 1.0 fusion.17
  232.8 47.6 %all-to-all-done.4 = f32[32,128,128]{2,1,0:T(8,128)S(1)} async-done(((f32[32,128,128]{2,1,0:T(8,128)}), f32[32,128,128]{2,1,0:T(8,128)S(1)}, u32[]{:S(2)}, u32[]{:S(2)}) %all-to-all-start.4) | async-done | bytes 2097184 | tf_op jit(solution)/shard_map/all_to_all | solution.py:327
  280.4 1.3 copy-done.1
  281.7 5.1 %unpack.1 = f32[4096,128]{1,0:T(8,128)} custom-call(f32[4096,128]{1,0:T(8,128)} %bitcast.52), custom_call_target="tpu_custom_call" | custom-call | tf_op jit(solution)/shard_map/unpack/pallas_call | solution.py:89
  (30 shorter events, 3.9 us)
Async XLA Ops:
  2.0 8.8 %all-to-all-start.1 = ((f32[4,2,1024]{2,1,0:T(2,128)}), f32[4,2,1024]{2,1,0:T(2,128)S(1)}, u32[]{:S(2)}, u32[]{:S(2)}) async-start(f32[4,2,1024]{2,1,0:T(2,128)} %broadcast_in_dim.7), calls=%async_computation.1 | async-start | bytes 65536 | tf_op jit(solution)/shard_map/all_to_all | solution.py:314
  10.8 70.0 %all-to-all-start = ((f32[32,168,128]{2,1,0:T(8,128)}), f32[32,168,128]{2,1,0:T(8,128)S(1)}, u32[]{:S(2)}, u32[]{:S(2)}) async-start(f32[32,168,128]{2,1,0:T(8,128)} %pack.1), calls=%async_computation | async-start | bytes 5505024 | tf_op jit(solution)/shard_map/all_to_all | solution.py:317
  80.7 1.6 copy-start
  129.5 13.2 %all-to-all-start.5 = ((f32[32,8,256]{2,1,0:T(8,128)}), f32[32,8,256]{2,1,0:T(8,128)S(1)}, u32[]{:S(2)}, u32[]{:S(2)}) async-start(f32[32,8,256]{2,1,0:T(8,128)} %bitcast.55), calls=%async_computation.5 | async-start | bytes 524288 | tf_op jit(solution)/shard_map/all_to_all | solution.py:305
  143.4 13.2 %all-to-all-start.3 = ((f32[32,8,256]{2,1,0:T(8,128)}), f32[32,8,256]{2,1,0:T(8,128)S(1)}, u32[]{:S(2)}, u32[]{:S(2)}) async-start(f32[32,8,256]{2,1,0:T(8,128)} %broadcast_in_dim.8), calls=%async_computation.3 | async-start | bytes 524288 | tf_op jit(solution)/shard_map/all_to_all | solution.py:307
  157.3 68.6 %all-to-all-start.6 = ((f32[32,8,256]{2,1,0:T(8,128)}), f32[32,8,256]{2,1,0:T(8,128)S(1)}, u32[]{:S(2)}, u32[]{:S(2)}) async-start(f32[32,8,256]{2,1,0:T(8,128)} %broadcast_in_dim.9), calls=%async_computation.6 | async-start | bytes 524288 | tf_op jit(solution)/shard_map/all_to_all | solution.py:307
  226.0 54.4 %all-to-all-start.4 = ((f32[32,128,128]{2,1,0:T(8,128)}), f32[32,128,128]{2,1,0:T(8,128)S(1)}, u32[]{:S(2)}, u32[]{:S(2)}) async-start(f32[32,128,128]{2,1,0:T(8,128)} %apply_inverse.1), calls=%async_computation.4 | async-start | bytes 4194304 | tf_op jit(solution)/shard_map/all_to_all | solution.py:327
  280.4 1.3 copy-start.1

commit v2 on v1

--- a/solution.py
+++ b/solution.py
@@ -1,3 +1,5 @@
+import functools
+
 import jax
 import jax.numpy as jnp
 from jax import lax
@@ -16,6 +18,8 @@
 WINDOW = 42
 VMEM = pltpu.CompilerParams(vmem_limit_bytes=56 * 1024 * 1024)
 HIGHEST = lax.Precision.HIGHEST
+UNROLL = 3
+OWN = slice(2 * 128 + 64, 18 * 128 + 64)
 
 
 def dot(left, right, dims=((1,), (0,)), precision=None):
@@ -97,9 +101,9 @@
 
 def coef_kernel(reg_ref, onsite_ref, hop_ref, kx_ref, ky_ref, ch_ref, cl_ref):
     def decode(index):
-        band = (index % 2) * 4 + (index // 32) % 4
+        band = (index % 2) * 4 + ((index // 32) % 2) * 2 + (index // 4) % 2
         x = ((index // 8) % 4) * 2 + (index // 2) % 2
-        column = (index // 4) % 2
+        column = (index // 64) % 2
         return band, x, column
 
     def one_hot(values, shape, axis):
@@ -107,8 +111,8 @@
 
     b_r, x_r, y_r = decode(lax.broadcasted_iota(jnp.int32, (128, 8), 0))
     band_rows = one_hot(b_r, (128, 8), 1)
-    b_c, _, _ = decode(lax.broadcasted_iota(jnp.int32, (8, 384), 1))
-    band_cols = one_hot(b_c, (8, 384), 0)
+    b_c, _, _ = decode(lax.broadcasted_iota(jnp.int32, (8, 256), 1) + 64)
+    band_cols = one_hot(b_c, (8, 256), 0)
     reg = reg_ref[...]
     hop = dot(band_rows, hop_ref[...], ((1,), (1,)), HIGHEST)
 
@@ -121,7 +125,7 @@
             total = total + jnp.where(codes == m + 1.0, hop[:, m : m + 1], 0.0)
         return total
 
-    second = (lax.broadcasted_iota(jnp.int32, (128, LANES), 0) // 4) % 2 == 1
+    second = lax.broadcasted_iota(jnp.int32, (128, LANES), 0) >= 64
 
     def aligned(table):
         return jnp.where(second, pltpu.roll(table, LANES - 1, 1), table)
@@ -135,10 +139,10 @@
     fields += [aligned(valid), aligned(centre)]
     fields += [aligned(-0.5 * (here + side) * valid) for side in (up, down, before, after)]
 
-    b_r, x_r, y_r = decode(lax.broadcasted_iota(jnp.int32, (128, 384), 0))
-    k = lax.broadcasted_iota(jnp.int32, (128, 384), 1)
-    b_c, x_c, y_c = decode(k)
-    dy = 2 * (k // 128 - 1) + y_c - y_r
+    b_r, x_r, y_r = decode(lax.broadcasted_iota(jnp.int32, (128, 256), 0))
+    k = lax.broadcasted_iota(jnp.int32, (128, 256), 1)
+    b_c, x_c, _ = decode(k + 64)
+    dy = k // 64 - 1 - y_r
     dx = x_c - x_r
     same = b_r == b_c
 
@@ -173,47 +177,58 @@
 
 
 def coefficients(reg, onsite_table, hop_table, coupling_x, coupling_y):
-    shape = jax.ShapeDtypeStruct((WINDOW // 2, 128, 384), jnp.bfloat16)
+    shape = jax.ShapeDtypeStruct((WINDOW // 2, 128, 256), jnp.bfloat16)
     return pl.pallas_call(
         coef_kernel, out_shape=(shape, shape), compiler_params=VMEM, name="coefficients"
     )(reg, onsite_table, hop_table, coupling_x, coupling_y)
 
 
-def filter_kernel(r_ref, ch_ref, cl_ref, vh_ref, vl_ref, g_ref, m_ref, fa, fb, ah, al, bh, bl):
+def halves(even, odd):
+    even, odd = (value.reshape(-1, 8, LANES) for value in (even, odd))
+    first = lax.broadcasted_iota(jnp.int32, (1, 8, LANES), 1) < 4
+    return (
+        jnp.where(first, even, pltpu.roll(odd, 4, 1)),
+        jnp.where(first, pltpu.roll(even, 4, 1), odd),
+    )
+
+
+def filter_kernel(r_ref, ch_ref, cl_ref, vh_ref, vl_ref, g_ref, fa, fb, ah, al, bh, bl):
     pairs = WINDOW // 2
     block = 128
-    zero = jnp.zeros((block, 256), jnp.bfloat16)
+    edge = 64
+    zero = jnp.zeros((edge, 256), jnp.bfloat16)
     for ref in (ah, al, bh, bl):
-        ref[0:block, :] = zero
-        ref[(pairs + 1) * block :, :] = zero
+        ref[0:edge, :] = zero
+        ref[pairs * block + edge :, :] = zero
     for slab in range(4):
         for half in range(2):
-            pieces = [r_ref[(half * 4 + j) * 4 + slab] for j in range(4)]
-            for low, piece in enumerate(exchange(pieces, 32)):
-                high_part, low_part = split(piece)
-                for pair in range(pairs):
-                    at = pair * block + low * 32 + slab * 8
-                    lanes = slice(half * 128, half * 128 + 128)
-                    fa[at : at + 8, lanes] = piece[pair * 8 : pair * 8 + 8]
-    ah[block : (pairs + 1) * block, :], al[block : (pairs + 1) * block, :] = split(fa[...])
-
-    def product(pair, high, low, first=0, last=3):
-        rows = pl.ds((pair + first) * block, (last - first) * block)
-        cols = slice(first * block, last * block)
+            lanes = slice(half * 128, half * 128 + 128)
+            pieces = exchange([r_ref[(half * 4 + j) * 4 + slab] for j in range(4)], 32)
+            for mid in range(2):
+                for column, piece in enumerate(halves(pieces[2 * mid], pieces[2 * mid + 1])):
+                    for pair in range(pairs):
+                        at = pair * block + column * 64 + mid * 32 + slab * 8
+                        fa[at : at + 8, lanes] = piece[pair]
+    ah[edge : pairs * block + edge, :], al[edge : pairs * block + edge, :] = split(fa[...])
+
+    def product(pair, high, low):
+        rows = pl.ds(pair * block, 256)
         vh, vl = high[rows, :], low[rows, :]
-        c_high, c_low = ch_ref[pair, :, cols], cl_ref[pair, :, cols]
-        return dot(c_high, vh) + (dot(c_high, vl) + dot(c_low, vh))
+        c_high, c_low = ch_ref[pair], cl_ref[pair]
+        return dot(
+            jnp.concatenate([c_high, c_high, c_low], axis=1), jnp.concatenate([vh, vl, vh], axis=0)
+        )
 
     def store(pair, value, field, high, low):
         field[pl.ds(pair * block, block), :] = value
-        rows = pl.ds((pair + 1) * block, block)
+        rows = pl.ds(pair * block + edge, block)
         high[rows, :], low[rows, :] = split(value)
 
     def first(pair, carry):
         store(pair, 0.5 * product(pair, ah, al), fb, bh, bl)
         return carry
 
-    lax.fori_loop(0, pairs, first, 0)
+    lax.fori_loop(0, pairs, first, 0, unroll=UNROLL)
 
     def later(source_high, source_low, old, high, low):
         def body(pair, carry):
@@ -223,110 +238,215 @@
 
         return body
 
-    lax.fori_loop(1, pairs - 1, later(bh, bl, fa, ah, al), 0)
-    lax.fori_loop(1, pairs - 1, later(ah, al, fb, bh, bl), 0)
-    lax.fori_loop(2, pairs - 2, later(bh, bl, fa, ah, al), 0)
-    own = slice(3 * block, 19 * block)
-    top = slice(3 * block, 20 * block)
-
-    def image(pair, carry):
-        value = product(pair, ah, al)
-        rows = pl.ds((pair + 1) * block, block)
-        bh[rows, :], bl[rows, :] = split(value)
-        return carry
-
-    lax.fori_loop(3, 18, image, 0)
-    value = product(2, ah, al, 1, 3)
-    bh[3 * block : 4 * block, :], bl[3 * block : 4 * block, :] = split(value)
-    value = product(18, ah, al, 0, 1)
-    row = lax.broadcasted_iota(jnp.int32, (block, 256), 0)
-    value = jnp.where((row // 4) % 2 == 0, value, 0.0)
-    bh[19 * block : 20 * block, :], bl[19 * block : 20 * block, :] = split(value)
-    vh_ref[...] = ah[own, :]
-    vl_ref[...] = al[own, :]
+    lax.fori_loop(1, pairs - 1, later(bh, bl, fa, ah, al), 0, unroll=UNROLL)
+    lax.fori_loop(1, pairs - 1, later(ah, al, fb, bh, bl), 0, unroll=UNROLL)
+    lax.fori_loop(2, pairs - 2, later(bh, bl, fa, ah, al), 0, unroll=UNROLL)
+    vh_ref[...] = ah[...]
+    vl_ref[...] = al[...]
     dims = ((0,), (0,))
-    cross = dot(ah[own, :], al[own, :], dims)
-    gram = dot(ah[own, :], ah[own, :], dims) + (cross + cross.T)
-    moment = dot(ah[top, :], bh[top, :], dims) + (
-        dot(ah[top, :], bl[top, :], dims) + dot(al[top, :], bh[top, :], dims)
-    )
-    g_ref[...] = gram
-    m_ref[...] = (0.5 * SCALE) * moment + SHIFT * gram
+    cross = dot(ah[OWN, :], al[OWN, :], dims)
+    g_ref[...] = dot(ah[OWN, :], ah[OWN, :], dims) + (cross + cross.T)
 
 
 def filtered_blocks(received, coef_high, coef_low):
     rows = (WINDOW // 2) * 128
-    half = jax.ShapeDtypeStruct((2048, 256), jnp.bfloat16)
+    half = jax.ShapeDtypeStruct((rows + 128, 256), jnp.bfloat16)
     square = jax.ShapeDtypeStruct((256, 256), jnp.float32)
     return pl.pallas_call(
         filter_kernel,
-        out_shape=(half, half, square, square),
+        out_shape=(half, half, square),
         scratch_shapes=[pltpu.VMEM((rows, 256), jnp.float32)] * 2
-        + [pltpu.VMEM((rows + 256, 256), jnp.bfloat16)] * 4,
+        + [pltpu.VMEM((rows + 128, 256), jnp.bfloat16)] * 4,
         compiler_params=VMEM,
         name="filtered",
     )(received, coef_high, coef_low)
 
 
-def apply_kernel(vh_ref, vl_ref, w_ref, o_ref, scr):
+def moment_kernel(vh_ref, vl_ref, ch_ref, cl_ref, g_ref, m_ref, bh, bl):
+    block, edge = 128, 64
+
+    def image(pair, rows, drop=0):
+        vh, vl = vh_ref[rows, :], vl_ref[rows, :]
+        c_high, c_low = ch_ref[pair, :, drop:], cl_ref[pair, :, drop:]
+        value = dot(
+            jnp.concatenate([c_high, c_high, c_low], axis=1), jnp.concatenate([vh, vl, vh], axis=0)
+        )
+        at = pl.ds((pair - 2) * block, block)
+        bh[at, :], bl[at, :] = split(value)
+
+    def body(pair, carry):
+        image(pair, pl.ds(pair * block, 256))
+        return carry
+
+    image(2, slice(2 * block + edge, 4 * block), edge)
+    lax.fori_loop(3, 18, body, 0, unroll=3)
+    rows = slice(18 * block, 18 * block + edge)
+    c_high, c_low = ch_ref[18, 0:edge, 0:edge], cl_ref[18, 0:edge, 0:edge]
+    value = dot(c_high, vh_ref[rows, :]) + (dot(c_high, vl_ref[rows, :]) + dot(c_low, vh_ref[rows, :]))
+    bh[16 * block :, :], bl[16 * block :, :] = split(value)
+    dims = ((0,), (0,))
+    top = slice(OWN.start, OWN.stop + edge)
+    high = vh_ref[top, :]
+    moment = dot(high, bh[...], dims) + (dot(high, bl[...], dims) + dot(vl_ref[top, :], bh[...], dims))
+    m_ref[...] = (0.5 * SCALE) * moment + SHIFT * g_ref[...]
+
+
+def moment_of(vh, vl, coef_high, coef_low, gram):
+    return pl.pallas_call(
+        moment_kernel,
+        out_shape=jax.ShapeDtypeStruct((256, 256), jnp.float32),
+        scratch_shapes=[pltpu.VMEM((16 * 128 + 64, 256), jnp.bfloat16)] * 2,
+        compiler_params=VMEM,
+        cost_estimate=pl.CostEstimate(flops=int(4e9), transcendentals=0, bytes_accessed=int(1e7)),
+        name="moment",
+    )(vh, vl, coef_high, coef_low, gram)
+
+
+def panel_inverse(block):
+    row = lax.broadcasted_iota(jnp.int32, (8, LANES), 0)
+    lane = lax.broadcasted_iota(jnp.int32, (8, LANES), 1)
+
+    def spread(tile, k):
+        return jnp.broadcast_to(tile[k % 8 : k % 8 + 1], (8, LANES))
+
+    cols = [
+        [jnp.broadcast_to(block[8 * t : 8 * t + 8, j : j + 1], (8, LANES)) for t in range(4)]
+        for j in range(32)
+    ]
+    inverse = [(lane == row + 8 * t).astype(jnp.float32) for t in range(4)]
+    pivots = [jnp.ones((8, LANES), jnp.float32) for t in range(4)]
+    for k in range(32):
+        own = k // 8
+        pivot = spread(cols[k][own], k)
+        pivots[own] = jnp.where(row == k % 8, pivot, pivots[own])
+        scale = 1.0 / pivot
+        ratio = {t: cols[k][t] * scale for t in range(own, 4)}
+        ratio[own] = jnp.where(row > k % 8, ratio[own], 0.0)
+        line = spread(inverse[own], k)
+        for j in range(k + 1, 32):
+            weight = spread(ratio[j // 8], j)
+            for t in range(j // 8, 4):
+                cols[j][t] = cols[j][t] - cols[k][t] * weight
+        for t in range(own, 4):
+            inverse[t] = inverse[t] - ratio[t] * line
+    return jnp.concatenate([inverse[t] * lax.rsqrt(pivots[t]) for t in range(4)], axis=0)
+
+
+def half_inverse(aug):
+    def panel(p, carry):
+        rows = pl.ds(pl.multiple_of(32 * p, 32), 32)
+        lines = aug[rows, :]
+        inverse = panel_inverse(pltpu.roll(lines[:, :LANES], LANES - 32 * p, 1))
+        lines = dot(inverse[:, :32], lines, precision=HIGHEST)
+        aug[rows, :] = lines
+        lane = lax.broadcasted_iota(jnp.int32, (32, LANES), 1)
+        upper = jnp.where(lane >= 32 * (p + 1), lines[:, :LANES], 0.0)
+        aug[...] = aug[...] - dot(upper, lines, ((0,), (0,)), HIGHEST)
+        return carry
+
+    lax.fori_loop(0, 4, panel, 0)
+
+
+def basis_kernel(entries, g_ref, vh_ref, vl_ref, w_ref, o_ref, aug, scr):
+    row = lax.broadcasted_iota(jnp.int32, (LANES, LANES), 0)
+    eye = (row == lax.broadcasted_iota(jnp.int32, (LANES, LANES), 1)).astype(jnp.float32)
+    scale = 1.0 / entries
+    aug[:, :LANES] = g_ref[:LANES, :LANES] * scale
+    aug[:, LANES:] = eye
+    half_inverse(aug)
+    first = aug[:, LANES:]
+    upper = dot(first, g_ref[:LANES, LANES:] * scale, precision=HIGHEST)
+    aug[:, :LANES] = g_ref[LANES:, LANES:] * scale - dot(upper, upper, ((0,), (0,)), HIGHEST)
+    aug[:, LANES:] = eye
+    half_inverse(aug)
+    second = aug[:, LANES:]
+    corner = dot(upper, first, ((0,), (0,)), HIGHEST)
+    w_ref[:LANES, :LANES] = first
+    w_ref[:LANES, LANES:] = jnp.zeros((LANES, LANES), jnp.float32)
+    w_ref[LANES:, :LANES] = -dot(second, corner, precision=HIGHEST)
+    w_ref[LANES:, LANES:] = second
     wh, wl = split(w_ref[...])
-    vh = vh_ref[...]
+    vh = vh_ref[OWN, :]
     scr[...] = dot(vh, wh, ((1,), (1,))) + (
-        dot(vh, wl, ((1,), (1,))) + dot(vl_ref[...], wh, ((1,), (1,)))
+        dot(vh, wl, ((1,), (1,))) + dot(vl_ref[OWN, :], wh, ((1,), (1,)))
     )
     for slab in range(4):
         for half in range(2):
             lanes = slice(half * 128, half * 128 + 128)
             pieces = []
-            for low in range(4):
-                rows = [
-                    scr[pair * 128 + low * 32 + slab * 8 : pair * 128 + low * 32 + slab * 8 + 8, lanes]
-                    for pair in range(16)
-                ]
-                pieces.append(jnp.concatenate(rows, axis=0))
+            for mid in range(2):
+                columns = []
+                for column in range(2):
+                    at = column * 64 + mid * 32 + slab * 8
+                    columns.append(
+                        jnp.concatenate(
+                            [scr[pair * 128 + at : pair * 128 + at + 8, lanes] for pair in range(16)], axis=0
+                        )
+                    )
+                pieces += [value.reshape(128, LANES) for value in halves(*columns)]
             for j, piece in enumerate(exchange(pieces, 32)):
                 o_ref[(half * 4 + j) * 4 + slab] = piece
 
 
-def apply_inverse(vh, vl, inverse):
+def basis(gram, entries, vh, vl):
     return pl.pallas_call(
-        apply_kernel,
-        out_shape=jax.ShapeDtypeStruct((32, 128, LANES), jnp.float32),
-        scratch_shapes=[pltpu.VMEM((2048, 256), jnp.float32)],
+        functools.partial(basis_kernel, entries),
+        out_shape=(
+            jax.ShapeDtypeStruct((256, 256), jnp.float32),
+            jax.ShapeDtypeStruct((32, 128, LANES), jnp.float32),
+        ),
+        scratch_shapes=[pltpu.VMEM((LANES, 256), jnp.float32), pltpu.VMEM((2048, 256), jnp.float32)],
         compiler_params=VMEM,
-        name="apply_inverse",
-    )(vh, vl, inverse)
-
-
-def total(square):
+        cost_estimate=pl.CostEstimate(flops=int(4e9), transcendentals=0, bytes_accessed=int(2e7)),
+        name="basis",
+    )(gram, vh, vl)
+
+
+def parts_of(square):
     count = lax.axis_size(ALL)
-    size = square.shape[0]
-    parts = square.reshape(count, size // count, size)
-    share = lax.all_to_all(parts, ALL, 0, 0, tiled=True).sum(0)
-    spread = jnp.broadcast_to(share[None], parts.shape)
-    return lax.all_to_all(spread, ALL, 0, 0, tiled=True).reshape(size, size)
+    return square.reshape(count, -1, square.shape[1])
+
+
+def swap(parts):
+    return lax.all_to_all(parts, ALL, 0, 0, tiled=True)
+
+
+def for_all(share):
+    return jnp.broadcast_to(share[None], (lax.axis_size(ALL),) + share.shape)
+
+
+def project_kernel(entries, moment_ref, w_ref, p_ref):
+    first = pl.multiple_of(32 * lax.axis_index("blk"), 32)
+    half_done = dot(w_ref[pl.ds(first, 32), :], moment_ref[...], precision=HIGHEST) * (1.0 / entries)
+    p_ref[...] = dot(half_done, w_ref[...], ((1,), (1,)), HIGHEST)
+
+
+def project(moment, inverse, entries):
+    return pl.pallas_call(
+        functools.partial(project_kernel, entries),
+        out_shape=jax.ShapeDtypeStruct((32, 256), jnp.float32),
+        compiler_params=VMEM,
+        name="project",
+    )(moment, inverse)
 
 
 def fast(states_in, region, onsite_table, hop_table, coupling_x, coupling_y):
-    slabs = lax.axis_size("slab")
-    device = lax.axis_index("blk") * slabs + lax.axis_index("slab")
-    codes = (region + 1).astype(jnp.float32)
-    codes = lax.all_to_all(jnp.broadcast_to(codes[None], (slabs,) + codes.shape), "slab", 0, 0, tiled=True)
-    codes = jnp.pad(codes.reshape(8, 1024), ((0, 0), (LEFT + 1, LANES)))
+    device = lax.axis_index("blk") * lax.axis_size("slab") + lax.axis_index("slab")
+    entries = float(BANDS * 8 * 1024)
+    codes = lax.all_gather((region + 1).astype(jnp.float32), "slab", axis=0, tiled=True)
+    received = swap(pack(states_in))
+    codes = jnp.pad(codes, ((0, 0), (LEFT + 1, LANES)))
     codes = lax.dynamic_slice(codes, (0, 32 * device), (8, LANES))
-    received = lax.all_to_all(pack(states_in), ALL, 0, 0, tiled=True)
     coef_high, coef_low = coefficients(codes, onsite_table, hop_table, coupling_x, coupling_y)
-    vh, vl, gram, moment = filtered_blocks(received, coef_high, coef_low)
-    entries = float(BANDS * 8 * 1024)
-    gram = total(gram) / entries
-    moment = total(moment) / entries
-    factor = jnp.linalg.cholesky(gram)
-    inverse = lax.linalg.triangular_solve(
-        factor, jnp.eye(256, dtype=jnp.float32), left_side=True, lower=True
-    )
-    states_out = unpack(lax.all_to_all(apply_inverse(vh, vl, inverse), ALL, 0, 0, tiled=True))
-    mine = lax.dynamic_slice_in_dim(inverse, lax.axis_index("blk") * 32, 32, 0)
-    projected = dot(dot(mine, moment, precision=HIGHEST), inverse, ((1,), (1,)), HIGHEST)
+    vh, vl, own_gram = filtered_blocks(received, coef_high, coef_low)
+    own_moment = moment_of(vh, vl, coef_high, coef_low, own_gram)
+    share = swap(parts_of(own_gram)).sum(0)
+    both = swap(jnp.concatenate([for_all(share), parts_of(own_moment)], axis=1))
+    inverse, blocks = basis(both[:, :8].reshape(256, 256), entries, vh, vl)
+    moment = swap(for_all(both[:, 8:].sum(0))).reshape(256, 256)
+    blocks, moment = lax.optimization_barrier((blocks, moment))
+    states_out = unpack(swap(blocks))
+    projected = project(moment, inverse, entries)
     return states_out, projected
 
 

time: 288 us -> 210 us (0.73)
  other arithmetic: 55.5 us -> 1.76 us
  waiting for transfers between devices: 122 us -> 97 us
  blocking collectives: 15 us -> 26.4 us
  local copies, waits for them, and re-layouts: 9.64 us -> 5.01 us
  starting transfers between devices: 24.6 us -> 20.8 us
    another operation x10 -> x0, other arithmetic: 54.6 us -> none  [the longest x6 33.9 us: fast(): factor = jnp.linalg.cholesky(gram)]
    all_to_all x6 -> x4, waiting for transfers between devices: 122 us -> 97 us  [swap(): return lax.all_to_all(parts, ALL, 0, 0, tiled=True)]
    all_gather x0 -> x1, blocking collectives: none -> 8.62 us  [fast(): lax.all_gather((region + 1).astype(jnp.float32), 'slab', axis=0, tiled=True)]
    another operation x9 -> x0, local copies, waits for them, and re-layouts: 3.88 us -> none
    all_to_all x6 -> x4, starting transfers between devices: 24.6 us -> 20.8 us  [swap(): return lax.all_to_all(parts, ALL, 0, 0, tiled=True)]
    pallas_call x2 -> x4, Pallas kernels: 36.8 us -> 40.6 us  [the longest x1 16.1 us: filtered_blocks(): pl.pallas_call(filter_kernel, out_shape=(half, half, square), scratch_sha...]
  transfers between devices with their start and end apart: 6 -> 4, of which waited for: 4 -> 3; matrix products, arithmetic and copies ran while one was open for 22% -> 0% of each run, Pallas kernels for 6% -> 15%
where the time goes in v2:
time: 210 us; the launch traced here: 209 us
  waiting for transfers between devices  97 us (46%)
  Pallas kernels  57.4 us (27%)
  blocking collectives  26.4 us (13%)
  starting transfers between devices  20.8 us (10%)
  local copies, waits for them, and re-layouts  5.01 us (2%)
    all_to_all x4, waiting for transfers between devices, swap(): return lax.all_to_all(parts, ALL, 0, 0, tiled=True)  97 us
    all_to_all x4, starting transfers between devices, swap(): return lax.all_to_all(parts, ALL, 0, 0, tiled=True)  20.8 us
    all_to_all x1, blocking collectives, swap(): return lax.all_to_all(parts, ALL, 0, 0, tiled=True)  17.8 us
    pallas_call x1, Pallas kernels, filtered_blocks(): pl.pallas_call(filter_kernel, out_shape=(half, half, square), scratch_sha...  16.1 us
    pallas_call x1, Pallas kernels, basis(): pl.pallas_call(functools.partial(basis_kernel, entries), out_shape=(jax.S...  15.6 us
    all_gather x1, blocking collectives, fast(): lax.all_gather((region + 1).astype(jnp.float32), 'slab', axis=0, tiled=True)  8.62 us
    pallas_call x1, Pallas kernels, coefficients(): pl.pallas_call(coef_kernel, out_shape=(shape, shape), compiler_params=VME...  7.09 us
    pallas_call x1, Pallas kernels, moment_of(): pl.pallas_call(moment_kernel, out_shape=jax.ShapeDtypeStruct((256, 256),...  6.52 us
  transfers between devices with their start and end apart: 4, of which 3 were waited for; matrix products, arithmetic and copies ran while one was open for 0% of the time, Pallas kernels for 15%

profile of v2, /device:TPU:0, one launch (start us, length us, event | category | flops | bytes accessed | tf_op | source)
XLA Modules:
  0.0 209.0 jit_solution(3151752178158494900)
XLA Ops:
  0.6 4.6 %pack.1 = f32[32,168,128]{2,1,0:T(8,128)} custom-call(f32[4096,128]{1,0:T(8,128)} %bitcast.19), custom_call_target="tpu_custom_call" | custom-call | tf_op jit(solution)/shard_map/pack/pallas_call | solution.py:72
  5.2 0.0 copy-start.3
  5.2 7.3 %all-to-all-start = ((f32[32,168,128]{2,1,0:T(8,128)}), f32[32,168,128]{2,1,0:T(8,128)S(1)}, u32[]{:S(2)}, u32[]{:S(2)}) async-start(f32[32,168,128]{2,1,0:T(8,128)} %pack.1), calls=%async_computation | async-start | bytes 5505024 | tf_op jit(solution)/shard_map/all_to_all | solution.py:411
  12.5 0.0 copy-done.3
  12.5 8.6 %all-gather = f32[4,2,1024]{2,1,0:T(2,128)S(1)} all-gather(f32[1,2,1024]{2,1,0:T(2,128)S(1)} %convert_bitcast_fusion), channel_id=1, replica_groups=mesh['blk'=8,'slab'=4] {'slab'}, dimensions={0}, use_global_device_ids=true | all-gather | bytes 40960 | tf_op jit(solution)/shard_map/all_gather | solution.py:436
  21.2 0.7 pad_dynamic-slice_fusion.reg_ref
  21.9 7.1 %coefficients.1 = (bf16[21,128,256]{2,1,0:T(8,128)(2,1)}, bf16[21,128,256]{2,1,0:T(8,128)(2,1)}) custom-call(f32[8,128]{1,0:T(8,128)} %pad_dynamic-slice_fusion.reg_ref, f32[4,8,8]{2,1,0:T(8,128)} %onsite_ref.1, f32[4,8]{1,0:T(4,128)} %hop_ref.1, f32[8,8]{1,0:T(8,128)} %kx_ref.1, f32[8,8]{1,0:T(8,128)} %ky_ref.1), custom_call_target="tpu_custom_call" | custom-call | tf_op jit(solution)/shard_map/coefficients/pallas_call | solution.py:181
  28.9 46.7 %all-to-all-done.r_ref = f32[32,168,128]{2,1,0:T(8,128)S(1)} async-done(((f32[32,168,128]{2,1,0:T(8,128)}), f32[32,168,128]{2,1,0:T(8,128)S(1)}, u32[]{:S(2)}, u32[]{:S(2)}) %all-to-all-start) | async-done | bytes 2752544 | tf_op jit(solution)/shard_map/all_to_all | solution.py:411
  75.6 0.0 copy-start
  75.6 1.5 copy-done
  77.2 16.1 %filtered.1 = (bf16[2816,256]{1,0:T(8,128)(2,1)}, bf16[2816,256]{1,0:T(8,128)(2,1)}, f32[256,256]{1,0:T(8,128)}) custom-call(f32[32,168,128]{2,1,0:T(8,128)} %copy-done, bf16[21,128,256]{2,1,0:T(8,128)(2,1)} %get-tuple-element.11.ch_ref, bf16[21,128,256]{2,1,0:T(8,128)(2,1)} %get-tuple-element.12.cl_ref), custom_call_target="tpu_custom_call" | custom-call | tf_op jit(solution)/shard_map/filtered/pallas_call | solution.py:255
  93.3 4.6 %all-to-all-start.1 = ((f32[32,8,256]{2,1,0:T(8,128)}), f32[32,8,256]{2,1,0:T(8,128)S(1)}, u32[]{:S(2)}, u32[]{:S(2)}) async-start(f32[32,8,256]{2,1,0:T(8,128)} %bitcast.22), calls=%async_computation.1 | async-start | bytes 524288 | tf_op jit(solution)/shard_map/all_to_all | solution.py:411
  97.9 6.5 %moment.1 = f32[256,256]{1,0:T(8,128)} custom-call(bf16[2816,256]{1,0:T(8,128)(2,1)} %get-tuple-element.14.vh_ref, bf16[2816,256]{1,0:T(8,128)(2,1)} %get-tuple-element.15.vl_ref, bf16[21,128,256]{2,1,0:T(8,128)(2,1)} %get-tuple-element.11.ch_ref, bf16[21,128,256]{2,1,0:T(8,128)(2,1)} %get-tuple-element.12.cl_ref, f32[256,256]{1,0:T(8,128)} %get-tuple-element.13.g_ref), custom_call_target="tpu_custom_call" | custom-call | flops 4000000000 | bytes 10000000 | tf_op jit(solution)/shard_map/moment/pallas_call | solution.py:295
  104.4 3.9 %all-to-all-done.1 = f32[32,8,256]{2,1,0:T(8,128)S(1)} async-done(((f32[32,8,256]{2,1,0:T(8,128)}), f32[32,8,256]{2,1,0:T(8,128)S(1)}, u32[]{:S(2)}, u32[]{:S(2)}) %all-to-all-start.1) | async-done | bytes 262176 | tf_op jit(solution)/shard_map/all_to_all | solution.py:411
  108.3 1.0 pad_maximum_fusion
  109.3 17.8 %all_to_all.25 = f32[32,16,256]{2,1,0:T(8,128)S(1)} all-to-all(f32[32,16,256]{2,1,0:T(8,128)S(1)} %pad_maximum_fusion), channel_id=1, replica_groups=mesh['blk'=8,'slab'=4] {'blk','slab'}, dimensions={0} | all-to-all | bytes 1048576 | tf_op jit(solution)/shard_map/all_to_all | solution.py:411
  127.1 0.7 slice_reduce_fusion
  127.8 0.7 broadcast_in_dim.5
  128.5 3.1 %all-to-all-start.3 = ((f32[32,8,256]{2,1,0:T(8,128)}), f32[32,8,256]{2,1,0:T(8,128)S(1)}, u32[]{:S(2)}, u32[]{:S(2)}) async-start(f32[32,8,256]{2,1,0:T(8,128)} %broadcast_in_dim.5), calls=%async_computation.3 | async-start | bytes 524288 | tf_op jit(solution)/shard_map/all_to_all | solution.py:411
  131.6 15.6 %basis.1 = (f32[256,256]{1,0:T(8,128)}, f32[32,128,128]{2,1,0:T(8,128)}) custom-call(f32[256,256]{1,0:T(8,128)} %get-tuple-element.21.g_ref, bf16[2816,256]{1,0:T(8,128)(2,1)} %get-tuple-element.14.vh_ref, bf16[2816,256]{1,0:T(8,128)(2,1)} %get-tuple-element.15.vl_ref), custom_call_target="tpu_custom_call" | custom-call | flops 4000000000 | bytes 20000000 | tf_op jit(solution)/shard_map/basis/pallas_call | solution.py:392
  147.2 0.0 all-to-all-done.3
  147.2 0.0 copy-start.2
  147.2 0.7 copy-done.2
  147.9 5.8 %all-to-all-start.4 = ((f32[32,128,128]{2,1,0:T(8,128)}), f32[32,128,128]{2,1,0:T(8,128)S(1)}, u32[]{:S(2)}, u32[]{:S(2)}) async-start(f32[32,128,128]{2,1,0:T(8,128)} %get-tuple-element.17), calls=%async_computation.4 | async-start | bytes 4194304 | tf_op jit(solution)/shard_map/all_to_all | solution.py:411
  153.8 2.4 %project.1 = f32[32,256]{1,0:T(8,128)} custom-call(f32[256,256]{1,0:T(8,128)} %bitcast.21, f32[256,256]{1,0:T(8,128)} %get-tuple-element.19.w_ref), custom_call_target="tpu_custom_call" | custom-call | tf_op jit(solution)/shard_map/project/pallas_call | solution.py:425
  156.1 46.4 %all-to-all-done.4 = f32[32,128,128]{2,1,0:T(8,128)S(1)} async-done(((f32[32,128,128]{2,1,0:T(8,128)}), f32[32,128,128]{2,1,0:T(8,128)S(1)}, u32[]{:S(2)}, u32[]{:S(2)}) %all-to-all-start.4) | async-done | bytes 2097184 | tf_op jit(solution)/shard_map/all_to_all | solution.py:411
  202.6 0.0 copy-start.1
  202.6 1.3 copy-done.1
  203.9 5.1 %unpack.1 = f32[4096,128]{1,0:T(8,128)} custom-call(f32[4096,128]{1,0:T(8,128)} %bitcast.18), custom_call_target="tpu_custom_call" | custom-call | tf_op jit(solution)/shard_map/unpack/pallas_call | solution.py:93
  (4 shorter events, 0.1 us)
Async XLA Ops:
  5.2 7.3 %copy-start.3 = (s32[2,1024]{1,0:T(2,128)S(1)}, s32[2,1024]{1,0:T(2,128)}, u32[]{:S(2)}) copy-start(s32[2,1024]{1,0:T(2,128)} %param.7) | copy-start | bytes 24580
  5.2 70.4 %all-to-all-start = ((f32[32,168,128]{2,1,0:T(8,128)}), f32[32,168,128]{2,1,0:T(8,128)S(1)}, u32[]{:S(2)}, u32[]{:S(2)}) async-start(f32[32,168,128]{2,1,0:T(8,128)} %pack.1), calls=%async_computation | async-start | bytes 5505024 | tf_op jit(solution)/shard_map/all_to_all | solution.py:411
  75.6 1.5 copy-start
  93.3 15.0 %all-to-all-start.1 = ((f32[32,8,256]{2,1,0:T(8,128)}), f32[32,8,256]{2,1,0:T(8,128)S(1)}, u32[]{:S(2)}, u32[]{:S(2)}) async-start(f32[32,8,256]{2,1,0:T(8,128)} %bitcast.22), calls=%async_computation.1 | async-start | bytes 524288 | tf_op jit(solution)/shard_map/all_to_all | solution.py:411
  128.5 18.7 %all-to-all-start.3 = ((f32[32,8,256]{2,1,0:T(8,128)}), f32[32,8,256]{2,1,0:T(8,128)S(1)}, u32[]{:S(2)}, u32[]{:S(2)}) async-start(f32[32,8,256]{2,1,0:T(8,128)} %broadcast_in_dim.5), calls=%async_computation.3 | async-start | bytes 524288 | tf_op jit(solution)/shard_map/all_to_all | solution.py:411
  147.2 0.7 copy-start.2
  147.9 54.6 %all-to-all-start.4 = ((f32[32,128,128]{2,1,0:T(8,128)}), f32[32,128,128]{2,1,0:T(8,128)S(1)}, u32[]{:S(2)}, u32[]{:S(2)}) async-start(f32[32,128,128]{2,1,0:T(8,128)} %get-tuple-element.17), calls=%async_computation.4 | async-start | bytes 4194304 | tf_op jit(solution)/shard_map/all_to_all | solution.py:411
  202.6 1.3 copy-start.1

commit v3 on v2

--- a/solution.py
+++ b/solution.py
@@ -16,10 +16,16 @@
 ALL = ("blk", "slab")
 LEFT = 4
 WINDOW = 42
-VMEM = pltpu.CompilerParams(vmem_limit_bytes=56 * 1024 * 1024)
+VMEM = pltpu.CompilerParams(vmem_limit_bytes=24 * 1024 * 1024)
+ON_CHIP = pl.BlockSpec(memory_space=pltpu.VMEM)
+OFF_CHIP = pl.BlockSpec(memory_space=pltpu.HBM)
 HIGHEST = lax.Precision.HIGHEST
-UNROLL = 3
+UNROLL = 7
 OWN = slice(2 * 128 + 64, 18 * 128 + 64)
+
+
+def off_chip(*arrays):
+    return [pltpu.with_memory_space_constraint(array, pltpu.HBM) for array in arrays]
 
 
 def dot(left, right, dims=((1,), (0,)), precision=None):
@@ -50,49 +56,82 @@
     return pieces
 
 
-def pack_kernel(x_ref, o_ref, scr):
+def pack_kernel(x_ref, o_ref, buf, scr, in_sem, out_sem):
+    loads = [
+        pltpu.make_async_copy(x_ref.at[:, pl.ds(8 * part, 8), :], buf.at[part], in_sem.at[part])
+        for part in range(2)
+    ]
+    for load in loads:
+        load.start()
     scr[0 : LEFT * 4, :] = jnp.zeros((LEFT * 4, LANES), jnp.float32)
     tail = (LEFT + 1024) * 4
     scr[tail:, :] = jnp.zeros((scr.shape[0] - tail, LANES), jnp.float32)
-    for tile in range(8):
-        for r in range(4):
-            row, high = r // 2, r % 2
-            parts = [
-                x_ref[pl.ds(((high * 4 + low) * 8 + tile) * 2 + row, 32, stride=128), :]
-                for low in range(4)
-            ]
-            turned = jnp.concatenate(parts, axis=0).T
-            scr[pl.ds((LEFT + 128 * tile) * 4 + r, 128, stride=4), :] = turned
-    for d in range(32):
-        o_ref[d] = scr[128 * d : 128 * d + WINDOW * 4, :]
+    sends = [
+        pltpu.make_async_copy(scr.at[pl.ds(128 * d, WINDOW * 4), :], o_ref.at[d], out_sem.at[d])
+        for d in range(32)
+    ]
+    for part in range(2):
+        loads[part].wait()
+        rows = buf.at[part].reshape(2048, LANES)
+        for tile in range(4):
+            for r in range(4):
+                row, high = r // 2, r % 2
+                parts = [
+                    rows[pl.ds((high * 4 + low) * 8 + tile * 2 + row, 32, stride=64), :]
+                    for low in range(4)
+                ]
+                turned = jnp.concatenate(parts, axis=0).T
+                scr[pl.ds((LEFT + 512 * part + 128 * tile) * 4 + r, 128, stride=4), :] = turned
+        for send in sends[15 * part : 15 + 17 * part]:
+            send.start()
+    for send in sends:
+        send.wait()
 
 
 def pack(x):
-    rows = x.reshape(32, 8, 2, 8, LANES).transpose(0, 1, 3, 2, 4).reshape(4096, LANES)
+    rows = x.reshape(32, 8, 2, 8, LANES).transpose(0, 1, 3, 2, 4).reshape(256, 16, LANES)
     return pl.pallas_call(
         pack_kernel,
-        out_shape=jax.ShapeDtypeStruct((32, WINDOW * 4, LANES), jnp.float32),
-        scratch_shapes=[pltpu.VMEM((4136, LANES), jnp.float32)],
+        out_shape=pltpu.HBM((32, WINDOW * 4, LANES), jnp.float32),
+        in_specs=[OFF_CHIP],
+        out_specs=OFF_CHIP,
+        scratch_shapes=[
+            pltpu.VMEM((2, 256, 8, LANES), jnp.float32),
+            pltpu.VMEM((4136, LANES), jnp.float32),
+            pltpu.SemaphoreType.DMA((2,)),
+            pltpu.SemaphoreType.DMA((32,)),
+        ],
         compiler_params=VMEM,
         name="pack",
-    )(rows)
-
-
-def unpack_kernel(r_ref, o_ref):
-    for tile in range(8):
-        for r in range(4):
-            row, high = r // 2, r % 2
-            turned = r_ref[pl.ds(tile * 512 + r, 128, stride=4), :].T
-            for low in range(4):
-                o_ref[pl.ds(((high * 4 + low) * 8 + tile) * 2 + row, 32, stride=128), :] = turned[
-                    32 * low : 32 * low + 32
-                ]
+    )(*off_chip(rows))
+
+
+def unpack_kernel(r_ref, o_ref, buf, sem):
+    stores = []
+    for high in range(2):
+        rows = buf.at[high].reshape(2048, LANES)
+        for tile in range(8):
+            for row in range(2):
+                turned = r_ref[pl.ds(tile * 512 + row * 2 + high, 128, stride=4), :].T
+                for low in range(4):
+                    rows[pl.ds((low * 8 + tile) * 2 + row, 32, stride=64), :] = turned[
+                        32 * low : 32 * low + 32
+                    ]
+        stores.append(
+            pltpu.make_async_copy(buf.at[high], o_ref.at[:, pl.ds(64 * high, 64), :], sem.at[high])
+        )
+        stores[high].start()
+    for store in stores:
+        store.wait()
 
 
 def unpack(blocks):
     rows = pl.pallas_call(
         unpack_kernel,
-        out_shape=jax.ShapeDtypeStruct((4096, LANES), jnp.float32),
+        out_shape=pltpu.HBM((32, 128, LANES), jnp.float32),
+        in_specs=[ON_CHIP],
+        out_specs=OFF_CHIP,
+        scratch_shapes=[pltpu.VMEM((2, 32, 64, LANES), jnp.float32), pltpu.SemaphoreType.DMA((2,))],
         compiler_params=VMEM,
         name="unpack",
     )(blocks.reshape(4096, LANES))
@@ -177,9 +216,12 @@
 
 
 def coefficients(reg, onsite_table, hop_table, coupling_x, coupling_y):
-    shape = jax.ShapeDtypeStruct((WINDOW // 2, 128, 256), jnp.bfloat16)
+    shape = pltpu.HBM((WINDOW // 2, 128, 256), jnp.bfloat16)
     return pl.pallas_call(
-        coef_kernel, out_shape=(shape, shape), compiler_params=VMEM, name="coefficients"
+        coef_kernel,
+        out_shape=(shape, shape),
+        compiler_params=VMEM,
+        name="coefficients",
     )(reg, onsite_table, hop_table, coupling_x, coupling_y)
 
 
@@ -192,7 +234,15 @@
     )
 
 
-def filter_kernel(r_ref, ch_ref, cl_ref, vh_ref, vl_ref, g_ref, fa, fb, ah, al, bh, bl):
+def filter_kernel(
+    r_ref, ch_hbm, cl_hbm, vh_hbm, vl_hbm, g_ref, ch_ref, cl_ref, fa, fb, ah, al, bh, bl, sem
+):
+    loads = [
+        pltpu.make_async_copy(ch_hbm, ch_ref, sem.at[0]),
+        pltpu.make_async_copy(cl_hbm, cl_ref, sem.at[1]),
+    ]
+    for load in loads:
+        load.start()
     pairs = WINDOW // 2
     block = 128
     edge = 64
@@ -200,16 +250,23 @@
     for ref in (ah, al, bh, bl):
         ref[0:edge, :] = zero
         ref[pairs * block + edge :, :] = zero
-    for slab in range(4):
+    def ingest(pair, carry):
+        at = pl.multiple_of(pair * block, block)
+        source = pl.ds(pl.multiple_of(pair * 8, 8), 8)
         for half in range(2):
             lanes = slice(half * 128, half * 128 + 128)
-            pieces = exchange([r_ref[(half * 4 + j) * 4 + slab] for j in range(4)], 32)
-            for mid in range(2):
-                for column, piece in enumerate(halves(pieces[2 * mid], pieces[2 * mid + 1])):
-                    for pair in range(pairs):
-                        at = pair * block + column * 64 + mid * 32 + slab * 8
-                        fa[at : at + 8, lanes] = piece[pair]
-    ah[edge : pairs * block + edge, :], al[edge : pairs * block + edge, :] = split(fa[...])
+            for slab in range(4):
+                pieces = exchange([r_ref[(half * 4 + j) * 4 + slab, source, :] for j in range(4)], 32)
+                for mid in range(2):
+                    for column, piece in enumerate(halves(pieces[2 * mid], pieces[2 * mid + 1])):
+                        fa[pl.ds(at + (column * 64 + mid * 32 + slab * 8), 8), lanes] = piece[0]
+        rows = pl.ds(at + edge, block)
+        ah[rows, :], al[rows, :] = split(fa[pl.ds(at, block), :])
+        return carry
+
+    lax.fori_loop(0, pairs, ingest, 0, unroll=3)
+    for load in loads:
+        load.wait()
 
     def product(pair, high, low):
         rows = pl.ds(pair * block, 256)
@@ -241,25 +298,35 @@
     lax.fori_loop(1, pairs - 1, later(bh, bl, fa, ah, al), 0, unroll=UNROLL)
     lax.fori_loop(1, pairs - 1, later(ah, al, fb, bh, bl), 0, unroll=UNROLL)
     lax.fori_loop(2, pairs - 2, later(bh, bl, fa, ah, al), 0, unroll=UNROLL)
-    vh_ref[...] = ah[...]
-    vl_ref[...] = al[...]
+    stores = [
+        pltpu.make_async_copy(ah, vh_hbm, sem.at[2]),
+        pltpu.make_async_copy(al, vl_hbm, sem.at[3]),
+    ]
+    for store_out in stores:
+        store_out.start()
     dims = ((0,), (0,))
     cross = dot(ah[OWN, :], al[OWN, :], dims)
     g_ref[...] = dot(ah[OWN, :], ah[OWN, :], dims) + (cross + cross.T)
+    for store_out in stores:
+        store_out.wait()
 
 
 def filtered_blocks(received, coef_high, coef_low):
     rows = (WINDOW // 2) * 128
-    half = jax.ShapeDtypeStruct((rows + 128, 256), jnp.bfloat16)
+    half = pltpu.HBM((rows + 128, 256), jnp.bfloat16)
     square = jax.ShapeDtypeStruct((256, 256), jnp.float32)
     return pl.pallas_call(
         filter_kernel,
         out_shape=(half, half, square),
-        scratch_shapes=[pltpu.VMEM((rows, 256), jnp.float32)] * 2
-        + [pltpu.VMEM((rows + 128, 256), jnp.bfloat16)] * 4,
+        scratch_shapes=[pltpu.VMEM((WINDOW // 2, 128, 256), jnp.bfloat16)] * 2
+        + [pltpu.VMEM((rows, 256), jnp.float32)] * 2
+        + [pltpu.VMEM((rows + 128, 256), jnp.bfloat16)] * 4
+        + [pltpu.SemaphoreType.DMA((4,))],
+        in_specs=[ON_CHIP, OFF_CHIP, OFF_CHIP],
+        out_specs=(OFF_CHIP, OFF_CHIP, ON_CHIP),
         compiler_params=VMEM,
         name="filtered",
-    )(received, coef_high, coef_low)
+    )(received, *off_chip(coef_high, coef_low))
 
 
 def moment_kernel(vh_ref, vl_ref, ch_ref, cl_ref, g_ref, m_ref, bh, bl):
@@ -299,7 +366,7 @@
         compiler_params=VMEM,
         cost_estimate=pl.CostEstimate(flops=int(4e9), transcendentals=0, bytes_accessed=int(1e7)),
         name="moment",
-    )(vh, vl, coef_high, coef_low, gram)
+    )(*off_chip(vh, vl, coef_high, coef_low), gram)
 
 
 def panel_inverse(block):
@@ -347,32 +414,41 @@
     lax.fori_loop(0, 4, panel, 0)
 
 
-def basis_kernel(entries, g_ref, vh_ref, vl_ref, w_ref, o_ref, aug, scr):
+def basis_kernel(entries, both_ref, vh_hbm, vl_hbm, w_ref, o_hbm, gram, aug, vh, vl, scr, out, sem, out_sem):
+    loads = [
+        pltpu.make_async_copy(vh_hbm.at[OWN, :], vh, sem.at[0]),
+        pltpu.make_async_copy(vl_hbm.at[OWN, :], vl, sem.at[1]),
+    ]
+    for load in loads:
+        load.start()
     row = lax.broadcasted_iota(jnp.int32, (LANES, LANES), 0)
     eye = (row == lax.broadcasted_iota(jnp.int32, (LANES, LANES), 1)).astype(jnp.float32)
-    scale = 1.0 / entries
-    aug[:, :LANES] = g_ref[:LANES, :LANES] * scale
+    gram[...] = both_ref[:, 0:8, :].reshape(256, 256) * (1.0 / entries)
+    aug[:, :LANES] = gram[:LANES, :LANES]
     aug[:, LANES:] = eye
     half_inverse(aug)
     first = aug[:, LANES:]
-    upper = dot(first, g_ref[:LANES, LANES:] * scale, precision=HIGHEST)
-    aug[:, :LANES] = g_ref[LANES:, LANES:] * scale - dot(upper, upper, ((0,), (0,)), HIGHEST)
+    upper = dot(first, gram[:LANES, LANES:], precision=HIGHEST)
+    aug[:, :LANES] = gram[LANES:, LANES:] - dot(upper, upper, ((0,), (0,)), HIGHEST)
     aug[:, LANES:] = eye
+    corner = dot(upper, first, ((0,), (0,)), HIGHEST)
     half_inverse(aug)
     second = aug[:, LANES:]
-    corner = dot(upper, first, ((0,), (0,)), HIGHEST)
     w_ref[:LANES, :LANES] = first
     w_ref[:LANES, LANES:] = jnp.zeros((LANES, LANES), jnp.float32)
     w_ref[LANES:, :LANES] = -dot(second, corner, precision=HIGHEST)
     w_ref[LANES:, LANES:] = second
-    wh, wl = split(w_ref[...])
-    vh = vh_ref[OWN, :]
-    scr[...] = dot(vh, wh, ((1,), (1,))) + (
-        dot(vh, wl, ((1,), (1,))) + dot(vl_ref[OWN, :], wh, ((1,), (1,)))
-    )
-    for slab in range(4):
-        for half in range(2):
-            lanes = slice(half * 128, half * 128 + 128)
+    for load in loads:
+        load.wait()
+    sends = [pltpu.make_async_copy(out.at[d], o_hbm.at[d], out_sem.at[d]) for d in range(32)]
+    for half in range(2):
+        used = LANES * (half + 1)
+        wh, wl = split(w_ref[LANES * half : used, :used])
+        values = [vh[:, :used], vl[:, :used], vh[:, :used]]
+        scr[...] = dot(
+            jnp.concatenate(values, axis=1), jnp.concatenate([wh, wh, wl], axis=1), ((1,), (1,))
+        )
+        for slab in range(4):
             pieces = []
             for mid in range(2):
                 columns = []
@@ -380,26 +456,41 @@
                     at = column * 64 + mid * 32 + slab * 8
                     columns.append(
                         jnp.concatenate(
-                            [scr[pair * 128 + at : pair * 128 + at + 8, lanes] for pair in range(16)], axis=0
+                            [scr[pair * 128 + at : pair * 128 + at + 8, :] for pair in range(16)], axis=0
                         )
                     )
                 pieces += [value.reshape(128, LANES) for value in halves(*columns)]
             for j, piece in enumerate(exchange(pieces, 32)):
-                o_ref[(half * 4 + j) * 4 + slab] = piece
-
-
-def basis(gram, entries, vh, vl):
+                d = (half * 4 + j) * 4 + slab
+                out[d] = piece
+                sends[d].start()
+    for send in sends:
+        send.wait()
+
+
+def basis(both, entries, vh, vl):
     return pl.pallas_call(
         functools.partial(basis_kernel, entries),
         out_shape=(
             jax.ShapeDtypeStruct((256, 256), jnp.float32),
-            jax.ShapeDtypeStruct((32, 128, LANES), jnp.float32),
+            pltpu.HBM((32, 128, LANES), jnp.float32),
         ),
-        scratch_shapes=[pltpu.VMEM((LANES, 256), jnp.float32), pltpu.VMEM((2048, 256), jnp.float32)],
+        in_specs=[ON_CHIP, OFF_CHIP, OFF_CHIP],
+        out_specs=(ON_CHIP, OFF_CHIP),
+        scratch_shapes=[
+            pltpu.VMEM((256, 256), jnp.float32),
+            pltpu.VMEM((LANES, 256), jnp.float32),
+            pltpu.VMEM((2048, 256), jnp.bfloat16),
+            pltpu.VMEM((2048, 256), jnp.bfloat16),
+            pltpu.VMEM((2048, LANES), jnp.float32),
+            pltpu.VMEM((32, LANES, LANES), jnp.float32),
+            pltpu.SemaphoreType.DMA((2,)),
+            pltpu.SemaphoreType.DMA((32,)),
+        ],
         compiler_params=VMEM,
         cost_estimate=pl.CostEstimate(flops=int(4e9), transcendentals=0, bytes_accessed=int(2e7)),
         name="basis",
-    )(gram, vh, vl)
+    )(both, *off_chip(vh, vl))
 
 
 def parts_of(square):
@@ -425,6 +516,8 @@
     return pl.pallas_call(
         functools.partial(project_kernel, entries),
         out_shape=jax.ShapeDtypeStruct((32, 256), jnp.float32),
+        in_specs=[ON_CHIP] * 2,
+        out_specs=ON_CHIP,
         compiler_params=VMEM,
         name="project",
     )(moment, inverse)
@@ -442,7 +535,7 @@
     own_moment = moment_of(vh, vl, coef_high, coef_low, own_gram)
     share = swap(parts_of(own_gram)).sum(0)
     both = swap(jnp.concatenate([for_all(share), parts_of(own_moment)], axis=1))
-    inverse, blocks = basis(both[:, :8].reshape(256, 256), entries, vh, vl)
+    inverse, blocks = basis(both, entries, vh, vl)
     moment = swap(for_all(both[:, 8:].sum(0))).reshape(256, 256)
     blocks, moment = lax.optimization_barrier((blocks, moment))
     states_out = unpack(swap(blocks))

time: 210 us -> 197 us (0.938)
  Pallas kernels: 57.4 us -> 47.4 us
  local copies, waits for them, and re-layouts: 5.01 us -> 0.88 us
  waiting for transfers between devices: 97 us -> 100 us
    unnamed x9 -> x11, local copies, waits for them, and re-layouts: 3.6 us -> 0.06 us
    pallas_call x2, Pallas kernels: 9.69 us -> 6.57 us  [the longest x1 4.04 us: pack(): pl.pallas_call(pack_kernel, out_shape=pltpu.HBM((32, WINDOW * 4, LANES),...]
    all_to_all x4, waiting for transfers between devices: 97 us -> 100 us  [swap(): return lax.all_to_all(parts, ALL, 0, 0, tiled=True)]
    pallas_call x1, Pallas kernels: 16.1 us -> 13.7 us  [filtered_blocks(): pl.pallas_call(filter_kernel, out_shape=(half, half, square), scratch_sha...]
  transfers between devices with their start and end apart: 4 -> 4, of which waited for: 3 -> 3; matrix products, arithmetic and copies ran while one was open for 0% -> 0% of each run, Pallas kernels for 15% -> 14%
where the time goes in v3:
time: 197 us
  waiting for transfers between devices  100 us (51%)
  Pallas kernels  47.4 us (24%)
  blocking collectives  26.4 us (13%)
  starting transfers between devices  20.8 us (11%)
    all_to_all x4, waiting for transfers between devices, swap(): return lax.all_to_all(parts, ALL, 0, 0, tiled=True)  100 us
    all_to_all x4, starting transfers between devices, swap(): return lax.all_to_all(parts, ALL, 0, 0, tiled=True)  20.8 us
    all_to_all x1, blocking collectives, swap(): return lax.all_to_all(parts, ALL, 0, 0, tiled=True)  17.8 us
    pallas_call x1, Pallas kernels, filtered_blocks(): pl.pallas_call(filter_kernel, out_shape=(half, half, square), scratch_sha...  13.7 us
    pallas_call x1, Pallas kernels, basis(): pl.pallas_call(functools.partial(basis_kernel, entries), out_shape=(jax.S...  13.7 us
    all_gather x1, blocking collectives, fast(): lax.all_gather((region + 1).astype(jnp.float32), 'slab', axis=0, tiled=True)  8.62 us
    pallas_call x1, Pallas kernels, coefficients(): pl.pallas_call(coef_kernel, out_shape=(shape, shape), compiler_params=VME...  6.34 us
    pallas_call x1, Pallas kernels, moment_of(): pl.pallas_call(moment_kernel, out_shape=jax.ShapeDtypeStruct((256, 256),...  5.81 us
  transfers between devices with their start and end apart: 4, of which 3 were waited for; matrix products, arithmetic and copies ran while one was open for 0% of the time, Pallas kernels for 14%

profile of v3, /device:TPU:0, one launch (start us, length us, event | category | flops | bytes accessed | tf_op | source)
XLA Modules:
  0.0 196.6 jit_solution(5894923471893989649)
XLA Ops:
  0.6 4.0 %pack.1 = f32[32,168,128]{2,1,0:T(8,128)} custom-call(f32[256,16,128]{2,1,0:T(8,128)} %bitcast.19), custom_call_target="tpu_custom_call" | custom-call | tf_op jit(solution)/shard_map/pack/pallas_call | solution.py:93
  4.7 0.0 copy-start.4
  4.7 0.0 copy-start
  4.7 0.0 copy-start.1
  4.7 0.0 copy-start.2
  4.7 0.0 copy-start.3
  4.7 7.3 %all-to-all-start = ((f32[32,168,128]{2,1,0:T(8,128)}), f32[32,168,128]{2,1,0:T(8,128)S(1)}, u32[]{:S(2)}, u32[]{:S(2)}) async-start(f32[32,168,128]{2,1,0:T(8,128)} %pack.1), calls=%async_computation | async-start | bytes 5505024 | tf_op jit(solution)/shard_map/all_to_all | solution.py:502
  12.1 0.0 copy-done.4
  12.1 8.6 %all-gather = f32[4,2,1024]{2,1,0:T(2,128)S(1)} all-gather(f32[1,2,1024]{2,1,0:T(2,128)S(1)} %convert_bitcast_fusion), channel_id=1, replica_groups=mesh['blk'=8,'slab'=4] {'slab'}, dimensions={0}, use_global_device_ids=true | all-gather | bytes 40960 | tf_op jit(solution)/shard_map/all_gather | solution.py:529
  20.7 0.1 pad_dynamic-slice_fusion.reg_ref
  20.8 0.0 copy-done
  20.8 0.0 copy-done.1
  20.8 0.0 copy-done.2
  20.8 0.0 copy-done.3
  20.8 6.3 %coefficients.1 = (bf16[21,128,256]{2,1,0:T(8,128)(2,1)}, bf16[21,128,256]{2,1,0:T(8,128)(2,1)}) custom-call(f32[8,128]{1,0:T(8,128)S(1)} %pad_dynamic-slice_fusion.reg_ref, f32[4,8,8]{2,1,0:T(8,128)S(1)} %copy-done, f32[4,8]{1,0:T(4,128)S(1)} %copy-done.3, f32[8,8]{1,0:T(8,128)S(1)} %copy-done.1, f32[8,8]{1,0:T(8,128)S(1)} %copy-done.2), custom_call_target="tpu_custom_call" | custom-call | tf_op jit(solution)/shard_map/coefficients/pallas_call | solution.py:220
  27.2 48.0 %all-to-all-done.r_ref = f32[32,168,128]{2,1,0:T(8,128)S(1)} async-done(((f32[32,168,128]{2,1,0:T(8,128)}), f32[32,168,128]{2,1,0:T(8,128)S(1)}, u32[]{:S(2)}, u32[]{:S(2)}) %all-to-all-start) | async-done | bytes 2752544 | tf_op jit(solution)/shard_map/all_to_all | solution.py:502
  75.2 13.7 %filtered.1 = (bf16[2816,256]{1,0:T(8,128)(2,1)}, bf16[2816,256]{1,0:T(8,128)(2,1)}, f32[256,256]{1,0:T(8,128)}) custom-call(f32[32,168,128]{2,1,0:T(8,128)S(1)} %all-to-all-done.r_ref, bf16[21,128,256]{2,1,0:T(8,128)(2,1)} %get-tuple-element.11.ch_hbm.ch_ref, bf16[21,128,256]{2,1,0:T(8,128)(2,1)} %get-tuple-element.12.cl_hbm.cl_ref), custom_call_target="tpu_custom_call" | custom-call | tf_op jit(solution)/shard_map/filtered/pallas_call | solution.py:318
  88.9 4.6 %all-to-all-start.1 = ((f32[32,8,256]{2,1,0:T(8,128)}), f32[32,8,256]{2,1,0:T(8,128)S(1)}, u32[]{:S(2)}, u32[]{:S(2)}) async-start(f32[32,8,256]{2,1,0:T(8,128)} %bitcast.4), calls=%async_computation.1 | async-start | bytes 524288 | tf_op jit(solution)/shard_map/all_to_all | solution.py:502
  93.5 5.8 %moment.1 = f32[256,256]{1,0:T(8,128)S(1)} custom-call(bf16[2816,256]{1,0:T(8,128)(2,1)} %get-tuple-element.14.vh_ref.vh_hbm, bf16[2816,256]{1,0:T(8,128)(2,1)} %get-tuple-element.15.vl_ref.vl_hbm, bf16[21,128,256]{2,1,0:T(8,128)(2,1)} %get-tuple-element.11.ch_hbm.ch_ref, bf16[21,128,256]{2,1,0:T(8,128)(2,1)} %get-tuple-element.12.cl_hbm.cl_ref, ...), custom_call_target="tpu_custom_call" | custom-call | flops 4000000000 | bytes 10000000 | tf_op jit(solution)/shard_map/moment/pallas_call | solution.py:362
  99.3 4.6 %all-to-all-done.1 = f32[32,8,256]{2,1,0:T(8,128)S(1)} async-done(((f32[32,8,256]{2,1,0:T(8,128)}), f32[32,8,256]{2,1,0:T(8,128)S(1)}, u32[]{:S(2)}, u32[]{:S(2)}) %all-to-all-start.1) | async-done | bytes 262176 | tf_op jit(solution)/shard_map/all_to_all | solution.py:502
  104.0 17.8 %all_to_all.25.both_ref = f32[32,16,256]{2,1,0:T(8,128)S(1)} all-to-all(f32[32,16,256]{2,1,0:T(8,128)S(1)} %pad_maximum_fusion), channel_id=1, replica_groups=mesh['blk'=8,'slab'=4] {'blk','slab'}, dimensions={0} | all-to-all | bytes 1048576 | tf_op jit(solution)/shard_map/all_to_all | solution.py:502
  121.8 0.7 broadcast_in_dim.5
  122.6 3.1 %all-to-all-start.3 = ((f32[32,8,256]{2,1,0:T(8,128)}), f32[32,8,256]{2,1,0:T(8,128)S(1)}, u32[]{:S(2)}, u32[]{:S(2)}) async-start(f32[32,8,256]{2,1,0:T(8,128)} %broadcast_in_dim.5), calls=%async_computation.3 | async-start | bytes 524288 | tf_op jit(solution)/shard_map/all_to_all | solution.py:502
  125.6 13.7 %basis.1 = (f32[256,256]{1,0:T(8,128)S(1)}, f32[32,128,128]{2,1,0:T(8,128)}) custom-call(f32[32,16,256]{2,1,0:T(8,128)S(1)} %all_to_all.25.both_ref, bf16[2816,256]{1,0:T(8,128)(2,1)} %get-tuple-element.14.vh_ref.vh_hbm, bf16[2816,256]{1,0:T(8,128)(2,1)} %get-tuple-element.15.vl_ref.vl_hbm), custom_call_target="tpu_custom_call" | custom-call | flops 4000000000 | bytes 20000000 | tf_op jit(solution)/shard_map/basis/pallas_call | solution.py:472
  139.3 0.0 all-to-all-done.3
  139.3 5.8 %all-to-all-start.4 = ((f32[32,128,128]{2,1,0:T(8,128)}), f32[32,128,128]{2,1,0:T(8,128)S(1)}, u32[]{:S(2)}, u32[]{:S(2)}) async-start(f32[32,128,128]{2,1,0:T(8,128)} %get-tuple-element.17), calls=%async_computation.4 | async-start | bytes 4194304 | tf_op jit(solution)/shard_map/all_to_all | solution.py:502
  145.2 1.3 project.1
  146.5 47.4 %all-to-all-done.4 = f32[32,128,128]{2,1,0:T(8,128)S(1)} async-done(((f32[32,128,128]{2,1,0:T(8,128)}), f32[32,128,128]{2,1,0:T(8,128)S(1)}, u32[]{:S(2)}, u32[]{:S(2)}) %all-to-all-start.4) | async-done | bytes 2097184 | tf_op jit(solution)/shard_map/all_to_all | solution.py:502
  194.0 2.5 %unpack.1 = f32[32,128,128]{2,1,0:T(8,128)} custom-call(f32[4096,128]{1,0:T(8,128)S(1)} %bitcast.16), custom_call_target="tpu_custom_call" | custom-call | tf_op jit(solution)/shard_map/unpack/pallas_call | solution.py:129
  (6 shorter events, 0.2 us)
Async XLA Ops:
  4.7 7.4 %copy-start.4 = (s32[2,1024]{1,0:T(2,128)S(1)}, s32[2,1024]{1,0:T(2,128)}, u32[]{:S(2)}) copy-start(s32[2,1024]{1,0:T(2,128)} %param.7) | copy-start | bytes 24580
  4.7 16.1 %copy-start = (f32[4,8,8]{2,1,0:T(8,128)S(1)}, f32[4,8,8]{2,1,0:T(8,128)}, u32[]{:S(2)}) copy-start(f32[4,8,8]{2,1,0:T(8,128)} %onsite_ref.1) | copy-start | bytes 3076
  4.7 16.1 %copy-start.1 = (f32[8,8]{1,0:T(8,128)S(1)}, f32[8,8]{1,0:T(8,128)}, u32[]{:S(2)}) copy-start(f32[8,8]{1,0:T(8,128)} %kx_ref.1) | copy-start | bytes 772
  4.7 16.1 %copy-start.2 = (f32[8,8]{1,0:T(8,128)S(1)}, f32[8,8]{1,0:T(8,128)}, u32[]{:S(2)}) copy-start(f32[8,8]{1,0:T(8,128)} %ky_ref.1) | copy-start | bytes 772
  4.7 16.1 %copy-start.3 = (f32[4,8]{1,0:T(4,128)S(1)}, f32[4,8]{1,0:T(4,128)}, u32[]{:S(2)}) copy-start(f32[4,8]{1,0:T(4,128)} %hop_ref.1) | copy-start | bytes 388
  4.7 70.5 %all-to-all-start = ((f32[32,168,128]{2,1,0:T(8,128)}), f32[32,168,128]{2,1,0:T(8,128)S(1)}, u32[]{:S(2)}, u32[]{:S(2)}) async-start(f32[32,168,128]{2,1,0:T(8,128)} %pack.1), calls=%async_computation | async-start | bytes 5505024 | tf_op jit(solution)/shard_map/all_to_all | solution.py:502
  88.9 15.0 %all-to-all-start.1 = ((f32[32,8,256]{2,1,0:T(8,128)}), f32[32,8,256]{2,1,0:T(8,128)S(1)}, u32[]{:S(2)}, u32[]{:S(2)}) async-start(f32[32,8,256]{2,1,0:T(8,128)} %bitcast.4), calls=%async_computation.1 | async-start | bytes 524288 | tf_op jit(solution)/shard_map/all_to_all | solution.py:502
  122.6 16.8 %all-to-all-start.3 = ((f32[32,8,256]{2,1,0:T(8,128)}), f32[32,8,256]{2,1,0:T(8,128)S(1)}, u32[]{:S(2)}, u32[]{:S(2)}) async-start(f32[32,8,256]{2,1,0:T(8,128)} %broadcast_in_dim.5), calls=%async_computation.3 | async-start | bytes 524288 | tf_op jit(solution)/shard_map/all_to_all | solution.py:502
  139.3 54.6 %all-to-all-start.4 = ((f32[32,128,128]{2,1,0:T(8,128)}), f32[32,128,128]{2,1,0:T(8,128)S(1)}, u32[]{:S(2)}, u32[]{:S(2)}) async-start(f32[32,128,128]{2,1,0:T(8,128)} %get-tuple-element.17), calls=%async_computation.4 | async-start | bytes 4194304 | tf_op jit(solution)/shard_map/all_to_all | solution.py:502

commit v4 on v3

--- a/solution.py
+++ b/solution.py
@@ -20,8 +20,10 @@
 ON_CHIP = pl.BlockSpec(memory_space=pltpu.VMEM)
 OFF_CHIP = pl.BlockSpec(memory_space=pltpu.HBM)
 HIGHEST = lax.Precision.HIGHEST
-UNROLL = 7
-OWN = slice(2 * 128 + 64, 18 * 128 + 64)
+OWN = slice(0, 2048)
+OWN_PAIRS = 2, 18
+PAIR = 128
+EDGE = 64
 
 
 def off_chip(*arrays):
@@ -63,11 +65,8 @@
     ]
     for load in loads:
         load.start()
-    scr[0 : LEFT * 4, :] = jnp.zeros((LEFT * 4, LANES), jnp.float32)
-    tail = (LEFT + 1024) * 4
-    scr[tail:, :] = jnp.zeros((scr.shape[0] - tail, LANES), jnp.float32)
     sends = [
-        pltpu.make_async_copy(scr.at[pl.ds(128 * d, WINDOW * 4), :], o_ref.at[d], out_sem.at[d])
+        pltpu.make_async_copy(scr.at[pl.ds(128 * d, 128), :], o_ref.at[d], out_sem.at[d])
         for d in range(32)
     ]
     for part in range(2):
@@ -81,8 +80,8 @@
                     for low in range(4)
                 ]
                 turned = jnp.concatenate(parts, axis=0).T
-                scr[pl.ds((LEFT + 512 * part + 128 * tile) * 4 + r, 128, stride=4), :] = turned
-        for send in sends[15 * part : 15 + 17 * part]:
+                scr[pl.ds((512 * part + 128 * tile) * 4 + r, 128, stride=4), :] = turned
+        for send in sends[16 * part : 16 * part + 16]:
             send.start()
     for send in sends:
         send.wait()
@@ -92,12 +91,12 @@
     rows = x.reshape(32, 8, 2, 8, LANES).transpose(0, 1, 3, 2, 4).reshape(256, 16, LANES)
     return pl.pallas_call(
         pack_kernel,
-        out_shape=pltpu.HBM((32, WINDOW * 4, LANES), jnp.float32),
+        out_shape=pltpu.HBM((32, LANES, LANES), jnp.float32),
         in_specs=[OFF_CHIP],
         out_specs=OFF_CHIP,
         scratch_shapes=[
             pltpu.VMEM((2, 256, 8, LANES), jnp.float32),
-            pltpu.VMEM((4136, LANES), jnp.float32),
+            pltpu.VMEM((4096, LANES), jnp.float32),
             pltpu.SemaphoreType.DMA((2,)),
             pltpu.SemaphoreType.DMA((32,)),
         ],
@@ -234,99 +233,153 @@
     )
 
 
-def filter_kernel(
-    r_ref, ch_hbm, cl_hbm, vh_hbm, vl_hbm, g_ref, ch_ref, cl_ref, fa, fb, ah, al, bh, bl, sem
-):
+def ingest(ref, start, pair, field, high, low):
+    at = pair * PAIR
+    for half in range(2):
+        lanes = slice(half * LANES, half * LANES + LANES)
+        for slab in range(4):
+            pieces = exchange([ref[(half * 4 + j) * 4 + slab, pl.ds(start, 8), :] for j in range(4)], 32)
+            for mid in range(2):
+                for column, piece in enumerate(halves(pieces[2 * mid], pieces[2 * mid + 1])):
+                    field[pl.ds(at + (column * 64 + mid * 32 + slab * 8), 8), lanes] = piece[0]
+    rows = pl.ds(at + EDGE, PAIR)
+    high[rows, :], low[rows, :] = split(field[pl.ds(at, PAIR), :])
+
+
+def product(pair, ch_ref, cl_ref, high, low):
+    rows = pl.ds(pair * PAIR, 2 * PAIR)
+    vh, vl = high[rows, :], low[rows, :]
+    c_high, c_low = ch_ref[pair], cl_ref[pair]
+    return dot(
+        jnp.concatenate([c_high, c_high, c_low], axis=1), jnp.concatenate([vh, vl, vh], axis=0)
+    )
+
+
+def steps(ch_ref, cl_ref, fa, fb, ah, al, bh, bl):
+    def store(pair, value, field, high, low):
+        field[pl.ds(pair * PAIR, PAIR), :] = value
+        rows = pl.ds(pair * PAIR + EDGE, PAIR)
+        high[rows, :], low[rows, :] = split(value)
+
+    def first(pair):
+        store(pair, 0.5 * product(pair, ch_ref, cl_ref, ah, al), fb, bh, bl)
+
+    def later(old, high, low, source_high, source_low):
+        def step(pair):
+            rows = pl.ds(pair * PAIR, PAIR)
+            value = product(pair, ch_ref, cl_ref, source_high, source_low) - old[rows, :]
+            store(pair, value, old, high, low)
+
+        return step
+
+    even, odd = later(fa, ah, al, bh, bl), later(fb, bh, bl, ah, al)
+    return first, even, odd, even
+
+
+def interior_kernel(r_ref, ch_hbm, cl_hbm, fa, fb, ah, al, bh, bl, ch_ref, cl_ref, sem):
     loads = [
         pltpu.make_async_copy(ch_hbm, ch_ref, sem.at[0]),
         pltpu.make_async_copy(cl_hbm, cl_ref, sem.at[1]),
     ]
     for load in loads:
         load.start()
-    pairs = WINDOW // 2
-    block = 128
-    edge = 64
-    zero = jnp.zeros((edge, 256), jnp.bfloat16)
-    for ref in (ah, al, bh, bl):
-        ref[0:edge, :] = zero
-        ref[pairs * block + edge :, :] = zero
-    def ingest(pair, carry):
-        at = pl.multiple_of(pair * block, block)
-        source = pl.ds(pl.multiple_of(pair * 8, 8), 8)
-        for half in range(2):
-            lanes = slice(half * 128, half * 128 + 128)
-            for slab in range(4):
-                pieces = exchange([r_ref[(half * 4 + j) * 4 + slab, source, :] for j in range(4)], 32)
-                for mid in range(2):
-                    for column, piece in enumerate(halves(pieces[2 * mid], pieces[2 * mid + 1])):
-                        fa[pl.ds(at + (column * 64 + mid * 32 + slab * 8), 8), lanes] = piece[0]
-        rows = pl.ds(at + edge, block)
-        ah[rows, :], al[rows, :] = split(fa[pl.ds(at, block), :])
+
+    def take(pair, carry):
+        ingest(r_ref, pl.multiple_of((pair - OWN_PAIRS[0]) * 8, 8), pair, fa, ah, al)
         return carry
 
-    lax.fori_loop(0, pairs, ingest, 0, unroll=3)
+    lax.fori_loop(*OWN_PAIRS, take, 0, unroll=4)
     for load in loads:
         load.wait()
-
-    def product(pair, high, low):
-        rows = pl.ds(pair * block, 256)
-        vh, vl = high[rows, :], low[rows, :]
-        c_high, c_low = ch_ref[pair], cl_ref[pair]
-        return dot(
-            jnp.concatenate([c_high, c_high, c_low], axis=1), jnp.concatenate([vh, vl, vh], axis=0)
-        )
-
-    def store(pair, value, field, high, low):
-        field[pl.ds(pair * block, block), :] = value
-        rows = pl.ds(pair * block + edge, block)
-        high[rows, :], low[rows, :] = split(value)
-
-    def first(pair, carry):
-        store(pair, 0.5 * product(pair, ah, al), fb, bh, bl)
-        return carry
-
-    lax.fori_loop(0, pairs, first, 0, unroll=UNROLL)
-
-    def later(source_high, source_low, old, high, low):
-        def body(pair, carry):
-            rows = pl.ds(pair * block, block)
-            store(pair, product(pair, source_high, source_low) - old[rows, :], old, high, low)
+    for count, step in enumerate(steps(ch_ref, cl_ref, fa, fb, ah, al, bh, bl)):
+
+        def body(pair, carry, step=step):
+            step(pair)
             return carry
 
-        return body
-
-    lax.fori_loop(1, pairs - 1, later(bh, bl, fa, ah, al), 0, unroll=UNROLL)
-    lax.fori_loop(1, pairs - 1, later(ah, al, fb, bh, bl), 0, unroll=UNROLL)
-    lax.fori_loop(2, pairs - 2, later(bh, bl, fa, ah, al), 0, unroll=UNROLL)
-    stores = [
-        pltpu.make_async_copy(ah, vh_hbm, sem.at[2]),
-        pltpu.make_async_copy(al, vl_hbm, sem.at[3]),
-    ]
-    for store_out in stores:
-        store_out.start()
+        low, high = OWN_PAIRS[0] + 1 + count, OWN_PAIRS[1] - 1 - count
+        lax.fori_loop(low, high, body, 0, unroll=(high - low) // 2)
+
+
+def interior(received, coef_high, coef_low):
+    pairs = WINDOW // 2
+    field = pltpu.VMEM((pairs * PAIR, 256), jnp.float32)
+    half = pltpu.VMEM((pairs * PAIR + 2 * EDGE, 256), jnp.bfloat16)
+    bands = pltpu.VMEM((pairs, PAIR, 256), jnp.bfloat16)
+    return pl.pallas_call(
+        interior_kernel,
+        out_shape=(field,) * 2 + (half,) * 4 + (bands,) * 2,
+        in_specs=[ON_CHIP, OFF_CHIP, OFF_CHIP],
+        out_specs=(ON_CHIP,) * 8,
+        scratch_shapes=[pltpu.SemaphoreType.DMA((2,))],
+        compiler_params=VMEM,
+        cost_estimate=pl.CostEstimate(flops=int(8e9), transcendentals=0, bytes_accessed=int(2e7)),
+        name="interior",
+    )(received, *off_chip(coef_high, coef_low))
+
+
+def edges_kernel(left_ref, right_ref, *refs):
+    (ch_ref, cl_ref), (vh_hbm, vl_hbm, g_ref) = refs[6:8], refs[8:11]
+    fa, fb, ah, al, bh, bl = fields = refs[11:17]
+    sem = refs[17]
+    pairs = WINDOW // 2
+    first_row = OWN_PAIRS[0] * PAIR + EDGE
+
+    def results(low, high, index):
+        rows = pl.ds(low + EDGE, high - low)
+        target = pl.ds(low + EDGE - first_row, high - low)
+        return [
+            pltpu.make_async_copy(ah.at[rows, :], vh_hbm.at[target, :], sem.at[index]),
+            pltpu.make_async_copy(al.at[rows, :], vl_hbm.at[target, :], sem.at[index + 1]),
+        ]
+
+    inner = OWN_PAIRS[0] + 4, OWN_PAIRS[1] - 4
+    stores = results(inner[0] * PAIR, inner[1] * PAIR, 0)
+    for store in stores:
+        store.start()
+    zero = jnp.zeros((EDGE, 256), jnp.bfloat16)
+    for ref in (ah, al, bh, bl):
+        ref[0:EDGE, :] = zero
+        ref[pairs * PAIR + EDGE :, :] = zero
+    for pair in range(OWN_PAIRS[0]):
+        ingest(left_ref, pair * 8, pair, fa, ah, al)
+    for pair in range(OWN_PAIRS[1], pairs):
+        ingest(right_ref, (pair - OWN_PAIRS[1]) * 8, pair, fa, ah, al)
+    reach = ((0, pairs), (1, pairs - 1), (1, pairs - 1), (2, pairs - 2))
+    for count, step in enumerate(steps(ch_ref, cl_ref, *fields)):
+        low, high = OWN_PAIRS[0] + 1 + count, OWN_PAIRS[1] - 1 - count
+        for pair in list(range(reach[count][0], low)) + list(range(high, reach[count][1])):
+            step(pair)
+    last = OWN_PAIRS[1] * PAIR + EDGE
+    stores += results(OWN_PAIRS[0] * PAIR, inner[0] * PAIR, 2) + results(inner[1] * PAIR, last, 4)
+    for store in stores[2:]:
+        store.start()
+    own = slice(first_row, OWN_PAIRS[1] * PAIR + EDGE)
     dims = ((0,), (0,))
-    cross = dot(ah[OWN, :], al[OWN, :], dims)
-    g_ref[...] = dot(ah[OWN, :], ah[OWN, :], dims) + (cross + cross.T)
-    for store_out in stores:
-        store_out.wait()
+    cross = dot(ah[own, :], al[own, :], dims)
+    g_ref[...] = dot(ah[own, :], ah[own, :], dims) + (cross + cross.T)
+    for store in stores:
+        store.wait()
 
 
 def filtered_blocks(received, coef_high, coef_low):
-    rows = (WINDOW // 2) * 128
-    half = pltpu.HBM((rows + 128, 256), jnp.bfloat16)
-    square = jax.ShapeDtypeStruct((256, 256), jnp.float32)
+    count = lax.axis_size(ALL)
+    chain = [(i, i + 1) for i in range(count - 1)]
+    left = lax.ppermute(received[:, 128 - 4 * LEFT :], ALL, chain)
+    right = lax.ppermute(received[:, : 4 * (WINDOW - LEFT - 32)], ALL, [(j, i) for i, j in chain])
+    state = interior(received, coef_high, coef_low)
+    half = pltpu.HBM((2048 + EDGE, 256), jnp.bfloat16)
+    fields = [pltpu.VMEM(value.shape, value.dtype) for value in state[:6]]
     return pl.pallas_call(
-        filter_kernel,
-        out_shape=(half, half, square),
-        scratch_shapes=[pltpu.VMEM((WINDOW // 2, 128, 256), jnp.bfloat16)] * 2
-        + [pltpu.VMEM((rows, 256), jnp.float32)] * 2
-        + [pltpu.VMEM((rows + 128, 256), jnp.bfloat16)] * 4
-        + [pltpu.SemaphoreType.DMA((4,))],
-        in_specs=[ON_CHIP, OFF_CHIP, OFF_CHIP],
-        out_specs=(OFF_CHIP, OFF_CHIP, ON_CHIP),
+        edges_kernel,
+        out_shape=(half, half, pltpu.VMEM((256, 256), jnp.float32), *fields),
+        in_specs=[ON_CHIP] * 10,
+        out_specs=(OFF_CHIP,) * 2 + (ON_CHIP,) * 7,
+        input_output_aliases={i + 2: i + 3 for i in range(6)},
+        scratch_shapes=[pltpu.SemaphoreType.DMA((6,))],
         compiler_params=VMEM,
-        name="filtered",
-    )(received, *off_chip(coef_high, coef_low))
+        name="edges",
+    )(left, right, *state)[:3]
 
 
 def moment_kernel(vh_ref, vl_ref, ch_ref, cl_ref, g_ref, m_ref, bh, bl):
@@ -342,19 +395,18 @@
         bh[at, :], bl[at, :] = split(value)
 
     def body(pair, carry):
-        image(pair, pl.ds(pair * block, 256))
+        image(pair, pl.ds(pl.multiple_of((pair - 3) * block + edge, edge), 256))
         return carry
 
-    image(2, slice(2 * block + edge, 4 * block), edge)
+    image(2, slice(0, block + edge), edge)
     lax.fori_loop(3, 18, body, 0, unroll=3)
-    rows = slice(18 * block, 18 * block + edge)
+    rows = slice(16 * block - edge, 16 * block)
     c_high, c_low = ch_ref[18, 0:edge, 0:edge], cl_ref[18, 0:edge, 0:edge]
     value = dot(c_high, vh_ref[rows, :]) + (dot(c_high, vl_ref[rows, :]) + dot(c_low, vh_ref[rows, :]))
     bh[16 * block :, :], bl[16 * block :, :] = split(value)
     dims = ((0,), (0,))
-    top = slice(OWN.start, OWN.stop + edge)
-    high = vh_ref[top, :]
-    moment = dot(high, bh[...], dims) + (dot(high, bl[...], dims) + dot(vl_ref[top, :], bh[...], dims))
+    high = vh_ref[...]
+    moment = dot(high, bh[...], dims) + (dot(high, bl[...], dims) + dot(vl_ref[...], bh[...], dims))
     m_ref[...] = (0.5 * SCALE) * moment + SHIFT * g_ref[...]
 
 
@@ -369,18 +421,19 @@
     )(*off_chip(vh, vl, coef_high, coef_low), gram)
 
 
-def panel_inverse(block):
+def panel_solve(block, lines):
     row = lax.broadcasted_iota(jnp.int32, (8, LANES), 0)
-    lane = lax.broadcasted_iota(jnp.int32, (8, LANES), 1)
 
     def spread(tile, k):
-        return jnp.broadcast_to(tile[k % 8 : k % 8 + 1], (8, LANES))
+        return jnp.broadcast_to(tile[k % 8 : k % 8 + 1], tile.shape)
 
     cols = [
         [jnp.broadcast_to(block[8 * t : 8 * t + 8, j : j + 1], (8, LANES)) for t in range(4)]
         for j in range(32)
     ]
-    inverse = [(lane == row + 8 * t).astype(jnp.float32) for t in range(4)]
+    lines = [
+        [lines[8 * t : 8 * t + 8, LANES * h : LANES * h + LANES] for h in range(2)] for t in range(4)
+    ]
     pivots = [jnp.ones((8, LANES), jnp.float32) for t in range(4)]
     for k in range(32):
         own = k // 8
@@ -389,22 +442,24 @@
         scale = 1.0 / pivot
         ratio = {t: cols[k][t] * scale for t in range(own, 4)}
         ratio[own] = jnp.where(row > k % 8, ratio[own], 0.0)
-        line = spread(inverse[own], k)
+        line = [spread(part, k) for part in lines[own]]
         for j in range(k + 1, 32):
             weight = spread(ratio[j // 8], j)
             for t in range(j // 8, 4):
                 cols[j][t] = cols[j][t] - cols[k][t] * weight
         for t in range(own, 4):
-            inverse[t] = inverse[t] - ratio[t] * line
-    return jnp.concatenate([inverse[t] * lax.rsqrt(pivots[t]) for t in range(4)], axis=0)
+            lines[t] = [part - ratio[t] * above for part, above in zip(lines[t], line)]
+    roots = [lax.rsqrt(pivots[t]) for t in range(4)]
+    return jnp.concatenate(
+        [jnp.concatenate([part * roots[t] for part in lines[t]], axis=1) for t in range(4)], axis=0
+    )
 
 
 def half_inverse(aug):
     def panel(p, carry):
         rows = pl.ds(pl.multiple_of(32 * p, 32), 32)
         lines = aug[rows, :]
-        inverse = panel_inverse(pltpu.roll(lines[:, :LANES], LANES - 32 * p, 1))
-        lines = dot(inverse[:, :32], lines, precision=HIGHEST)
+        lines = panel_solve(pltpu.roll(lines[:, :LANES], LANES - 32 * p, 1), lines)
         aug[rows, :] = lines
         lane = lax.broadcasted_iota(jnp.int32, (32, LANES), 1)
         upper = jnp.where(lane >= 32 * (p + 1), lines[:, :LANES], 0.0)

time: 197 us -> 185 us (0.939)
  waiting for transfers between devices: 100 us -> 87.5 us
  starting transfers between devices: 20.8 us -> 26.1 us
  Pallas kernels: 47.4 us -> 43.9 us
    all_to_all x4, waiting for transfers between devices: 100 us -> 87.5 us  [swap(): return lax.all_to_all(parts, ALL, 0, 0, tiled=True)]
    ppermute x0 -> x2, starting transfers between devices: none -> 3.03 us  [the longest x1 1.56 us: filtered_blocks(): left = lax.ppermute(received[:, 128 - 4 * LEFT:], ALL, chain)]
    all_to_all x4, starting transfers between devices: 20.8 us -> 23 us  [swap(): return lax.all_to_all(parts, ALL, 0, 0, tiled=True)]
    pallas_call x2 -> x3, Pallas kernels: 17.8 us -> 16 us  [the longest x1 8.22 us: interior(): pl.pallas_call(interior_kernel, out_shape=(field,) * 2 + (half,) * 4 + (b...]
  transfers between devices with their start and end apart: 4 -> 6, of which waited for: 3 -> 3; matrix products, arithmetic and copies ran while one was open for 0% -> 0% of each run, Pallas kernels for 14% -> 18%
where the time goes in v4:
time: 185 us
  waiting for transfers between devices  87.5 us (47%)
  Pallas kernels  43.9 us (24%)
  starting transfers between devices  26.1 us (14%)
  blocking collectives  25 us (14%)
    all_to_all x4, waiting for transfers between devices, swap(): return lax.all_to_all(parts, ALL, 0, 0, tiled=True)  87.5 us
    all_to_all x4, starting transfers between devices, swap(): return lax.all_to_all(parts, ALL, 0, 0, tiled=True)  23 us
    all_to_all x1, blocking collectives, swap(): return lax.all_to_all(parts, ALL, 0, 0, tiled=True)  17.8 us
    pallas_call x1, Pallas kernels, basis(): pl.pallas_call(functools.partial(basis_kernel, entries), out_shape=(jax.S...  12.2 us
    pallas_call x1, Pallas kernels, interior(): pl.pallas_call(interior_kernel, out_shape=(field,) * 2 + (half,) * 4 + (b...  8.22 us
    all_gather x1, blocking collectives, fast(): lax.all_gather((region + 1).astype(jnp.float32), 'slab', axis=0, tiled=True)  7.22 us
    pallas_call x1, Pallas kernels, coefficients(): pl.pallas_call(coef_kernel, out_shape=(shape, shape), compiler_params=VME...  6.31 us
    pallas_call x1, Pallas kernels, moment_of(): pl.pallas_call(moment_kernel, out_shape=jax.ShapeDtypeStruct((256, 256),...  5.6 us
  transfers between devices with their start and end apart: 6, of which 3 were waited for; matrix products, arithmetic and copies ran while one was open for 0% of the time, Pallas kernels for 18%

profile of v4, /device:TPU:0, one launch (start us, length us, event | category | flops | bytes accessed | tf_op | source)
XLA Modules:
  0.0 184.5 jit_solution(17192758634365778320)
XLA Ops:
  0.6 3.9 %pack.1 = f32[32,128,128]{2,1,0:T(8,128)} custom-call(f32[256,16,128]{2,1,0:T(8,128)} %bitcast.19), custom_call_target="tpu_custom_call" | custom-call | tf_op jit(solution)/shard_map/pack/pallas_call | solution.py:92
  4.5 0.0 copy-start.4
  4.5 0.0 copy-start
  4.5 0.0 copy-start.1
  4.5 0.0 copy-start.2
  4.6 0.0 copy-start.3
  4.6 7.3 %all-to-all-start = ((f32[32,128,128]{2,1,0:T(8,128)}), f32[32,128,128]{2,1,0:T(8,128)S(1)}, u32[]{:S(2)}, u32[]{:S(2)}) async-start(f32[32,128,128]{2,1,0:T(8,128)} %pack.1), calls=%async_computation | async-start | bytes 4194304 | tf_op jit(solution)/shard_map/all_to_all | solution.py:557
  11.9 0.0 copy-done.4
  11.9 7.2 %all-gather = f32[4,2,1024]{2,1,0:T(2,128)S(1)} all-gather(f32[1,2,1024]{2,1,0:T(2,128)S(1)} %convert_bitcast_fusion), channel_id=1, replica_groups=mesh['blk'=8,'slab'=4] {'slab'}, dimensions={0}, use_global_device_ids=true | all-gather | bytes 40960 | tf_op jit(solution)/shard_map/all_gather | solution.py:584
  19.2 0.1 pad_dynamic-slice_fusion.reg_ref
  19.2 0.0 copy-done
  19.2 0.0 copy-done.1
  19.3 6.3 %coefficients.1 = (bf16[21,128,256]{2,1,0:T(8,128)(2,1)}, bf16[21,128,256]{2,1,0:T(8,128)(2,1)}) custom-call(f32[8,128]{1,0:T(8,128)S(1)} %pad_dynamic-slice_fusion.reg_ref, f32[4,8,8]{2,1,0:T(8,128)S(1)} %copy-done, f32[4,8]{1,0:T(4,128)S(1)} %copy-done.3, f32[8,8]{1,0:T(8,128)S(1)} %copy-done.1, f32[8,8]{1,0:T(8,128)S(1)} %copy-done.2), custom_call_target="tpu_custom_call" | custom-call | tf_op jit(solution)/shard_map/coefficients/pallas_call | solution.py:219
  25.6 35.1 %all-to-all-done.r_ref = f32[32,128,128]{2,1,0:T(8,128)S(1)} async-done(((f32[32,128,128]{2,1,0:T(8,128)}), f32[32,128,128]{2,1,0:T(8,128)S(1)}, u32[]{:S(2)}, u32[]{:S(2)}) %all-to-all-start) | async-done | bytes 2097184 | tf_op jit(solution)/shard_map/all_to_all | solution.py:557
  60.7 1.6 collective-permute-start
  62.3 1.5 collective-permute-start.1
  63.8 8.2 %interior.1 = (f32[2688,256]{1,0:T(8,128)S(1)}, f32[2688,256]{1,0:T(8,128)S(1)}, bf16[2816,256]{1,0:T(8,128)(2,1)S(1)}, bf16[2816,256]{1,0:T(8,128)(2,1)S(1)}, b...) custom-call(f32[32,128,128]{2,1,0:T(8,128)S(1)} %all-to-all-done.r_r, ...), custom_call_target="tpu_custom_call" | custom-call | flops 8000000000 | bytes 20000000 | tf_op jit(solution)/shard_map/interior/pallas_call | solution.py:309
  72.0 0.0 collective-permute-done.left_ref
  72.0 0.0 collective-permute-done.1.right_ref
  72.0 3.9 %edges.1 = (bf16[2112,256]{1,0:T(8,128)(2,1)}, bf16[2112,256]{1,0:T(8,128)(2,1)}, f32[256,256]{1,0:T(8,128)}, f32[2688,256]{1,0:T(8,128)S(1)}, f32[2688,256]{1,0...) custom-call(f32[32,16,128]{2,1,0:T(8,128)S(1)} %collective-permute-d, ...), custom_call_target="tpu_custom_call", output_to_operand_aliasing={{3}: (2, {}), {4}: (3, {}), {5}: (4, {}), {6}: (5, {}), {7}... | custom-call | tf_op jit(solution)/shard_map/edges/pallas_call | solution.py:373
  75.9 6.8 %all-to-all-start.1 = ((f32[32,8,256]{2,1,0:T(8,128)}), f32[32,8,256]{2,1,0:T(8,128)S(1)}, u32[]{:S(2)}, u32[]{:S(2)}) async-start(f32[32,8,256]{2,1,0:T(8,128)} %bitcast.4), calls=%async_computation.1 | async-start | bytes 524288 | tf_op jit(solution)/shard_map/all_to_all | solution.py:557
  82.8 5.6 %moment.1 = f32[256,256]{1,0:T(8,128)S(1)} custom-call(bf16[2112,256]{1,0:T(8,128)(2,1)} %get-tuple-element.30.vh_ref.vh_hbm, bf16[2112,256]{1,0:T(8,128)(2,1)} %get-tuple-element.31.vl_ref.vl_hbm, bf16[21,128,256]{2,1,0:T(8,128)(2,1)} %get-tuple-element.19.ch_hbm.ch_ref, bf16[21,128,256]{2,1,0:T(8,128)(2,1)} %get-tuple-element.20.cl_hbm.cl_ref, ...), custom_call_target="tpu_custom_call" | custom-call | flops 4000000000 | bytes 10000000 | tf_op jit(solution)/shard_map/moment/pallas_call | solution.py:414
  88.4 5.0 %all-to-all-done.1 = f32[32,8,256]{2,1,0:T(8,128)S(1)} async-done(((f32[32,8,256]{2,1,0:T(8,128)}), f32[32,8,256]{2,1,0:T(8,128)S(1)}, u32[]{:S(2)}, u32[]{:S(2)}) %all-to-all-start.1) | async-done | bytes 262176 | tf_op jit(solution)/shard_map/all_to_all | solution.py:557
  93.5 17.8 %all_to_all.25.both_ref = f32[32,16,256]{2,1,0:T(8,128)S(1)} all-to-all(f32[32,16,256]{2,1,0:T(8,128)S(1)} %pad_maximum_fusion), channel_id=1, replica_groups=mesh['blk'=8,'slab'=4] {'blk','slab'}, dimensions={0} | all-to-all | bytes 1048576 | tf_op jit(solution)/shard_map/all_to_all | solution.py:557
  111.3 0.7 broadcast_in_dim.5
  112.0 3.1 %all-to-all-start.3 = ((f32[32,8,256]{2,1,0:T(8,128)}), f32[32,8,256]{2,1,0:T(8,128)S(1)}, u32[]{:S(2)}, u32[]{:S(2)}) async-start(f32[32,8,256]{2,1,0:T(8,128)} %broadcast_in_dim.5), calls=%async_computation.3 | async-start | bytes 524288 | tf_op jit(solution)/shard_map/all_to_all | solution.py:557
  115.1 12.2 %basis.1 = (f32[256,256]{1,0:T(8,128)S(1)}, f32[32,128,128]{2,1,0:T(8,128)}) custom-call(f32[32,16,256]{2,1,0:T(8,128)S(1)} %all_to_all.25.both_ref, bf16[2112,256]{1,0:T(8,128)(2,1)} %get-tuple-element.30.vh_ref.vh_hbm, bf16[2112,256]{1,0:T(8,128)(2,1)} %get-tuple-element.31.vl_ref.vl_hbm), custom_call_target="tpu_custom_call" | custom-call | flops 4000000000 | bytes 20000000 | tf_op jit(solution)/shard_map/basis/pallas_call | solution.py:527
  127.2 0.0 all-to-all-done.3
  127.2 5.8 %all-to-all-start.4 = ((f32[32,128,128]{2,1,0:T(8,128)}), f32[32,128,128]{2,1,0:T(8,128)S(1)}, u32[]{:S(2)}, u32[]{:S(2)}) async-start(f32[32,128,128]{2,1,0:T(8,128)} %get-tuple-element.33), calls=%async_computation.4 | async-start | bytes 4194304 | tf_op jit(solution)/shard_map/all_to_all | solution.py:557
  133.1 1.3 project.1
  134.4 47.4 %all-to-all-done.4 = f32[32,128,128]{2,1,0:T(8,128)S(1)} async-done(((f32[32,128,128]{2,1,0:T(8,128)}), f32[32,128,128]{2,1,0:T(8,128)S(1)}, u32[]{:S(2)}, u32[]{:S(2)}) %all-to-all-start.4) | async-done | bytes 2097184 | tf_op jit(solution)/shard_map/all_to_all | solution.py:557
  181.8 2.5 %unpack.1 = f32[32,128,128]{2,1,0:T(8,128)} custom-call(f32[4096,128]{1,0:T(8,128)S(1)} %bitcast.16), custom_call_target="tpu_custom_call" | custom-call | tf_op jit(solution)/shard_map/unpack/pallas_call | solution.py:128
  (10 shorter events, 0.2 us)
Async XLA Ops:
  4.5 7.4 %copy-start.4 = (s32[2,1024]{1,0:T(2,128)S(1)}, s32[2,1024]{1,0:T(2,128)}, u32[]{:S(2)}) copy-start(s32[2,1024]{1,0:T(2,128)} %param.7) | copy-start | bytes 24580
  4.5 14.7 %copy-start = (f32[4,8,8]{2,1,0:T(8,128)S(1)}, f32[4,8,8]{2,1,0:T(8,128)}, u32[]{:S(2)}) copy-start(f32[4,8,8]{2,1,0:T(8,128)} %onsite_ref.1) | copy-start | bytes 3076
  4.5 14.7 %copy-start.1 = (f32[8,8]{1,0:T(8,128)S(1)}, f32[8,8]{1,0:T(8,128)}, u32[]{:S(2)}) copy-start(f32[8,8]{1,0:T(8,128)} %kx_ref.1) | copy-start | bytes 772
  4.5 14.7 %copy-start.2 = (f32[8,8]{1,0:T(8,128)S(1)}, f32[8,8]{1,0:T(8,128)}, u32[]{:S(2)}) copy-start(f32[8,8]{1,0:T(8,128)} %ky_ref.1) | copy-start | bytes 772
  4.6 14.7 %copy-start.3 = (f32[4,8]{1,0:T(4,128)S(1)}, f32[4,8]{1,0:T(4,128)}, u32[]{:S(2)}) copy-start(f32[4,8]{1,0:T(4,128)} %hop_ref.1) | copy-start | bytes 388
  4.6 56.1 %all-to-all-start = ((f32[32,128,128]{2,1,0:T(8,128)}), f32[32,128,128]{2,1,0:T(8,128)S(1)}, u32[]{:S(2)}, u32[]{:S(2)}) async-start(f32[32,128,128]{2,1,0:T(8,128)} %pack.1), calls=%async_computation | async-start | bytes 4194304 | tf_op jit(solution)/shard_map/all_to_all | solution.py:557
  60.7 11.3 %collective-permute-start = (f32[32,16,128]{2,1,0:T(8,128)S(1)}, f32[32,16,128]{2,1,0:T(8,128)S(1)}, u32[]{:S(2)}, u32[]{:S(2)}) collective-permute-start(f32[32,16,128]{2,1,0:T(8,128)S(1)} %slice.12), channel_id=1, source_target_pairs={{0,1},{1,2},{2,3},{3,4},{4,5},{5,6},{6,7},{7,8},{8,9},{9,10},{10,1... | collective-permute-start | bytes 786440 | tf_op jit(solution)/shard_map/ppermute | solution.py:368
  62.3 9.7 %collective-permute-start.1 = (f32[32,24,128]{2,1,0:T(8,128)S(1)}, f32[32,24,128]{2,1,0:T(8,128)S(1)}, u32[]{:S(2)}, u32[]{:S(2)}) collective-permute-start(f32[32,24,128]{2,1,0:T(8,128)S(1)} %slice.13), channel_id=1, source_target_pairs={{1,0},{2,1},{3,2},{4,3},{5,4},{6,5},{7,6},{8,7},{9,8},{10,9},{11,1... | collective-permute-start | bytes 1179656 | tf_op jit(solution)/shard_map/ppermute | solution.py:369
  75.9 17.4 %all-to-all-start.1 = ((f32[32,8,256]{2,1,0:T(8,128)}), f32[32,8,256]{2,1,0:T(8,128)S(1)}, u32[]{:S(2)}, u32[]{:S(2)}) async-start(f32[32,8,256]{2,1,0:T(8,128)} %bitcast.4), calls=%async_computation.1 | async-start | bytes 524288 | tf_op jit(solution)/shard_map/all_to_all | solution.py:557
  112.0 15.2 %all-to-all-start.3 = ((f32[32,8,256]{2,1,0:T(8,128)}), f32[32,8,256]{2,1,0:T(8,128)S(1)}, u32[]{:S(2)}, u32[]{:S(2)}) async-start(f32[32,8,256]{2,1,0:T(8,128)} %broadcast_in_dim.5), calls=%async_computation.3 | async-start | bytes 524288 | tf_op jit(solution)/shard_map/all_to_all | solution.py:557
  127.2 54.6 %all-to-all-start.4 = ((f32[32,128,128]{2,1,0:T(8,128)}), f32[32,128,128]{2,1,0:T(8,128)S(1)}, u32[]{:S(2)}, u32[]{:S(2)}) async-start(f32[32,128,128]{2,1,0:T(8,128)} %get-tuple-element.33), calls=%async_computation.4 | async-start | bytes 4194304 | tf_op jit(solution)/shard_map/all_to_all | solution.py:557

commit v5 on v4

--- a/solution.py
+++ b/solution.py
@@ -233,6 +233,12 @@
     )
 
 
+def lower_blocks(square):
+    return jnp.concatenate(
+        [square[:LANES, :LANES], square[LANES:, :LANES], square[LANES:, LANES:]], axis=0
+    )
+
+
 def ingest(ref, start, pair, field, high, low):
     at = pair * PAIR
     for half in range(2):
@@ -357,7 +363,7 @@
     own = slice(first_row, OWN_PAIRS[1] * PAIR + EDGE)
     dims = ((0,), (0,))
     cross = dot(ah[own, :], al[own, :], dims)
-    g_ref[...] = dot(ah[own, :], ah[own, :], dims) + (cross + cross.T)
+    g_ref[...] = lower_blocks(dot(ah[own, :], ah[own, :], dims) + (cross + cross.T))
     for store in stores:
         store.wait()
 
@@ -372,7 +378,7 @@
     fields = [pltpu.VMEM(value.shape, value.dtype) for value in state[:6]]
     return pl.pallas_call(
         edges_kernel,
-        out_shape=(half, half, pltpu.VMEM((256, 256), jnp.float32), *fields),
+        out_shape=(half, half, pltpu.VMEM((3 * LANES, LANES), jnp.float32), *fields),
         in_specs=[ON_CHIP] * 10,
         out_specs=(OFF_CHIP,) * 2 + (ON_CHIP,) * 7,
         input_output_aliases={i + 2: i + 3 for i in range(6)},
@@ -407,13 +413,13 @@
     dims = ((0,), (0,))
     high = vh_ref[...]
     moment = dot(high, bh[...], dims) + (dot(high, bl[...], dims) + dot(vl_ref[...], bh[...], dims))
-    m_ref[...] = (0.5 * SCALE) * moment + SHIFT * g_ref[...]
+    m_ref[...] = (0.5 * SCALE) * lower_blocks(moment) + SHIFT * g_ref[...]
 
 
 def moment_of(vh, vl, coef_high, coef_low, gram):
     return pl.pallas_call(
         moment_kernel,
-        out_shape=jax.ShapeDtypeStruct((256, 256), jnp.float32),
+        out_shape=jax.ShapeDtypeStruct((3 * LANES, LANES), jnp.float32),
         scratch_shapes=[pltpu.VMEM((16 * 128 + 64, 256), jnp.bfloat16)] * 2,
         compiler_params=VMEM,
         cost_estimate=pl.CostEstimate(flops=int(4e9), transcendentals=0, bytes_accessed=int(1e7)),
@@ -478,13 +484,14 @@
         load.start()
     row = lax.broadcasted_iota(jnp.int32, (LANES, LANES), 0)
     eye = (row == lax.broadcasted_iota(jnp.int32, (LANES, LANES), 1)).astype(jnp.float32)
-    gram[...] = both_ref[:, 0:8, :].reshape(256, 256) * (1.0 / entries)
-    aug[:, :LANES] = gram[:LANES, :LANES]
+    for d in range(32):
+        gram[12 * d : 12 * d + 12, :] = both_ref[24 * d : 24 * d + 12, :] * (1.0 / entries)
+    aug[:, :LANES] = gram[:LANES, :]
     aug[:, LANES:] = eye
     half_inverse(aug)
     first = aug[:, LANES:]
-    upper = dot(first, gram[:LANES, LANES:], precision=HIGHEST)
-    aug[:, :LANES] = gram[LANES:, LANES:] - dot(upper, upper, ((0,), (0,)), HIGHEST)
+    upper = dot(first, gram[LANES : 2 * LANES, :], ((1,), (1,)), HIGHEST)
+    aug[:, :LANES] = gram[2 * LANES :, :] - dot(upper, upper, ((0,), (0,)), HIGHEST)
     aug[:, LANES:] = eye
     corner = dot(upper, first, ((0,), (0,)), HIGHEST)
     half_inverse(aug)
@@ -533,7 +540,7 @@
         in_specs=[ON_CHIP, OFF_CHIP, OFF_CHIP],
         out_specs=(ON_CHIP, OFF_CHIP),
         scratch_shapes=[
-            pltpu.VMEM((256, 256), jnp.float32),
+            pltpu.VMEM((3 * LANES, LANES), jnp.float32),
             pltpu.VMEM((LANES, 256), jnp.float32),
             pltpu.VMEM((2048, 256), jnp.bfloat16),
             pltpu.VMEM((2048, 256), jnp.bfloat16),
@@ -545,16 +552,16 @@
         compiler_params=VMEM,
         cost_estimate=pl.CostEstimate(flops=int(4e9), transcendentals=0, bytes_accessed=int(2e7)),
         name="basis",
-    )(both, *off_chip(vh, vl))
-
-
-def parts_of(square):
-    count = lax.axis_size(ALL)
-    return square.reshape(count, -1, square.shape[1])
+    )(both.reshape(768, LANES), *off_chip(vh, vl))
+
+
+def parts_of(blocks):
+    return blocks.reshape(lax.axis_size(ALL), -1, 4, LANES)
 
 
 def swap(parts):
-    return lax.all_to_all(parts, ALL, 0, 0, tiled=True)
+    rows = parts.reshape((-1,) + parts.shape[-2:])
+    return lax.all_to_all(rows, ALL, 0, 0, tiled=True).reshape(parts.shape)
 
 
 def for_all(share):
@@ -563,7 +570,16 @@
 
 def project_kernel(entries, moment_ref, w_ref, p_ref):
     first = pl.multiple_of(32 * lax.axis_index("blk"), 32)
-    half_done = dot(w_ref[pl.ds(first, 32), :], moment_ref[...], precision=HIGHEST) * (1.0 / entries)
+    mine = w_ref[pl.ds(first, 32), :]
+    left, right = mine[:, :LANES], mine[:, LANES:]
+    above, below, last = (moment_ref[LANES * k : LANES * k + LANES, :] for k in range(3))
+    half_done = jnp.concatenate(
+        [
+            dot(left, above, precision=HIGHEST) + dot(right, below, precision=HIGHEST),
+            dot(left, below, ((1,), (1,)), HIGHEST) + dot(right, last, precision=HIGHEST),
+        ],
+        axis=1,
+    ) * (1.0 / entries)
     p_ref[...] = dot(half_done, w_ref[...], ((1,), (1,)), HIGHEST)
 
 
@@ -591,7 +607,7 @@
     share = swap(parts_of(own_gram)).sum(0)
     both = swap(jnp.concatenate([for_all(share), parts_of(own_moment)], axis=1))
     inverse, blocks = basis(both, entries, vh, vl)
-    moment = swap(for_all(both[:, 8:].sum(0))).reshape(256, 256)
+    moment = swap(for_all(both[:, 3:].sum(0))).reshape(3 * LANES, LANES)
     blocks, moment = lax.optimization_barrier((blocks, moment))
     states_out = unpack(swap(blocks))
     projected = project(moment, inverse, entries)

time: 185 us -> 181 us (0.978)
  blocking collectives: 25 us -> 22.9 us
    all_to_all x1, blocking collectives: 17.8 us -> 15.7 us  [swap(): return lax.all_to_all(rows, ALL, 0, 0, tiled=True).reshape(parts.shape)]
  transfers between devices with their start and end apart: 6 -> 6, of which waited for: 3 -> 3; matrix products, arithmetic and copies ran while one was open for 0% -> 0% of each run, Pallas kernels for 18% -> 19%
where the time goes in v5:
time: 181 us
  waiting for transfers between devices  85.8 us (47%)
  Pallas kernels  44.2 us (24%)
  starting transfers between devices  25.6 us (14%)
  blocking collectives  22.9 us (13%)
    all_to_all x4, waiting for transfers between devices, swap(): return lax.all_to_all(rows, ALL, 0, 0, tiled=True).reshape(parts.shape)  85.8 us
    all_to_all x4, starting transfers between devices, swap(): return lax.all_to_all(rows, ALL, 0, 0, tiled=True).reshape(parts.shape)  22.6 us
    all_to_all x1, blocking collectives, swap(): return lax.all_to_all(rows, ALL, 0, 0, tiled=True).reshape(parts.shape)  15.7 us
    pallas_call x1, Pallas kernels, basis(): pl.pallas_call(functools.partial(basis_kernel, entries), out_shape=(jax.S...  12.4 us
    pallas_call x1, Pallas kernels, interior(): pl.pallas_call(interior_kernel, out_shape=(field,) * 2 + (half,) * 4 + (b...  8.22 us
    all_gather x1, blocking collectives, fast(): lax.all_gather((region + 1).astype(jnp.float32), 'slab', axis=0, tiled=True)  7.22 us
    pallas_call x1, Pallas kernels, coefficients(): pl.pallas_call(coef_kernel, out_shape=(shape, shape), compiler_params=VME...  6.31 us
    pallas_call x1, Pallas kernels, moment_of(): pl.pallas_call(moment_kernel, out_shape=jax.ShapeDtypeStruct((3 * LANES,...  5.58 us
  transfers between devices with their start and end apart: 6, of which 3 were waited for; matrix products, arithmetic and copies ran while one was open for 0% of the time, Pallas kernels for 19%

profile of v5, /device:TPU:0, one launch (start us, length us, event | category | flops | bytes accessed | tf_op | source)
XLA Modules:
  0.0 180.6 jit_solution(2336315567518542058)
XLA Ops:
  0.6 3.9 %pack.1 = f32[32,128,128]{2,1,0:T(8,128)} custom-call(f32[256,16,128]{2,1,0:T(8,128)} %bitcast.26), custom_call_target="tpu_custom_call" | custom-call | tf_op jit(solution)/shard_map/pack/pallas_call | solution.py:92
  4.5 0.0 copy-start.4
  4.5 0.0 copy-start
  4.5 0.0 copy-start.1
  4.5 0.0 copy-start.2
  4.6 0.0 copy-start.3
  4.6 7.3 %all-to-all-start = ((f32[32,128,128]{2,1,0:T(8,128)}), f32[32,128,128]{2,1,0:T(8,128)S(1)}, u32[]{:S(2)}, u32[]{:S(2)}) async-start(f32[32,128,128]{2,1,0:T(8,128)} %pack.1), calls=%async_computation | async-start | bytes 4194304 | tf_op jit(solution)/shard_map/all_to_all | solution.py:564
  11.9 0.0 copy-done.4
  11.9 7.2 %all-gather = f32[4,2,1024]{2,1,0:T(2,128)S(1)} all-gather(f32[1,2,1024]{2,1,0:T(2,128)S(1)} %convert_bitcast_fusion), channel_id=1, replica_groups=mesh['blk'=8,'slab'=4] {'slab'}, dimensions={0}, use_global_device_ids=true | all-gather | bytes 40960 | tf_op jit(solution)/shard_map/all_gather | solution.py:600
  19.2 0.1 pad_dynamic-slice_fusion.reg_ref
  19.3 6.3 %coefficients.1 = (bf16[21,128,256]{2,1,0:T(8,128)(2,1)}, bf16[21,128,256]{2,1,0:T(8,128)(2,1)}) custom-call(f32[8,128]{1,0:T(8,128)S(1)} %pad_dynamic-slice_fusion.reg_ref, f32[4,8,8]{2,1,0:T(8,128)S(1)} %copy-done, f32[4,8]{1,0:T(4,128)S(1)} %copy-done.3, f32[8,8]{1,0:T(8,128)S(1)} %copy-done.1, f32[8,8]{1,0:T(8,128)S(1)} %copy-done.2), custom_call_target="tpu_custom_call" | custom-call | tf_op jit(solution)/shard_map/coefficients/pallas_call | solution.py:219
  25.6 35.1 %all-to-all-done.r_ref = f32[32,128,128]{2,1,0:T(8,128)S(1)} async-done(((f32[32,128,128]{2,1,0:T(8,128)}), f32[32,128,128]{2,1,0:T(8,128)S(1)}, u32[]{:S(2)}, u32[]{:S(2)}) %all-to-all-start) | async-done | bytes 2097184 | tf_op jit(solution)/shard_map/all_to_all | solution.py:564
  60.7 1.6 collective-permute-start
  62.3 1.5 collective-permute-start.1
  63.8 8.2 %interior.1 = (f32[2688,256]{1,0:T(8,128)S(1)}, f32[2688,256]{1,0:T(8,128)S(1)}, bf16[2816,256]{1,0:T(8,128)(2,1)S(1)}, bf16[2816,256]{1,0:T(8,128)(2,1)S(1)}, b...) custom-call(f32[32,128,128]{2,1,0:T(8,128)S(1)} %all-to-all-done.r_r, ...), custom_call_target="tpu_custom_call" | custom-call | flops 8000000000 | bytes 20000000 | tf_op jit(solution)/shard_map/interior/pallas_call | solution.py:315
  72.0 0.0 collective-permute-done.left_ref
  72.0 0.0 collective-permute-done.1.right_ref
  72.0 3.9 %edges.1 = (bf16[2112,256]{1,0:T(8,128)(2,1)}, bf16[2112,256]{1,0:T(8,128)(2,1)}, f32[384,128]{1,0:T(8,128)}, f32[2688,256]{1,0:T(8,128)S(1)}, f32[2688,256]{1,0...) custom-call(f32[32,16,128]{2,1,0:T(8,128)S(1)} %collective-permute-d, ...), custom_call_target="tpu_custom_call", output_to_operand_aliasing={{3}: (2, {}), {4}: (3, {}), {5}: (4, {}), {6}: (5, {}), {7}... | custom-call | tf_op jit(solution)/shard_map/edges/pallas_call | solution.py:379
  75.9 6.8 %all-to-all-start.1 = ((f32[96,4,128]{2,1,0:T(4,128)}), f32[96,4,128]{2,1,0:T(4,128)S(1)}, u32[]{:S(2)}, u32[]{:S(2)}) async-start(f32[96,4,128]{2,1,0:T(4,128)} %bitcast.4), calls=%async_computation.1 | async-start | bytes 393216 | tf_op jit(solution)/shard_map/all_to_all | solution.py:564
  82.8 5.6 %moment.1 = f32[384,128]{1,0:T(8,128)S(1)} custom-call(bf16[2112,256]{1,0:T(8,128)(2,1)} %get-tuple-element.30.vh_ref.vh_hbm, bf16[2112,256]{1,0:T(8,128)(2,1)} %get-tuple-element.31.vl_ref.vl_hbm, bf16[21,128,256]{2,1,0:T(8,128)(2,1)} %get-tuple-element.19.ch_hbm.ch_ref, bf16[21,128,256]{2,1,0:T(8,128)(2,1)} %get-tuple-element.20.cl_hbm.cl_ref, ...), custom_call_target="tpu_custom_call" | custom-call | flops 4000000000 | bytes 10000000 | tf_op jit(solution)/shard_map/moment/pallas_call | solution.py:420
  88.4 3.3 %all-to-all-done.1 = f32[96,4,128]{2,1,0:T(4,128)S(1)} async-done(((f32[96,4,128]{2,1,0:T(4,128)}), f32[96,4,128]{2,1,0:T(4,128)S(1)}, u32[]{:S(2)}, u32[]{:S(2)}) %all-to-all-start.1) | async-done | bytes 196640 | tf_op jit(solution)/shard_map/all_to_all | solution.py:564
  91.7 0.1 reduce_sum.18
  91.8 0.1 pad_maximum_fusion
  91.9 15.7 %all_to_all.25 = f32[192,4,128]{2,1,0:T(4,128)S(1)} all-to-all(f32[192,4,128]{2,1,0:T(4,128)S(1)} %bitcast.28), channel_id=1, replica_groups=mesh['blk'=8,'slab'=4] {'blk','slab'}, dimensions={0} | all-to-all | bytes 786432 | tf_op jit(solution)/shard_map/all_to_all | solution.py:564
  107.6 0.7 broadcast_in_dim.5
  108.3 2.6 %all-to-all-start.3 = ((f32[96,4,128]{2,1,0:T(4,128)}), f32[96,4,128]{2,1,0:T(4,128)S(1)}, u32[]{:S(2)}, u32[]{:S(2)}) async-start(f32[96,4,128]{2,1,0:T(4,128)} %bitcast.10), calls=%async_computation.3 | async-start | bytes 393216 | tf_op jit(solution)/shard_map/all_to_all | solution.py:564
  110.9 12.4 %basis.1 = (f32[256,256]{1,0:T(8,128)S(1)}, f32[32,128,128]{2,1,0:T(8,128)}) custom-call(f32[768,128]{1,0:T(8,128)S(1)} %bitcast.23, bf16[2112,256]{1,0:T(8,128)(2,1)} %get-tuple-element.30.vh_ref.vh_hbm, bf16[2112,256]{1,0:T(8,128)(2,1)} %get-tuple-element.31.vl_ref.vl_hbm), custom_call_target="tpu_custom_call" | custom-call | flops 4000000000 | bytes 20000000 | tf_op jit(solution)/shard_map/basis/pallas_call | solution.py:534
  123.3 0.0 all-to-all-done.3
  123.3 5.8 %all-to-all-start.4 = ((f32[32,128,128]{2,1,0:T(8,128)}), f32[32,128,128]{2,1,0:T(8,128)S(1)}, u32[]{:S(2)}, u32[]{:S(2)}) async-start(f32[32,128,128]{2,1,0:T(8,128)} %get-tuple-element.33), calls=%async_computation.4 | async-start | bytes 4194304 | tf_op jit(solution)/shard_map/all_to_all | solution.py:564
  129.2 1.4 project.1
  130.6 47.4 %all-to-all-done.4 = f32[32,128,128]{2,1,0:T(8,128)S(1)} async-done(((f32[32,128,128]{2,1,0:T(8,128)}), f32[32,128,128]{2,1,0:T(8,128)S(1)}, u32[]{:S(2)}, u32[]{:S(2)}) %all-to-all-start.4) | async-done | bytes 2097184 | tf_op jit(solution)/shard_map/all_to_all | solution.py:564
  177.9 2.5 %unpack.1 = f32[32,128,128]{2,1,0:T(8,128)} custom-call(f32[4096,128]{1,0:T(8,128)S(1)} %bitcast.21), custom_call_target="tpu_custom_call" | custom-call | tf_op jit(solution)/shard_map/unpack/pallas_call | solution.py:128
  (10 shorter events, 0.2 us)
Async XLA Ops:
  4.5 7.4 %copy-start.4 = (s32[2,1024]{1,0:T(2,128)S(1)}, s32[2,1024]{1,0:T(2,128)}, u32[]{:S(2)}) copy-start(s32[2,1024]{1,0:T(2,128)} %param.7) | copy-start | bytes 24580
  4.5 14.7 %copy-start = (f32[4,8,8]{2,1,0:T(8,128)S(1)}, f32[4,8,8]{2,1,0:T(8,128)}, u32[]{:S(2)}) copy-start(f32[4,8,8]{2,1,0:T(8,128)} %onsite_ref.1) | copy-start | bytes 3076
  4.5 14.7 %copy-start.1 = (f32[8,8]{1,0:T(8,128)S(1)}, f32[8,8]{1,0:T(8,128)}, u32[]{:S(2)}) copy-start(f32[8,8]{1,0:T(8,128)} %kx_ref.1) | copy-start | bytes 772
  4.5 14.7 %copy-start.2 = (f32[8,8]{1,0:T(8,128)S(1)}, f32[8,8]{1,0:T(8,128)}, u32[]{:S(2)}) copy-start(f32[8,8]{1,0:T(8,128)} %ky_ref.1) | copy-start | bytes 772
  4.6 14.7 %copy-start.3 = (f32[4,8]{1,0:T(4,128)S(1)}, f32[4,8]{1,0:T(4,128)}, u32[]{:S(2)}) copy-start(f32[4,8]{1,0:T(4,128)} %hop_ref.1) | copy-start | bytes 388
  4.6 56.1 %all-to-all-start = ((f32[32,128,128]{2,1,0:T(8,128)}), f32[32,128,128]{2,1,0:T(8,128)S(1)}, u32[]{:S(2)}, u32[]{:S(2)}) async-start(f32[32,128,128]{2,1,0:T(8,128)} %pack.1), calls=%async_computation | async-start | bytes 4194304 | tf_op jit(solution)/shard_map/all_to_all | solution.py:564
  60.7 11.3 %collective-permute-start = (f32[32,16,128]{2,1,0:T(8,128)S(1)}, f32[32,16,128]{2,1,0:T(8,128)S(1)}, u32[]{:S(2)}, u32[]{:S(2)}) collective-permute-start(f32[32,16,128]{2,1,0:T(8,128)S(1)} %slice.12), channel_id=1, source_target_pairs={{0,1},{1,2},{2,3},{3,4},{4,5},{5,6},{6,7},{7,8},{8,9},{9,10},{10,1... | collective-permute-start | bytes 786440 | tf_op jit(solution)/shard_map/ppermute | solution.py:374
  62.3 9.7 %collective-permute-start.1 = (f32[32,24,128]{2,1,0:T(8,128)S(1)}, f32[32,24,128]{2,1,0:T(8,128)S(1)}, u32[]{:S(2)}, u32[]{:S(2)}) collective-permute-start(f32[32,24,128]{2,1,0:T(8,128)S(1)} %slice.13), channel_id=1, source_target_pairs={{1,0},{2,1},{3,2},{4,3},{5,4},{6,5},{7,6},{8,7},{9,8},{10,9},{11,1... | collective-permute-start | bytes 1179656 | tf_op jit(solution)/shard_map/ppermute | solution.py:375
  75.9 15.7 %all-to-all-start.1 = ((f32[96,4,128]{2,1,0:T(4,128)}), f32[96,4,128]{2,1,0:T(4,128)S(1)}, u32[]{:S(2)}, u32[]{:S(2)}) async-start(f32[96,4,128]{2,1,0:T(4,128)} %bitcast.4), calls=%async_computation.1 | async-start | bytes 393216 | tf_op jit(solution)/shard_map/all_to_all | solution.py:564
  108.3 15.0 %all-to-all-start.3 = ((f32[96,4,128]{2,1,0:T(4,128)}), f32[96,4,128]{2,1,0:T(4,128)S(1)}, u32[]{:S(2)}, u32[]{:S(2)}) async-start(f32[96,4,128]{2,1,0:T(4,128)} %bitcast.10), calls=%async_computation.3 | async-start | bytes 393216 | tf_op jit(solution)/shard_map/all_to_all | solution.py:564
  123.3 54.6 %all-to-all-start.4 = ((f32[32,128,128]{2,1,0:T(8,128)}), f32[32,128,128]{2,1,0:T(8,128)S(1)}, u32[]{:S(2)}, u32[]{:S(2)}) async-start(f32[32,128,128]{2,1,0:T(8,128)} %get-tuple-element.33), calls=%async_computation.4 | async-start | bytes 4194304 | tf_op jit(solution)/shard_map/all_to_all | solution.py:564

commit v6 on v5

--- a/solution.py
+++ b/solution.py
@@ -294,7 +294,7 @@
         ingest(r_ref, pl.multiple_of((pair - OWN_PAIRS[0]) * 8, 8), pair, fa, ah, al)
         return carry
 
-    lax.fori_loop(*OWN_PAIRS, take, 0, unroll=4)
+    lax.fori_loop(*OWN_PAIRS, take, 0, unroll=2)
     for load in loads:
         load.wait()
     for count, step in enumerate(steps(ch_ref, cl_ref, fa, fb, ah, al, bh, bl)):
@@ -304,7 +304,7 @@
             return carry
 
         low, high = OWN_PAIRS[0] + 1 + count, OWN_PAIRS[1] - 1 - count
-        lax.fori_loop(low, high, body, 0, unroll=(high - low) // 2)
+        lax.fori_loop(low, high, body, 0, unroll=high - low)
 
 
 def interior(received, coef_high, coef_low):
@@ -371,8 +371,8 @@
 def filtered_blocks(received, coef_high, coef_low):
     count = lax.axis_size(ALL)
     chain = [(i, i + 1) for i in range(count - 1)]
+    right = lax.ppermute(received[:, : 4 * (WINDOW - LEFT - 32)], ALL, [(j, i) for i, j in chain])
     left = lax.ppermute(received[:, 128 - 4 * LEFT :], ALL, chain)
-    right = lax.ppermute(received[:, : 4 * (WINDOW - LEFT - 32)], ALL, [(j, i) for i, j in chain])
     state = interior(received, coef_high, coef_low)
     half = pltpu.HBM((2048 + EDGE, 256), jnp.bfloat16)
     fields = [pltpu.VMEM(value.shape, value.dtype) for value in state[:6]]
@@ -447,12 +447,12 @@
         pivots[own] = jnp.where(row == k % 8, pivot, pivots[own])
         scale = 1.0 / pivot
         ratio = {t: cols[k][t] * scale for t in range(own, 4)}
-        ratio[own] = jnp.where(row > k % 8, ratio[own], 0.0)
         line = [spread(part, k) for part in lines[own]]
         for j in range(k + 1, 32):
-            weight = spread(ratio[j // 8], j)
+            weight = spread(cols[k][j // 8], j)
             for t in range(j // 8, 4):
-                cols[j][t] = cols[j][t] - cols[k][t] * weight
+                cols[j][t] = cols[j][t] - ratio[t] * weight
+        ratio[own] = jnp.where(row > k % 8, ratio[own], 0.0)
         for t in range(own, 4):
             lines[t] = [part - ratio[t] * above for part, above in zip(lines[t], line)]
     roots = [lax.rsqrt(pivots[t]) for t in range(4)]
@@ -467,9 +467,13 @@
         lines = aug[rows, :]
         lines = panel_solve(pltpu.roll(lines[:, :LANES], LANES - 32 * p, 1), lines)
         aug[rows, :] = lines
-        lane = lax.broadcasted_iota(jnp.int32, (32, LANES), 1)
-        upper = jnp.where(lane >= 32 * (p + 1), lines[:, :LANES], 0.0)
-        aug[...] = aug[...] - dot(upper, lines, ((0,), (0,)), HIGHEST)
+
+        @pl.when(p < 3)
+        def update():
+            lane = lax.broadcasted_iota(jnp.int32, (32, LANES), 1)
+            upper = jnp.where(lane >= 32 * (p + 1), lines[:, :LANES], 0.0)
+            aug[...] = aug[...] - dot(upper, lines, ((0,), (0,)), HIGHEST)
+
         return carry
 
     lax.fori_loop(0, 4, panel, 0)

time: 181 us -> 179 us (0.989)
  Pallas kernels: 44.2 us -> 39.7 us
  starting transfers between devices: 25.6 us -> 27.9 us
    pallas_call x1, Pallas kernels: 8.22 us -> 4.61 us  [interior(): pl.pallas_call(interior_kernel, out_shape=(field,) * 2 + (half,) * 4 + (b...]
    all_to_all x4, starting transfers between devices: 22.6 us -> 24.8 us  [swap(): return lax.all_to_all(rows, ALL, 0, 0, tiled=True).reshape(parts.shape)]
  transfers between devices with their start and end apart: 6 -> 6, of which waited for: 3 -> 3; matrix products, arithmetic and copies ran while one was open for 0% -> 0% of each run, Pallas kernels for 19% -> 16%
where the time goes in v6:
time: 179 us; the launch traced here: 178 us
  waiting for transfers between devices  85.8 us (48%)
  Pallas kernels  39.7 us (22%)
  starting transfers between devices  27.9 us (16%)
  blocking collectives  22.9 us (13%)
    all_to_all x4, waiting for transfers between devices, swap(): return lax.all_to_all(rows, ALL, 0, 0, tiled=True).reshape(parts.shape)  85.8 us
    all_to_all x4, starting transfers between devices, swap(): return lax.all_to_all(rows, ALL, 0, 0, tiled=True).reshape(parts.shape)  24.8 us
    all_to_all x1, blocking collectives, swap(): return lax.all_to_all(rows, ALL, 0, 0, tiled=True).reshape(parts.shape)  15.7 us
    pallas_call x1, Pallas kernels, basis(): pl.pallas_call(functools.partial(basis_kernel, entries), out_shape=(jax.S...  11.5 us
    all_gather x1, blocking collectives, fast(): lax.all_gather((region + 1).astype(jnp.float32), 'slab', axis=0, tiled=True)  7.22 us
    pallas_call x1, Pallas kernels, coefficients(): pl.pallas_call(coef_kernel, out_shape=(shape, shape), compiler_params=VME...  6.31 us
    pallas_call x1, Pallas kernels, moment_of(): pl.pallas_call(moment_kernel, out_shape=jax.ShapeDtypeStruct((3 * LANES,...  5.59 us
    pallas_call x1, Pallas kernels, interior(): pl.pallas_call(interior_kernel, out_shape=(field,) * 2 + (half,) * 4 + (b...  4.61 us
  transfers between devices with their start and end apart: 6, of which 3 were waited for; matrix products, arithmetic and copies ran while one was open for 0% of the time, Pallas kernels for 16%

profile of v6, /device:TPU:0, one launch (start us, length us, event | category | flops | bytes accessed | tf_op | source)
XLA Modules:
  0.0 178.4 jit_solution(12955564312311031804)
XLA Ops:
  0.6 3.9 %pack.1 = f32[32,128,128]{2,1,0:T(8,128)} custom-call(f32[256,16,128]{2,1,0:T(8,128)} %bitcast.26), custom_call_target="tpu_custom_call" | custom-call | tf_op jit(solution)/shard_map/pack/pallas_call | solution.py:92
  4.5 0.0 copy-start.4
  4.5 0.0 copy-start
  4.5 0.0 copy-start.1
  4.5 0.0 copy-start.2
  4.6 0.0 copy-start.3
  4.6 7.3 %all-to-all-start = ((f32[32,128,128]{2,1,0:T(8,128)}), f32[32,128,128]{2,1,0:T(8,128)S(1)}, u32[]{:S(2)}, u32[]{:S(2)}) async-start(f32[32,128,128]{2,1,0:T(8,128)} %pack.1), calls=%async_computation | async-start | bytes 4194304 | tf_op jit(solution)/shard_map/all_to_all | solution.py:568
  11.9 0.0 copy-done.4
  11.9 7.2 %all-gather = f32[4,2,1024]{2,1,0:T(2,128)S(1)} all-gather(f32[1,2,1024]{2,1,0:T(2,128)S(1)} %convert_bitcast_fusion), channel_id=1, replica_groups=mesh['blk'=8,'slab'=4] {'slab'}, dimensions={0}, use_global_device_ids=true | all-gather | bytes 40960 | tf_op jit(solution)/shard_map/all_gather | solution.py:604
  19.2 0.1 pad_dynamic-slice_fusion.reg_ref
  19.3 6.3 %coefficients.1 = (bf16[21,128,256]{2,1,0:T(8,128)(2,1)}, bf16[21,128,256]{2,1,0:T(8,128)(2,1)}) custom-call(f32[8,128]{1,0:T(8,128)S(1)} %pad_dynamic-slice_fusion.reg_ref, f32[4,8,8]{2,1,0:T(8,128)S(1)} %copy-done, f32[4,8]{1,0:T(4,128)S(1)} %copy-done.3, f32[8,8]{1,0:T(8,128)S(1)} %copy-done.1, f32[8,8]{1,0:T(8,128)S(1)} %copy-done.2), custom_call_target="tpu_custom_call" | custom-call | tf_op jit(solution)/shard_map/coefficients/pallas_call | solution.py:219
  25.6 35.1 %all-to-all-done.r_ref = f32[32,128,128]{2,1,0:T(8,128)S(1)} async-done(((f32[32,128,128]{2,1,0:T(8,128)}), f32[32,128,128]{2,1,0:T(8,128)S(1)}, u32[]{:S(2)}, u32[]{:S(2)}) %all-to-all-start) | async-done | bytes 2097184 | tf_op jit(solution)/shard_map/all_to_all | solution.py:568
  60.7 1.6 collective-permute-start
  62.3 1.5 collective-permute-start.1
  63.8 4.6 %interior.1 = (f32[2688,256]{1,0:T(8,128)S(1)}, f32[2688,256]{1,0:T(8,128)S(1)}, bf16[2816,256]{1,0:T(8,128)(2,1)S(1)}, bf16[2816,256]{1,0:T(8,128)(2,1)S(1)}, b...) custom-call(f32[32,128,128]{2,1,0:T(8,128)S(1)} %all-to-all-done.r_r, ...), custom_call_target="tpu_custom_call" | custom-call | flops 8000000000 | bytes 20000000 | tf_op jit(solution)/shard_map/interior/pallas_call | solution.py:315
  68.4 0.0 collective-permute-done.left_ref
  68.4 0.0 collective-permute-done.1.right_ref
  68.4 3.9 %edges.1 = (bf16[2112,256]{1,0:T(8,128)(2,1)}, bf16[2112,256]{1,0:T(8,128)(2,1)}, f32[384,128]{1,0:T(8,128)}, f32[2688,256]{1,0:T(8,128)S(1)}, f32[2688,256]{1,0...) custom-call(f32[32,16,128]{2,1,0:T(8,128)S(1)} %collective-permute-d, ...), custom_call_target="tpu_custom_call", output_to_operand_aliasing={{3}: (2, {}), {4}: (3, {}), {5}: (4, {}), {6}: (5, {}), {7}... | custom-call | tf_op jit(solution)/shard_map/edges/pallas_call | solution.py:379
  72.3 9.1 %all-to-all-start.1 = ((f32[96,4,128]{2,1,0:T(4,128)}), f32[96,4,128]{2,1,0:T(4,128)S(1)}, u32[]{:S(2)}, u32[]{:S(2)}) async-start(f32[96,4,128]{2,1,0:T(4,128)} %bitcast.4), calls=%async_computation.1 | async-start | bytes 393216 | tf_op jit(solution)/shard_map/all_to_all | solution.py:568
  81.4 5.6 %moment.1 = f32[384,128]{1,0:T(8,128)S(1)} custom-call(bf16[2112,256]{1,0:T(8,128)(2,1)} %get-tuple-element.30.vh_ref.vh_hbm, bf16[2112,256]{1,0:T(8,128)(2,1)} %get-tuple-element.31.vl_ref.vl_hbm, bf16[21,128,256]{2,1,0:T(8,128)(2,1)} %get-tuple-element.19.ch_hbm.ch_ref, bf16[21,128,256]{2,1,0:T(8,128)(2,1)} %get-tuple-element.20.cl_hbm.cl_ref, ...), custom_call_target="tpu_custom_call" | custom-call | flops 4000000000 | bytes 10000000 | tf_op jit(solution)/shard_map/moment/pallas_call | solution.py:420
  87.0 3.3 %all-to-all-done.1 = f32[96,4,128]{2,1,0:T(4,128)S(1)} async-done(((f32[96,4,128]{2,1,0:T(4,128)}), f32[96,4,128]{2,1,0:T(4,128)S(1)}, u32[]{:S(2)}, u32[]{:S(2)}) %all-to-all-start.1) | async-done | bytes 196640 | tf_op jit(solution)/shard_map/all_to_all | solution.py:568
  90.3 0.1 reduce_sum.18
  90.4 0.1 pad_maximum_fusion
  90.5 15.7 %all_to_all.25 = f32[192,4,128]{2,1,0:T(4,128)S(1)} all-to-all(f32[192,4,128]{2,1,0:T(4,128)S(1)} %bitcast.28), channel_id=1, replica_groups=mesh['blk'=8,'slab'=4] {'blk','slab'}, dimensions={0} | all-to-all | bytes 786432 | tf_op jit(solution)/shard_map/all_to_all | solution.py:568
  106.2 0.7 broadcast_in_dim.5
  106.9 2.6 %all-to-all-start.3 = ((f32[96,4,128]{2,1,0:T(4,128)}), f32[96,4,128]{2,1,0:T(4,128)S(1)}, u32[]{:S(2)}, u32[]{:S(2)}) async-start(f32[96,4,128]{2,1,0:T(4,128)} %bitcast.10), calls=%async_computation.3 | async-start | bytes 393216 | tf_op jit(solution)/shard_map/all_to_all | solution.py:568
  109.6 11.5 %basis.1 = (f32[256,256]{1,0:T(8,128)S(1)}, f32[32,128,128]{2,1,0:T(8,128)}) custom-call(f32[768,128]{1,0:T(8,128)S(1)} %bitcast.23, bf16[2112,256]{1,0:T(8,128)(2,1)} %get-tuple-element.30.vh_ref.vh_hbm, bf16[2112,256]{1,0:T(8,128)(2,1)} %get-tuple-element.31.vl_ref.vl_hbm), custom_call_target="tpu_custom_call" | custom-call | flops 4000000000 | bytes 20000000 | tf_op jit(solution)/shard_map/basis/pallas_call | solution.py:538
  121.0 0.0 all-to-all-done.3
  121.0 5.8 %all-to-all-start.4 = ((f32[32,128,128]{2,1,0:T(8,128)}), f32[32,128,128]{2,1,0:T(8,128)S(1)}, u32[]{:S(2)}, u32[]{:S(2)}) async-start(f32[32,128,128]{2,1,0:T(8,128)} %get-tuple-element.33), calls=%async_computation.4 | async-start | bytes 4194304 | tf_op jit(solution)/shard_map/all_to_all | solution.py:568
  126.9 1.4 project.1
  128.3 47.4 %all-to-all-done.4 = f32[32,128,128]{2,1,0:T(8,128)S(1)} async-done(((f32[32,128,128]{2,1,0:T(8,128)}), f32[32,128,128]{2,1,0:T(8,128)S(1)}, u32[]{:S(2)}, u32[]{:S(2)}) %all-to-all-start.4) | async-done | bytes 2097184 | tf_op jit(solution)/shard_map/all_to_all | solution.py:568
  175.7 2.5 %unpack.1 = f32[32,128,128]{2,1,0:T(8,128)} custom-call(f32[4096,128]{1,0:T(8,128)S(1)} %bitcast.21), custom_call_target="tpu_custom_call" | custom-call | tf_op jit(solution)/shard_map/unpack/pallas_call | solution.py:128
  (10 shorter events, 0.2 us)
Async XLA Ops:
  4.5 7.4 %copy-start.4 = (s32[2,1024]{1,0:T(2,128)S(1)}, s32[2,1024]{1,0:T(2,128)}, u32[]{:S(2)}) copy-start(s32[2,1024]{1,0:T(2,128)} %param.7) | copy-start | bytes 24580
  4.5 14.7 %copy-start = (f32[4,8,8]{2,1,0:T(8,128)S(1)}, f32[4,8,8]{2,1,0:T(8,128)}, u32[]{:S(2)}) copy-start(f32[4,8,8]{2,1,0:T(8,128)} %onsite_ref.1) | copy-start | bytes 3076
  4.5 14.7 %copy-start.1 = (f32[8,8]{1,0:T(8,128)S(1)}, f32[8,8]{1,0:T(8,128)}, u32[]{:S(2)}) copy-start(f32[8,8]{1,0:T(8,128)} %kx_ref.1) | copy-start | bytes 772
  4.5 14.7 %copy-start.2 = (f32[8,8]{1,0:T(8,128)S(1)}, f32[8,8]{1,0:T(8,128)}, u32[]{:S(2)}) copy-start(f32[8,8]{1,0:T(8,128)} %ky_ref.1) | copy-start | bytes 772
  4.6 14.7 %copy-start.3 = (f32[4,8]{1,0:T(4,128)S(1)}, f32[4,8]{1,0:T(4,128)}, u32[]{:S(2)}) copy-start(f32[4,8]{1,0:T(4,128)} %hop_ref.1) | copy-start | bytes 388
  4.6 56.1 %all-to-all-start = ((f32[32,128,128]{2,1,0:T(8,128)}), f32[32,128,128]{2,1,0:T(8,128)S(1)}, u32[]{:S(2)}, u32[]{:S(2)}) async-start(f32[32,128,128]{2,1,0:T(8,128)} %pack.1), calls=%async_computation | async-start | bytes 4194304 | tf_op jit(solution)/shard_map/all_to_all | solution.py:568
  60.7 7.7 %collective-permute-start = (f32[32,16,128]{2,1,0:T(8,128)S(1)}, f32[32,16,128]{2,1,0:T(8,128)S(1)}, u32[]{:S(2)}, u32[]{:S(2)}) collective-permute-start(f32[32,16,128]{2,1,0:T(8,128)S(1)} %slice.12), channel_id=1, source_target_pairs={{0,1},{1,2},{2,3},{3,4},{4,5},{5,6},{6,7},{7,8},{8,9},{9,10},{10,1... | collective-permute-start | bytes 786440 | tf_op jit(solution)/shard_map/ppermute | solution.py:375
  62.3 6.1 %collective-permute-start.1 = (f32[32,24,128]{2,1,0:T(8,128)S(1)}, f32[32,24,128]{2,1,0:T(8,128)S(1)}, u32[]{:S(2)}, u32[]{:S(2)}) collective-permute-start(f32[32,24,128]{2,1,0:T(8,128)S(1)} %slice.13), channel_id=1, source_target_pairs={{1,0},{2,1},{3,2},{4,3},{5,4},{6,5},{7,6},{8,7},{9,8},{10,9},{11,1... | collective-permute-start | bytes 1179656 | tf_op jit(solution)/shard_map/ppermute | solution.py:374
  72.3 18.0 %all-to-all-start.1 = ((f32[96,4,128]{2,1,0:T(4,128)}), f32[96,4,128]{2,1,0:T(4,128)S(1)}, u32[]{:S(2)}, u32[]{:S(2)}) async-start(f32[96,4,128]{2,1,0:T(4,128)} %bitcast.4), calls=%async_computation.1 | async-start | bytes 393216 | tf_op jit(solution)/shard_map/all_to_all | solution.py:568
  106.9 14.1 %all-to-all-start.3 = ((f32[96,4,128]{2,1,0:T(4,128)}), f32[96,4,128]{2,1,0:T(4,128)S(1)}, u32[]{:S(2)}, u32[]{:S(2)}) async-start(f32[96,4,128]{2,1,0:T(4,128)} %bitcast.10), calls=%async_computation.3 | async-start | bytes 393216 | tf_op jit(solution)/shard_map/all_to_all | solution.py:568
  121.0 54.6 %all-to-all-start.4 = ((f32[32,128,128]{2,1,0:T(8,128)}), f32[32,128,128]{2,1,0:T(8,128)S(1)}, u32[]{:S(2)}, u32[]{:S(2)}) async-start(f32[32,128,128]{2,1,0:T(8,128)} %get-tuple-element.33), calls=%async_computation.4 | async-start | bytes 4194304 | tf_op jit(solution)/shard_map/all_to_all | solution.py:568

commit v7 on v6

--- a/solution.py
+++ b/solution.py
@@ -15,6 +15,7 @@
 LANES = 128
 ALL = ("blk", "slab")
 LEFT = 4
+RIGHT = 5
 WINDOW = 42
 VMEM = pltpu.CompilerParams(vmem_limit_bytes=24 * 1024 * 1024)
 ON_CHIP = pl.BlockSpec(memory_space=pltpu.VMEM)
@@ -22,8 +23,10 @@
 HIGHEST = lax.Precision.HIGHEST
 OWN = slice(0, 2048)
 OWN_PAIRS = 2, 18
+INNER = 6, 14
 PAIR = 128
 EDGE = 64
+PACKED = 320
 
 
 def off_chip(*arrays):
@@ -234,17 +237,30 @@
 
 
 def lower_blocks(square):
-    return jnp.concatenate(
-        [square[:LANES, :LANES], square[LANES:, :LANES], square[LANES:, LANES:]], axis=0
-    )
-
-
-def ingest(ref, start, pair, field, high, low):
+    first, last = square[:LANES, :LANES], square[LANES:, LANES:]
+    left = lax.broadcasted_iota(jnp.int32, (64, LANES), 1) < 64
+    corners = jnp.where(left, first[:64], pltpu.roll(last[:64], 64, 1))
+    return jnp.concatenate([corners, first[64:], last[64:], square[LANES:, :LANES]], axis=0)
+
+
+def whole_blocks(rows):
+    row = lax.broadcasted_iota(jnp.int32, (LANES, LANES), 0)
+    upper = (row < 64) & (lax.broadcasted_iota(jnp.int32, (LANES, LANES), 1) >= 64)
+
+    def mirrored(top, bottom):
+        block = jnp.concatenate([top, bottom], axis=0)
+        return jnp.where(upper, block.T, block)
+
+    first = mirrored(rows[:64], rows[64:128])
+    return first, rows[192:], mirrored(pltpu.roll(rows[:64], 64, 1), rows[128:192])
+
+
+def ingest(load, pair, field, high, low):
     at = pair * PAIR
     for half in range(2):
         lanes = slice(half * LANES, half * LANES + LANES)
         for slab in range(4):
-            pieces = exchange([ref[(half * 4 + j) * 4 + slab, pl.ds(start, 8), :] for j in range(4)], 32)
+            pieces = exchange([load((half * 4 + j) * 4 + slab) for j in range(4)], 32)
             for mid in range(2):
                 for column, piece in enumerate(halves(pieces[2 * mid], pieces[2 * mid + 1])):
                     field[pl.ds(at + (column * 64 + mid * 32 + slab * 8), 8), lanes] = piece[0]
@@ -282,7 +298,13 @@
     return first, even, odd, even
 
 
-def interior_kernel(r_ref, ch_hbm, cl_hbm, fa, fb, ah, al, bh, bl, ch_ref, cl_ref, sem):
+def gram_of(high, low):
+    dims = ((0,), (0,))
+    cross = dot(high, low, dims)
+    return dot(high, high, dims) + (cross + cross.T)
+
+
+def interior_kernel(r_ref, ch_hbm, cl_hbm, fa, fb, ah, al, bh, bl, ch_ref, cl_ref, g_ref, sem):
     loads = [
         pltpu.make_async_copy(ch_hbm, ch_ref, sem.at[0]),
         pltpu.make_async_copy(cl_hbm, cl_ref, sem.at[1]),
@@ -291,7 +313,8 @@
         load.start()
 
     def take(pair, carry):
-        ingest(r_ref, pl.multiple_of((pair - OWN_PAIRS[0]) * 8, 8), pair, fa, ah, al)
+        rows = pl.ds(pl.multiple_of((pair - OWN_PAIRS[0]) * 8, 8), 8)
+        ingest(lambda source: r_ref[source, rows, :], pair, fa, ah, al)
         return carry
 
     lax.fori_loop(*OWN_PAIRS, take, 0, unroll=2)
@@ -305,6 +328,8 @@
 
         low, high = OWN_PAIRS[0] + 1 + count, OWN_PAIRS[1] - 1 - count
         lax.fori_loop(low, high, body, 0, unroll=high - low)
+    rows = slice(INNER[0] * PAIR + EDGE, INNER[1] * PAIR + EDGE)
+    g_ref[...] = gram_of(ah[rows, :], al[rows, :])
 
 
 def interior(received, coef_high, coef_low):
@@ -314,9 +339,9 @@
     bands = pltpu.VMEM((pairs, PAIR, 256), jnp.bfloat16)
     return pl.pallas_call(
         interior_kernel,
-        out_shape=(field,) * 2 + (half,) * 4 + (bands,) * 2,
+        out_shape=(field,) * 2 + (half,) * 4 + (bands,) * 2 + (pltpu.VMEM((256, 256), jnp.float32),),
         in_specs=[ON_CHIP, OFF_CHIP, OFF_CHIP],
-        out_specs=(ON_CHIP,) * 8,
+        out_specs=(ON_CHIP,) * 9,
         scratch_shapes=[pltpu.SemaphoreType.DMA((2,))],
         compiler_params=VMEM,
         cost_estimate=pl.CostEstimate(flops=int(8e9), transcendentals=0, bytes_accessed=int(2e7)),
@@ -325,9 +350,9 @@
 
 
 def edges_kernel(left_ref, right_ref, *refs):
-    (ch_ref, cl_ref), (vh_hbm, vl_hbm, g_ref) = refs[6:8], refs[8:11]
-    fa, fb, ah, al, bh, bl = fields = refs[11:17]
-    sem = refs[17]
+    (ch_ref, cl_ref, inner_ref), (vh_hbm, vl_hbm, g_ref) = refs[6:9], refs[9:12]
+    fa, fb, ah, al, bh, bl = fields = refs[12:18]
+    sem = refs[18]
     pairs = WINDOW // 2
     first_row = OWN_PAIRS[0] * PAIR + EDGE
 
@@ -339,8 +364,7 @@
             pltpu.make_async_copy(al.at[rows, :], vl_hbm.at[target, :], sem.at[index + 1]),
         ]
 
-    inner = OWN_PAIRS[0] + 4, OWN_PAIRS[1] - 4
-    stores = results(inner[0] * PAIR, inner[1] * PAIR, 0)
+    stores = results(INNER[0] * PAIR, INNER[1] * PAIR, 0)
     for store in stores:
         store.start()
     zero = jnp.zeros((EDGE, 256), jnp.bfloat16)
@@ -348,22 +372,28 @@
         ref[0:EDGE, :] = zero
         ref[pairs * PAIR + EDGE :, :] = zero
     for pair in range(OWN_PAIRS[0]):
-        ingest(left_ref, pair * 8, pair, fa, ah, al)
+        ingest(lambda source, pair=pair: left_ref[source, 8 * pair : 8 * pair + 8, :], pair, fa, ah, al)
     for pair in range(OWN_PAIRS[1], pairs):
-        ingest(right_ref, (pair - OWN_PAIRS[1]) * 8, pair, fa, ah, al)
+
+        def load(source, start=8 * (pair - OWN_PAIRS[1])):
+            count = min(8, 4 * RIGHT - start)
+            rows = right_ref[4 * RIGHT * source + start : 4 * RIGHT * source + start + count, :]
+            return rows if count == 8 else jnp.concatenate([rows, jnp.zeros_like(rows)], axis=0)
+
+        ingest(load, pair, fa, ah, al)
     reach = ((0, pairs), (1, pairs - 1), (1, pairs - 1), (2, pairs - 2))
     for count, step in enumerate(steps(ch_ref, cl_ref, *fields)):
         low, high = OWN_PAIRS[0] + 1 + count, OWN_PAIRS[1] - 1 - count
         for pair in list(range(reach[count][0], low)) + list(range(high, reach[count][1])):
             step(pair)
     last = OWN_PAIRS[1] * PAIR + EDGE
-    stores += results(OWN_PAIRS[0] * PAIR, inner[0] * PAIR, 2) + results(inner[1] * PAIR, last, 4)
+    stores += results(OWN_PAIRS[0] * PAIR, INNER[0] * PAIR, 2) + results(INNER[1] * PAIR, last, 4)
     for store in stores[2:]:
         store.start()
-    own = slice(first_row, OWN_PAIRS[1] * PAIR + EDGE)
-    dims = ((0,), (0,))
-    cross = dot(ah[own, :], al[own, :], dims)
-    g_ref[...] = lower_blocks(dot(ah[own, :], ah[own, :], dims) + (cross + cross.T))
+    before = slice(first_row, INNER[0] * PAIR + EDGE)
+    after = slice(INNER[1] * PAIR + EDGE, OWN_PAIRS[1] * PAIR + EDGE)
+    high, low = (jnp.concatenate([ref[before, :], ref[after, :]], axis=0) for ref in (ah, al))
+    g_ref[...] = lower_blocks(inner_ref[...] + gram_of(high, low))
     for store in stores:
         store.wait()
 
@@ -371,15 +401,16 @@
 def filtered_blocks(received, coef_high, coef_low):
     count = lax.axis_size(ALL)
     chain = [(i, i + 1) for i in range(count - 1)]
-    right = lax.ppermute(received[:, : 4 * (WINDOW - LEFT - 32)], ALL, [(j, i) for i, j in chain])
+    leading = received.reshape(count, 32, 4, LANES)[:, :RIGHT]
+    right = lax.ppermute(leading, ALL, [(j, i) for i, j in chain]).reshape(-1, LANES)
     left = lax.ppermute(received[:, 128 - 4 * LEFT :], ALL, chain)
     state = interior(received, coef_high, coef_low)
     half = pltpu.HBM((2048 + EDGE, 256), jnp.bfloat16)
     fields = [pltpu.VMEM(value.shape, value.dtype) for value in state[:6]]
     return pl.pallas_call(
         edges_kernel,
-        out_shape=(half, half, pltpu.VMEM((3 * LANES, LANES), jnp.float32), *fields),
-        in_specs=[ON_CHIP] * 10,
+        out_shape=(half, half, pltpu.VMEM((PACKED, LANES), jnp.float32), *fields),
+        in_specs=[ON_CHIP] * 11,
         out_specs=(OFF_CHIP,) * 2 + (ON_CHIP,) * 7,
         input_output_aliases={i + 2: i + 3 for i in range(6)},
         scratch_shapes=[pltpu.SemaphoreType.DMA((6,))],
@@ -419,7 +450,7 @@
 def moment_of(vh, vl, coef_high, coef_low, gram):
     return pl.pallas_call(
         moment_kernel,
-        out_shape=jax.ShapeDtypeStruct((3 * LANES, LANES), jnp.float32),
+        out_shape=jax.ShapeDtypeStruct((PACKED, LANES), jnp.float32),
         scratch_shapes=[pltpu.VMEM((16 * 128 + 64, 256), jnp.bfloat16)] * 2,
         compiler_params=VMEM,
         cost_estimate=pl.CostEstimate(flops=int(4e9), transcendentals=0, bytes_accessed=int(1e7)),
@@ -489,13 +520,14 @@
     row = lax.broadcasted_iota(jnp.int32, (LANES, LANES), 0)
     eye = (row == lax.broadcasted_iota(jnp.int32, (LANES, LANES), 1)).astype(jnp.float32)
     for d in range(32):
-        gram[12 * d : 12 * d + 12, :] = both_ref[24 * d : 24 * d + 12, :] * (1.0 / entries)
-    aug[:, :LANES] = gram[:LANES, :]
+        gram[10 * d : 10 * d + 10, :] = both_ref[20 * d : 20 * d + 10, :] * (1.0 / entries)
+    above, below, after = whole_blocks(gram[...])
+    aug[:, :LANES] = above
     aug[:, LANES:] = eye
     half_inverse(aug)
     first = aug[:, LANES:]
-    upper = dot(first, gram[LANES : 2 * LANES, :], ((1,), (1,)), HIGHEST)
-    aug[:, :LANES] = gram[2 * LANES :, :] - dot(upper, upper, ((0,), (0,)), HIGHEST)
+    upper = dot(first, below, ((1,), (1,)), HIGHEST)
+    aug[:, :LANES] = after - dot(upper, upper, ((0,), (0,)), HIGHEST)
     aug[:, LANES:] = eye
     corner = dot(upper, first, ((0,), (0,)), HIGHEST)
     half_inverse(aug)
@@ -544,7 +576,7 @@
         in_specs=[ON_CHIP, OFF_CHIP, OFF_CHIP],
         out_specs=(ON_CHIP, OFF_CHIP),
         scratch_shapes=[
-            pltpu.VMEM((3 * LANES, LANES), jnp.float32),
+            pltpu.VMEM((PACKED, LANES), jnp.float32),
             pltpu.VMEM((LANES, 256), jnp.float32),
             pltpu.VMEM((2048, 256), jnp.bfloat16),
             pltpu.VMEM((2048, 256), jnp.bfloat16),
@@ -556,11 +588,11 @@
         compiler_params=VMEM,
         cost_estimate=pl.CostEstimate(flops=int(4e9), transcendentals=0, bytes_accessed=int(2e7)),
         name="basis",
-    )(both.reshape(768, LANES), *off_chip(vh, vl))
+    )(both.reshape(2 * PACKED, LANES), *off_chip(vh, vl))
 
 
 def parts_of(blocks):
-    return blocks.reshape(lax.axis_size(ALL), -1, 4, LANES)
+    return blocks.reshape(lax.axis_size(ALL), -1, 2, LANES)
 
 
 def swap(parts):
@@ -576,7 +608,7 @@
     first = pl.multiple_of(32 * lax.axis_index("blk"), 32)
     mine = w_ref[pl.ds(first, 32), :]
     left, right = mine[:, :LANES], mine[:, LANES:]
-    above, below, last = (moment_ref[LANES * k : LANES * k + LANES, :] for k in range(3))
+    above, below, last = whole_blocks(moment_ref[...])
     half_done = jnp.concatenate(
         [
             dot(left, above, precision=HIGHEST) + dot(right, below, precision=HIGHEST),
@@ -611,7 +643,7 @@
     share = swap(parts_of(own_gram)).sum(0)
     both = swap(jnp.concatenate([for_all(share), parts_of(own_moment)], axis=1))
     inverse, blocks = basis(both, entries, vh, vl)
-    moment = swap(for_all(both[:, 3:].sum(0))).reshape(3 * LANES, LANES)
+    moment = swap(for_all(both[:, 5:].sum(0))).reshape(PACKED, LANES)
     blocks, moment = lax.optimization_barrier((blocks, moment))
     states_out = unpack(swap(blocks))
     projected = project(moment, inverse, entries)

time: 179 us -> 177 us (0.989)
  transfers between devices with their start and end apart: 6 -> 6, of which waited for: 3 -> 3; matrix products, arithmetic and copies ran while one was open for 0% -> 0% of each run, Pallas kernels for 16% -> 17%
where the time goes in v7:
time: 177 us
  waiting for transfers between devices  85.3 us (48%)
  Pallas kernels  40.3 us (23%)
  starting transfers between devices  26.8 us (15%)
  blocking collectives  21.9 us (12%)
    all_to_all x4, waiting for transfers between devices, swap(): return lax.all_to_all(rows, ALL, 0, 0, tiled=True).reshape(parts.shape)  85.3 us
    all_to_all x4, starting transfers between devices, swap(): return lax.all_to_all(rows, ALL, 0, 0, tiled=True).reshape(parts.shape)  23.7 us
    all_to_all x1, blocking collectives, swap(): return lax.all_to_all(rows, ALL, 0, 0, tiled=True).reshape(parts.shape)  14.7 us
    pallas_call x1, Pallas kernels, basis(): pl.pallas_call(functools.partial(basis_kernel, entries), out_shape=(jax.S...  11.6 us
    all_gather x1, blocking collectives, fast(): lax.all_gather((region + 1).astype(jnp.float32), 'slab', axis=0, tiled=True)  7.22 us
    pallas_call x1, Pallas kernels, coefficients(): pl.pallas_call(coef_kernel, out_shape=(shape, shape), compiler_params=VME...  6.31 us
    pallas_call x1, Pallas kernels, moment_of(): pl.pallas_call(moment_kernel, out_shape=jax.ShapeDtypeStruct((PACKED, LAN...  5.64 us
    pallas_call x1, Pallas kernels, interior(): pl.pallas_call(interior_kernel, out_shape=(field,) * 2 + (half,) * 4 + (b...  4.95 us
  transfers between devices with their start and end apart: 6, of which 3 were waited for; matrix products, arithmetic and copies ran while one was open for 0% of the time, Pallas kernels for 17%

profile of v7, /device:TPU:0, one launch (start us, length us, event | category | flops | bytes accessed | tf_op | source)
XLA Modules:
  0.0 176.5 jit_solution(16533915578079103280)
XLA Ops:
  0.6 3.9 %pack.1 = f32[32,128,128]{2,1,0:T(8,128)} custom-call(f32[256,16,128]{2,1,0:T(8,128)} %bitcast.30), custom_call_target="tpu_custom_call" | custom-call | tf_op jit(solution)/shard_map/pack/pallas_call | solution.py:95
  4.5 0.0 copy-start.4
  4.5 0.0 copy-start
  4.5 0.0 copy-start.1
  4.5 0.0 copy-start.2
  4.6 0.0 copy-start.3
  4.6 7.3 %all-to-all-start = ((f32[32,128,128]{2,1,0:T(8,128)}), f32[32,128,128]{2,1,0:T(8,128)S(1)}, u32[]{:S(2)}, u32[]{:S(2)}) async-start(f32[32,128,128]{2,1,0:T(8,128)} %pack.1), calls=%async_computation | async-start | bytes 4194304 | tf_op jit(solution)/shard_map/all_to_all | solution.py:600
  11.9 7.2 %all-gather = f32[4,2,1024]{2,1,0:T(2,128)S(1)} all-gather(f32[1,2,1024]{2,1,0:T(2,128)S(1)} %convert_bitcast_fusion), channel_id=1, replica_groups=mesh['blk'=8,'slab'=4] {'slab'}, dimensions={0}, use_global_device_ids=true | all-gather | bytes 40960 | tf_op jit(solution)/shard_map/all_gather | solution.py:636
  19.2 0.1 pad_dynamic-slice_fusion.reg_ref
  19.3 6.3 %coefficients.1 = (bf16[21,128,256]{2,1,0:T(8,128)(2,1)}, bf16[21,128,256]{2,1,0:T(8,128)(2,1)}) custom-call(f32[8,128]{1,0:T(8,128)S(1)} %pad_dynamic-slice_fusion.reg_ref, f32[4,8,8]{2,1,0:T(8,128)S(1)} %copy-done, f32[4,8]{1,0:T(4,128)S(1)} %copy-done.3, f32[8,8]{1,0:T(8,128)S(1)} %copy-done.1, f32[8,8]{1,0:T(8,128)S(1)} %copy-done.2), custom_call_target="tpu_custom_call" | custom-call | tf_op jit(solution)/shard_map/coefficients/pallas_call | solution.py:222
  25.6 35.1 %all-to-all-done.r_ref = f32[32,128,128]{2,1,0:T(8,128)S(1)} async-done(((f32[32,128,128]{2,1,0:T(8,128)}), f32[32,128,128]{2,1,0:T(8,128)S(1)}, u32[]{:S(2)}, u32[]{:S(2)}) %all-to-all-start) | async-done | bytes 2097184 | tf_op jit(solution)/shard_map/all_to_all | solution.py:600
  60.7 1.6 collective-permute-start
  62.3 1.5 collective-permute-start.1
  63.8 5.0 %interior.1 = (f32[2688,256]{1,0:T(8,128)S(1)}, f32[2688,256]{1,0:T(8,128)S(1)}, bf16[2816,256]{1,0:T(8,128)(2,1)S(1)}, bf16[2816,256]{1,0:T(8,128)(2,1)S(1)}, b...) custom-call(f32[32,128,128]{2,1,0:T(8,128)S(1)} %all-to-all-done.r_r, ...), custom_call_target="tpu_custom_call" | custom-call | flops 8000000000 | bytes 20000000 | tf_op jit(solution)/shard_map/interior/pallas_call | solution.py:340
  68.7 0.0 collective-permute-done.left_ref
  68.7 0.0 collective-permute-done.1
  68.7 3.9 %edges.1 = (bf16[2112,256]{1,0:T(8,128)(2,1)}, bf16[2112,256]{1,0:T(8,128)(2,1)}, f32[320,128]{1,0:T(8,128)}, f32[2688,256]{1,0:T(8,128)S(1)}, f32[2688,256]{1,0...) custom-call(f32[32,16,128]{2,1,0:T(8,128)S(1)} %collective-permute-d, ...), custom_call_target="tpu_custom_call", output_to_operand_aliasing={{3}: (2, {}), {4}: (3, {}), {5}: (4, {}), {6}: (5, {}), {7}... | custom-call | tf_op jit(solution)/shard_map/edges/pallas_call | solution.py:410
  72.7 8.0 %all-to-all-start.1 = ((f32[160,2,128]{2,1,0:T(2,128)}), f32[160,2,128]{2,1,0:T(2,128)S(1)}, u32[]{:S(2)}, u32[]{:S(2)}) async-start(f32[160,2,128]{2,1,0:T(2,128)} %bitcast.6), calls=%async_computation.1 | async-start | bytes 327680 | tf_op jit(solution)/shard_map/all_to_all | solution.py:600
  80.7 5.6 %moment.1 = f32[320,128]{1,0:T(8,128)S(1)} custom-call(bf16[2112,256]{1,0:T(8,128)(2,1)} %get-tuple-element.32.vh_ref.vh_hbm, bf16[2112,256]{1,0:T(8,128)(2,1)} %get-tuple-element.33.vl_ref.vl_hbm, bf16[21,128,256]{2,1,0:T(8,128)(2,1)} %get-tuple-element.20.ch_hbm.ch_ref, bf16[21,128,256]{2,1,0:T(8,128)(2,1)} %get-tuple-element.21.cl_hbm.cl_ref, ...), custom_call_target="tpu_custom_call" | custom-call | flops 4000000000 | bytes 10000000 | tf_op jit(solution)/shard_map/moment/pallas_call | solution.py:451
  86.3 2.9 %all-to-all-done.1 = f32[160,2,128]{2,1,0:T(2,128)S(1)} async-done(((f32[160,2,128]{2,1,0:T(2,128)}), f32[160,2,128]{2,1,0:T(2,128)S(1)}, u32[]{:S(2)}, u32[]{:S(2)}) %all-to-all-start.1) | async-done | bytes 163872 | tf_op jit(solution)/shard_map/all_to_all | solution.py:600
  89.3 0.1 reduce_sum.18
  89.4 0.1 pad_maximum_fusion
  89.5 14.7 %all_to_all.25 = f32[320,2,128]{2,1,0:T(2,128)S(1)} all-to-all(f32[320,2,128]{2,1,0:T(2,128)S(1)} %bitcast.32), channel_id=1, replica_groups=mesh['blk'=8,'slab'=4] {'blk','slab'}, dimensions={0} | all-to-all | bytes 655360 | tf_op jit(solution)/shard_map/all_to_all | solution.py:600
  104.3 0.1 slice_reduce_fusion
  104.3 0.7 broadcast_in_dim.5
  105.0 2.6 %all-to-all-start.3 = ((f32[160,2,128]{2,1,0:T(2,128)}), f32[160,2,128]{2,1,0:T(2,128)S(1)}, u32[]{:S(2)}, u32[]{:S(2)}) async-start(f32[160,2,128]{2,1,0:T(2,128)} %bitcast.12), calls=%async_computation.3 | async-start | bytes 327680 | tf_op jit(solution)/shard_map/all_to_all | solution.py:600
  107.6 11.6 %basis.1 = (f32[256,256]{1,0:T(8,128)S(1)}, f32[32,128,128]{2,1,0:T(8,128)}) custom-call(f32[640,128]{1,0:T(8,128)S(1)} %bitcast.26, bf16[2112,256]{1,0:T(8,128)(2,1)} %get-tuple-element.32.vh_ref.vh_hbm, bf16[2112,256]{1,0:T(8,128)(2,1)} %get-tuple-element.33.vl_ref.vl_hbm), custom_call_target="tpu_custom_call" | custom-call | flops 4000000000 | bytes 20000000 | tf_op jit(solution)/shard_map/basis/pallas_call | solution.py:570
  119.2 0.0 all-to-all-done.3
  119.2 5.8 %all-to-all-start.4 = ((f32[32,128,128]{2,1,0:T(8,128)}), f32[32,128,128]{2,1,0:T(8,128)S(1)}, u32[]{:S(2)}, u32[]{:S(2)}) async-start(f32[32,128,128]{2,1,0:T(8,128)} %get-tuple-element.35), calls=%async_computation.4 | async-start | bytes 4194304 | tf_op jit(solution)/shard_map/all_to_all | solution.py:600
  125.0 1.5 project.1
  126.6 47.3 %all-to-all-done.4 = f32[32,128,128]{2,1,0:T(8,128)S(1)} async-done(((f32[32,128,128]{2,1,0:T(8,128)}), f32[32,128,128]{2,1,0:T(8,128)S(1)}, u32[]{:S(2)}, u32[]{:S(2)}) %all-to-all-start.4) | async-done | bytes 2097184 | tf_op jit(solution)/shard_map/all_to_all | solution.py:600
  173.8 2.5 %unpack.1 = f32[32,128,128]{2,1,0:T(8,128)} custom-call(f32[4096,128]{1,0:T(8,128)S(1)} %bitcast.23), custom_call_target="tpu_custom_call" | custom-call | tf_op jit(solution)/shard_map/unpack/pallas_call | solution.py:131
  (10 shorter events, 0.1 us)
Async XLA Ops:
  4.5 7.4 %copy-start.4 = (s32[2,1024]{1,0:T(2,128)S(1)}, s32[2,1024]{1,0:T(2,128)}, u32[]{:S(2)}) copy-start(s32[2,1024]{1,0:T(2,128)} %param.7) | copy-start | bytes 24580
  4.5 14.7 %copy-start = (f32[4,8,8]{2,1,0:T(8,128)S(1)}, f32[4,8,8]{2,1,0:T(8,128)}, u32[]{:S(2)}) copy-start(f32[4,8,8]{2,1,0:T(8,128)} %onsite_ref.1) | copy-start | bytes 3076
  4.5 14.7 %copy-start.1 = (f32[8,8]{1,0:T(8,128)S(1)}, f32[8,8]{1,0:T(8,128)}, u32[]{:S(2)}) copy-start(f32[8,8]{1,0:T(8,128)} %kx_ref.1) | copy-start | bytes 772
  4.5 14.7 %copy-start.2 = (f32[8,8]{1,0:T(8,128)S(1)}, f32[8,8]{1,0:T(8,128)}, u32[]{:S(2)}) copy-start(f32[8,8]{1,0:T(8,128)} %ky_ref.1) | copy-start | bytes 772
  4.6 14.7 %copy-start.3 = (f32[4,8]{1,0:T(4,128)S(1)}, f32[4,8]{1,0:T(4,128)}, u32[]{:S(2)}) copy-start(f32[4,8]{1,0:T(4,128)} %hop_ref.1) | copy-start | bytes 388
  4.6 56.1 %all-to-all-start = ((f32[32,128,128]{2,1,0:T(8,128)}), f32[32,128,128]{2,1,0:T(8,128)S(1)}, u32[]{:S(2)}, u32[]{:S(2)}) async-start(f32[32,128,128]{2,1,0:T(8,128)} %pack.1), calls=%async_computation | async-start | bytes 4194304 | tf_op jit(solution)/shard_map/all_to_all | solution.py:600
  60.7 8.1 %collective-permute-start = (f32[32,16,128]{2,1,0:T(8,128)S(1)}, f32[32,16,128]{2,1,0:T(8,128)S(1)}, u32[]{:S(2)}, u32[]{:S(2)}) collective-permute-start(f32[32,16,128]{2,1,0:T(8,128)S(1)} %slice.12), channel_id=1, source_target_pairs={{0,1},{1,2},{2,3},{3,4},{4,5},{5,6},{6,7},{7,8},{8,9},{9,10},{10,1... | collective-permute-start | bytes 786440 | tf_op jit(solution)/shard_map/ppermute | solution.py:406
  62.3 6.5 %collective-permute-start.1 = (f32[32,5,4,128]{3,2,1,0:T(4,128)S(1)}, f32[32,5,4,128]{3,2,1,0:T(4,128)S(1)}, u32[]{:S(2)}, u32[]{:S(2)}) collective-permute-start(f32[32,5,4,128]{3,2,1,0:T(4,128)S(1)} %slice.13), channel_id=1, source_target_pairs={{1,0},{2,1},{3,2},{4,3},{5,4},{6,5},{7,6},{8,7},{9,8},{10,9},{11,1... | collective-permute-start | bytes 983048 | tf_op jit(solution)/shard_map/ppermute | solution.py:405
  72.7 16.6 %all-to-all-start.1 = ((f32[160,2,128]{2,1,0:T(2,128)}), f32[160,2,128]{2,1,0:T(2,128)S(1)}, u32[]{:S(2)}, u32[]{:S(2)}) async-start(f32[160,2,128]{2,1,0:T(2,128)} %bitcast.6), calls=%async_computation.1 | async-start | bytes 327680 | tf_op jit(solution)/shard_map/all_to_all | solution.py:600
  105.0 14.2 %all-to-all-start.3 = ((f32[160,2,128]{2,1,0:T(2,128)}), f32[160,2,128]{2,1,0:T(2,128)S(1)}, u32[]{:S(2)}, u32[]{:S(2)}) async-start(f32[160,2,128]{2,1,0:T(2,128)} %bitcast.12), calls=%async_computation.3 | async-start | bytes 327680 | tf_op jit(solution)/shard_map/all_to_all | solution.py:600
  119.2 54.6 %all-to-all-start.4 = ((f32[32,128,128]{2,1,0:T(8,128)}), f32[32,128,128]{2,1,0:T(8,128)S(1)}, u32[]{:S(2)}, u32[]{:S(2)}) async-start(f32[32,128,128]{2,1,0:T(8,128)} %get-tuple-element.35), calls=%async_computation.4 | async-start | bytes 4194304 | tf_op jit(solution)/shard_map/all_to_all | solution.py:600

commit v8 on v7

--- a/solution.py
+++ b/solution.py
@@ -69,8 +69,10 @@
     for load in loads:
         load.start()
     sends = [
-        pltpu.make_async_copy(scr.at[pl.ds(128 * d, 128), :], o_ref.at[d], out_sem.at[d])
-        for d in range(32)
+        pltpu.make_async_copy(
+            scr.at[pl.ds(512 * k, 512), :].reshape(4, LANES, LANES), o_ref.at[pl.ds(4 * k, 4)], out_sem.at[k]
+        )
+        for k in range(8)
     ]
     for part in range(2):
         loads[part].wait()
@@ -84,8 +86,7 @@
                 ]
                 turned = jnp.concatenate(parts, axis=0).T
                 scr[pl.ds((512 * part + 128 * tile) * 4 + r, 128, stride=4), :] = turned
-        for send in sends[16 * part : 16 * part + 16]:
-            send.start()
+            sends[4 * part + tile].start()
     for send in sends:
         send.wait()
 
@@ -101,7 +102,7 @@
             pltpu.VMEM((2, 256, 8, LANES), jnp.float32),
             pltpu.VMEM((4096, LANES), jnp.float32),
             pltpu.SemaphoreType.DMA((2,)),
-            pltpu.SemaphoreType.DMA((32,)),
+            pltpu.SemaphoreType.DMA((8,)),
         ],
         compiler_params=VMEM,
         name="pack",

time: 177 us -> 177 us (level)
  no operation moved by 1% of the time
where the time goes in v8:
time: 177 us; the launch traced here: 176 us
  waiting for transfers between devices  85.3 us (48%)
  Pallas kernels  39.8 us (22%)
  starting transfers between devices  26.8 us (15%)
  blocking collectives  21.9 us (12%)
    all_to_all x4, waiting for transfers between devices, swap(): return lax.all_to_all(rows, ALL, 0, 0, tiled=True).reshape(parts.shape)  85.3 us
    all_to_all x4, starting transfers between devices, swap(): return lax.all_to_all(rows, ALL, 0, 0, tiled=True).reshape(parts.shape)  23.7 us
    all_to_all x1, blocking collectives, swap(): return lax.all_to_all(rows, ALL, 0, 0, tiled=True).reshape(parts.shape)  14.7 us
    pallas_call x1, Pallas kernels, basis(): pl.pallas_call(functools.partial(basis_kernel, entries), out_shape=(jax.S...  11.6 us
    all_gather x1, blocking collectives, fast(): lax.all_gather((region + 1).astype(jnp.float32), 'slab', axis=0, tiled=True)  7.22 us
    pallas_call x1, Pallas kernels, coefficients(): pl.pallas_call(coef_kernel, out_shape=(shape, shape), compiler_params=VME...  6.31 us
    pallas_call x1, Pallas kernels, moment_of(): pl.pallas_call(moment_kernel, out_shape=jax.ShapeDtypeStruct((PACKED, LAN...  5.64 us
    pallas_call x1, Pallas kernels, interior(): pl.pallas_call(interior_kernel, out_shape=(field,) * 2 + (half,) * 4 + (b...  4.95 us
  transfers between devices with their start and end apart: 6, of which 3 were waited for; matrix products, arithmetic and copies ran while one was open for 0% of the time, Pallas kernels for 17%

profile of v8, /device:TPU:0, one launch (start us, length us, event | category | flops | bytes accessed | tf_op | source)
XLA Modules:
  0.0 176.0 jit_solution(12736376759169092437)
XLA Ops:
  0.6 3.4 %pack.1 = f32[32,128,128]{2,1,0:T(8,128)} custom-call(f32[256,16,128]{2,1,0:T(8,128)} %bitcast.30), custom_call_target="tpu_custom_call" | custom-call | tf_op jit(solution)/shard_map/pack/pallas_call | solution.py:96
  4.0 0.0 copy-start.4
  4.0 0.0 copy-start
  4.1 0.0 copy-start.1
  4.1 0.0 copy-start.2
  4.1 0.0 copy-start.3
  4.1 7.3 %all-to-all-start = ((f32[32,128,128]{2,1,0:T(8,128)}), f32[32,128,128]{2,1,0:T(8,128)S(1)}, u32[]{:S(2)}, u32[]{:S(2)}) async-start(f32[32,128,128]{2,1,0:T(8,128)} %pack.1), calls=%async_computation | async-start | bytes 4194304 | tf_op jit(solution)/shard_map/all_to_all | solution.py:601
  11.4 7.2 %all-gather = f32[4,2,1024]{2,1,0:T(2,128)S(1)} all-gather(f32[1,2,1024]{2,1,0:T(2,128)S(1)} %convert_bitcast_fusion), channel_id=1, replica_groups=mesh['blk'=8,'slab'=4] {'slab'}, dimensions={0}, use_global_device_ids=true | all-gather | bytes 40960 | tf_op jit(solution)/shard_map/all_gather | solution.py:637
  18.7 0.1 pad_dynamic-slice_fusion.reg_ref
  18.8 6.3 %coefficients.1 = (bf16[21,128,256]{2,1,0:T(8,128)(2,1)}, bf16[21,128,256]{2,1,0:T(8,128)(2,1)}) custom-call(f32[8,128]{1,0:T(8,128)S(1)} %pad_dynamic-slice_fusion.reg_ref, f32[4,8,8]{2,1,0:T(8,128)S(1)} %copy-done, f32[4,8]{1,0:T(4,128)S(1)} %copy-done.3, f32[8,8]{1,0:T(8,128)S(1)} %copy-done.1, f32[8,8]{1,0:T(8,128)S(1)} %copy-done.2), custom_call_target="tpu_custom_call" | custom-call | tf_op jit(solution)/shard_map/coefficients/pallas_call | solution.py:223
  25.1 35.1 %all-to-all-done.r_ref = f32[32,128,128]{2,1,0:T(8,128)S(1)} async-done(((f32[32,128,128]{2,1,0:T(8,128)}), f32[32,128,128]{2,1,0:T(8,128)S(1)}, u32[]{:S(2)}, u32[]{:S(2)}) %all-to-all-start) | async-done | bytes 2097184 | tf_op jit(solution)/shard_map/all_to_all | solution.py:601
  60.2 1.6 collective-permute-start
  61.8 1.5 collective-permute-start.1
  63.3 4.9 %interior.1 = (f32[2688,256]{1,0:T(8,128)S(1)}, f32[2688,256]{1,0:T(8,128)S(1)}, bf16[2816,256]{1,0:T(8,128)(2,1)S(1)}, bf16[2816,256]{1,0:T(8,128)(2,1)S(1)}, b...) custom-call(f32[32,128,128]{2,1,0:T(8,128)S(1)} %all-to-all-done.r_r, ...), custom_call_target="tpu_custom_call" | custom-call | flops 8000000000 | bytes 20000000 | tf_op jit(solution)/shard_map/interior/pallas_call | solution.py:341
  68.2 0.0 collective-permute-done.left_ref
  68.3 0.0 collective-permute-done.1
  68.3 3.9 %edges.1 = (bf16[2112,256]{1,0:T(8,128)(2,1)}, bf16[2112,256]{1,0:T(8,128)(2,1)}, f32[320,128]{1,0:T(8,128)}, f32[2688,256]{1,0:T(8,128)S(1)}, f32[2688,256]{1,0...) custom-call(f32[32,16,128]{2,1,0:T(8,128)S(1)} %collective-permute-d, ...), custom_call_target="tpu_custom_call", output_to_operand_aliasing={{3}: (2, {}), {4}: (3, {}), {5}: (4, {}), {6}: (5, {}), {7}... | custom-call | tf_op jit(solution)/shard_map/edges/pallas_call | solution.py:411
  72.2 8.0 %all-to-all-start.1 = ((f32[160,2,128]{2,1,0:T(2,128)}), f32[160,2,128]{2,1,0:T(2,128)S(1)}, u32[]{:S(2)}, u32[]{:S(2)}) async-start(f32[160,2,128]{2,1,0:T(2,128)} %bitcast.6), calls=%async_computation.1 | async-start | bytes 327680 | tf_op jit(solution)/shard_map/all_to_all | solution.py:601
  80.2 5.6 %moment.1 = f32[320,128]{1,0:T(8,128)S(1)} custom-call(bf16[2112,256]{1,0:T(8,128)(2,1)} %get-tuple-element.32.vh_ref.vh_hbm, bf16[2112,256]{1,0:T(8,128)(2,1)} %get-tuple-element.33.vl_ref.vl_hbm, bf16[21,128,256]{2,1,0:T(8,128)(2,1)} %get-tuple-element.20.ch_hbm.ch_ref, bf16[21,128,256]{2,1,0:T(8,128)(2,1)} %get-tuple-element.21.cl_hbm.cl_ref, ...), custom_call_target="tpu_custom_call" | custom-call | flops 4000000000 | bytes 10000000 | tf_op jit(solution)/shard_map/moment/pallas_call | solution.py:452
  85.9 2.9 %all-to-all-done.1 = f32[160,2,128]{2,1,0:T(2,128)S(1)} async-done(((f32[160,2,128]{2,1,0:T(2,128)}), f32[160,2,128]{2,1,0:T(2,128)S(1)}, u32[]{:S(2)}, u32[]{:S(2)}) %all-to-all-start.1) | async-done | bytes 163872 | tf_op jit(solution)/shard_map/all_to_all | solution.py:601
  88.8 0.1 reduce_sum.18
  88.9 0.1 pad_maximum_fusion
  89.1 14.7 %all_to_all.25 = f32[320,2,128]{2,1,0:T(2,128)S(1)} all-to-all(f32[320,2,128]{2,1,0:T(2,128)S(1)} %bitcast.32), channel_id=1, replica_groups=mesh['blk'=8,'slab'=4] {'blk','slab'}, dimensions={0} | all-to-all | bytes 655360 | tf_op jit(solution)/shard_map/all_to_all | solution.py:601
  103.8 0.1 slice_reduce_fusion
  103.8 0.7 broadcast_in_dim.5
  104.6 2.6 %all-to-all-start.3 = ((f32[160,2,128]{2,1,0:T(2,128)}), f32[160,2,128]{2,1,0:T(2,128)S(1)}, u32[]{:S(2)}, u32[]{:S(2)}) async-start(f32[160,2,128]{2,1,0:T(2,128)} %bitcast.12), calls=%async_computation.3 | async-start | bytes 327680 | tf_op jit(solution)/shard_map/all_to_all | solution.py:601
  107.1 11.6 %basis.1 = (f32[256,256]{1,0:T(8,128)S(1)}, f32[32,128,128]{2,1,0:T(8,128)}) custom-call(f32[640,128]{1,0:T(8,128)S(1)} %bitcast.26, bf16[2112,256]{1,0:T(8,128)(2,1)} %get-tuple-element.32.vh_ref.vh_hbm, bf16[2112,256]{1,0:T(8,128)(2,1)} %get-tuple-element.33.vl_ref.vl_hbm), custom_call_target="tpu_custom_call" | custom-call | flops 4000000000 | bytes 20000000 | tf_op jit(solution)/shard_map/basis/pallas_call | solution.py:571
  118.7 0.0 all-to-all-done.3
  118.7 5.8 %all-to-all-start.4 = ((f32[32,128,128]{2,1,0:T(8,128)}), f32[32,128,128]{2,1,0:T(8,128)S(1)}, u32[]{:S(2)}, u32[]{:S(2)}) async-start(f32[32,128,128]{2,1,0:T(8,128)} %get-tuple-element.35), calls=%async_computation.4 | async-start | bytes 4194304 | tf_op jit(solution)/shard_map/all_to_all | solution.py:601
  124.6 1.5 project.1
  126.1 47.3 %all-to-all-done.4 = f32[32,128,128]{2,1,0:T(8,128)S(1)} async-done(((f32[32,128,128]{2,1,0:T(8,128)}), f32[32,128,128]{2,1,0:T(8,128)S(1)}, u32[]{:S(2)}, u32[]{:S(2)}) %all-to-all-start.4) | async-done | bytes 2097184 | tf_op jit(solution)/shard_map/all_to_all | solution.py:601
  173.3 2.5 %unpack.1 = f32[32,128,128]{2,1,0:T(8,128)} custom-call(f32[4096,128]{1,0:T(8,128)S(1)} %bitcast.23), custom_call_target="tpu_custom_call" | custom-call | tf_op jit(solution)/shard_map/unpack/pallas_call | solution.py:132
  (10 shorter events, 0.1 us)
Async XLA Ops:
  4.0 7.4 %copy-start.4 = (s32[2,1024]{1,0:T(2,128)S(1)}, s32[2,1024]{1,0:T(2,128)}, u32[]{:S(2)}) copy-start(s32[2,1024]{1,0:T(2,128)} %param.7) | copy-start | bytes 24580
  4.0 14.7 %copy-start = (f32[4,8,8]{2,1,0:T(8,128)S(1)}, f32[4,8,8]{2,1,0:T(8,128)}, u32[]{:S(2)}) copy-start(f32[4,8,8]{2,1,0:T(8,128)} %onsite_ref.1) | copy-start | bytes 3076
  4.1 14.7 %copy-start.1 = (f32[8,8]{1,0:T(8,128)S(1)}, f32[8,8]{1,0:T(8,128)}, u32[]{:S(2)}) copy-start(f32[8,8]{1,0:T(8,128)} %kx_ref.1) | copy-start | bytes 772
  4.1 14.7 %copy-start.2 = (f32[8,8]{1,0:T(8,128)S(1)}, f32[8,8]{1,0:T(8,128)}, u32[]{:S(2)}) copy-start(f32[8,8]{1,0:T(8,128)} %ky_ref.1) | copy-start | bytes 772
  4.1 14.7 %copy-start.3 = (f32[4,8]{1,0:T(4,128)S(1)}, f32[4,8]{1,0:T(4,128)}, u32[]{:S(2)}) copy-start(f32[4,8]{1,0:T(4,128)} %hop_ref.1) | copy-start | bytes 388
  4.1 56.1 %all-to-all-start = ((f32[32,128,128]{2,1,0:T(8,128)}), f32[32,128,128]{2,1,0:T(8,128)S(1)}, u32[]{:S(2)}, u32[]{:S(2)}) async-start(f32[32,128,128]{2,1,0:T(8,128)} %pack.1), calls=%async_computation | async-start | bytes 4194304 | tf_op jit(solution)/shard_map/all_to_all | solution.py:601
  60.2 8.1 %collective-permute-start = (f32[32,16,128]{2,1,0:T(8,128)S(1)}, f32[32,16,128]{2,1,0:T(8,128)S(1)}, u32[]{:S(2)}, u32[]{:S(2)}) collective-permute-start(f32[32,16,128]{2,1,0:T(8,128)S(1)} %slice.12), channel_id=1, source_target_pairs={{0,1},{1,2},{2,3},{3,4},{4,5},{5,6},{6,7},{7,8},{8,9},{9,10},{10,1... | collective-permute-start | bytes 786440 | tf_op jit(solution)/shard_map/ppermute | solution.py:407
  61.8 6.5 %collective-permute-start.1 = (f32[32,5,4,128]{3,2,1,0:T(4,128)S(1)}, f32[32,5,4,128]{3,2,1,0:T(4,128)S(1)}, u32[]{:S(2)}, u32[]{:S(2)}) collective-permute-start(f32[32,5,4,128]{3,2,1,0:T(4,128)S(1)} %slice.13), channel_id=1, source_target_pairs={{1,0},{2,1},{3,2},{4,3},{5,4},{6,5},{7,6},{8,7},{9,8},{10,9},{11,1... | collective-permute-start | bytes 983048 | tf_op jit(solution)/shard_map/ppermute | solution.py:406
  72.2 16.6 %all-to-all-start.1 = ((f32[160,2,128]{2,1,0:T(2,128)}), f32[160,2,128]{2,1,0:T(2,128)S(1)}, u32[]{:S(2)}, u32[]{:S(2)}) async-start(f32[160,2,128]{2,1,0:T(2,128)} %bitcast.6), calls=%async_computation.1 | async-start | bytes 327680 | tf_op jit(solution)/shard_map/all_to_all | solution.py:601
  104.6 14.2 %all-to-all-start.3 = ((f32[160,2,128]{2,1,0:T(2,128)}), f32[160,2,128]{2,1,0:T(2,128)S(1)}, u32[]{:S(2)}, u32[]{:S(2)}) async-start(f32[160,2,128]{2,1,0:T(2,128)} %bitcast.12), calls=%async_computation.3 | async-start | bytes 327680 | tf_op jit(solution)/shard_map/all_to_all | solution.py:601
  118.7 54.6 %all-to-all-start.4 = ((f32[32,128,128]{2,1,0:T(8,128)}), f32[32,128,128]{2,1,0:T(8,128)S(1)}, u32[]{:S(2)}, u32[]{:S(2)}) async-start(f32[32,128,128]{2,1,0:T(8,128)} %get-tuple-element.35), calls=%async_computation.4 | async-start | bytes 4194304 | tf_op jit(solution)/shard_map/all_to_all | solution.py:601

commit v9 on v8

--- a/solution.py
+++ b/solution.py
@@ -372,6 +372,8 @@
     for ref in (ah, al, bh, bl):
         ref[0:EDGE, :] = zero
         ref[pairs * PAIR + EDGE :, :] = zero
+    for ref in (bh, bl):
+        ref[(pairs - 1) * PAIR + EDGE : pairs * PAIR + EDGE, :] = jnp.zeros((PAIR, 256), jnp.bfloat16)
     for pair in range(OWN_PAIRS[0]):
         ingest(lambda source, pair=pair: left_ref[source, 8 * pair : 8 * pair + 8, :], pair, fa, ah, al)
     for pair in range(OWN_PAIRS[1], pairs):
@@ -382,7 +384,7 @@
             return rows if count == 8 else jnp.concatenate([rows, jnp.zeros_like(rows)], axis=0)
 
         ingest(load, pair, fa, ah, al)
-    reach = ((0, pairs), (1, pairs - 1), (1, pairs - 1), (2, pairs - 2))
+    reach = ((0, pairs - 1), (1, pairs - 1), (1, pairs - 2), (2, pairs - 2))
     for count, step in enumerate(steps(ch_ref, cl_ref, *fields)):
         low, high = OWN_PAIRS[0] + 1 + count, OWN_PAIRS[1] - 1 - count
         for pair in list(range(reach[count][0], low)) + list(range(high, reach[count][1])):

time: 177 us -> 176 us (level)
  no operation moved by 1% of the time
where the time goes in v9:
time: 176 us
  waiting for transfers between devices  85.3 us (48%)
  Pallas kernels  39.7 us (23%)
  starting transfers between devices  26.8 us (15%)
  blocking collectives  21.9 us (12%)
    all_to_all x4, waiting for transfers between devices, swap(): return lax.all_to_all(rows, ALL, 0, 0, tiled=True).reshape(parts.shape)  85.3 us
    all_to_all x4, starting transfers between devices, swap(): return lax.all_to_all(rows, ALL, 0, 0, tiled=True).reshape(parts.shape)  23.7 us
    all_to_all x1, blocking collectives, swap(): return lax.all_to_all(rows, ALL, 0, 0, tiled=True).reshape(parts.shape)  14.7 us
    pallas_call x1, Pallas kernels, basis(): pl.pallas_call(functools.partial(basis_kernel, entries), out_shape=(jax.S...  11.6 us
    all_gather x1, blocking collectives, fast(): lax.all_gather((region + 1).astype(jnp.float32), 'slab', axis=0, tiled=True)  7.22 us
    pallas_call x1, Pallas kernels, coefficients(): pl.pallas_call(coef_kernel, out_shape=(shape, shape), compiler_params=VME...  6.31 us
    pallas_call x1, Pallas kernels, moment_of(): pl.pallas_call(moment_kernel, out_shape=jax.ShapeDtypeStruct((PACKED, LAN...  5.63 us
    pallas_call x1, Pallas kernels, interior(): pl.pallas_call(interior_kernel, out_shape=(field,) * 2 + (half,) * 4 + (b...  4.95 us
  transfers between devices with their start and end apart: 6, of which 3 were waited for; matrix products, arithmetic and copies ran while one was open for 0% of the time, Pallas kernels for 17%

profile of v9, /device:TPU:0, one launch (start us, length us, event | category | flops | bytes accessed | tf_op | source)
XLA Modules:
  0.0 175.9 jit_solution(7487330896542193642)
XLA Ops:
  0.6 3.4 %pack.1 = f32[32,128,128]{2,1,0:T(8,128)} custom-call(f32[256,16,128]{2,1,0:T(8,128)} %bitcast.30), custom_call_target="tpu_custom_call" | custom-call | tf_op jit(solution)/shard_map/pack/pallas_call | solution.py:96
  4.0 0.0 copy-start.4
  4.0 0.0 copy-start
  4.1 0.0 copy-start.1
  4.1 0.0 copy-start.2
  4.1 0.0 copy-start.3
  4.1 7.3 %all-to-all-start = ((f32[32,128,128]{2,1,0:T(8,128)}), f32[32,128,128]{2,1,0:T(8,128)S(1)}, u32[]{:S(2)}, u32[]{:S(2)}) async-start(f32[32,128,128]{2,1,0:T(8,128)} %pack.1), calls=%async_computation | async-start | bytes 4194304 | tf_op jit(solution)/shard_map/all_to_all | solution.py:603
  11.4 7.2 %all-gather = f32[4,2,1024]{2,1,0:T(2,128)S(1)} all-gather(f32[1,2,1024]{2,1,0:T(2,128)S(1)} %convert_bitcast_fusion), channel_id=1, replica_groups=mesh['blk'=8,'slab'=4] {'slab'}, dimensions={0}, use_global_device_ids=true | all-gather | bytes 40960 | tf_op jit(solution)/shard_map/all_gather | solution.py:639
  18.7 0.1 pad_dynamic-slice_fusion.reg_ref
  18.8 6.3 %coefficients.1 = (bf16[21,128,256]{2,1,0:T(8,128)(2,1)}, bf16[21,128,256]{2,1,0:T(8,128)(2,1)}) custom-call(f32[8,128]{1,0:T(8,128)S(1)} %pad_dynamic-slice_fusion.reg_ref, f32[4,8,8]{2,1,0:T(8,128)S(1)} %copy-done, f32[4,8]{1,0:T(4,128)S(1)} %copy-done.3, f32[8,8]{1,0:T(8,128)S(1)} %copy-done.1, f32[8,8]{1,0:T(8,128)S(1)} %copy-done.2), custom_call_target="tpu_custom_call" | custom-call | tf_op jit(solution)/shard_map/coefficients/pallas_call | solution.py:223
  25.1 35.1 %all-to-all-done.r_ref = f32[32,128,128]{2,1,0:T(8,128)S(1)} async-done(((f32[32,128,128]{2,1,0:T(8,128)}), f32[32,128,128]{2,1,0:T(8,128)S(1)}, u32[]{:S(2)}, u32[]{:S(2)}) %all-to-all-start) | async-done | bytes 2097184 | tf_op jit(solution)/shard_map/all_to_all | solution.py:603
  60.2 1.6 collective-permute-start
  61.8 1.5 collective-permute-start.1
  63.3 4.9 %interior.1 = (f32[2688,256]{1,0:T(8,128)S(1)}, f32[2688,256]{1,0:T(8,128)S(1)}, bf16[2816,256]{1,0:T(8,128)(2,1)S(1)}, bf16[2816,256]{1,0:T(8,128)(2,1)S(1)}, b...) custom-call(f32[32,128,128]{2,1,0:T(8,128)S(1)} %all-to-all-done.r_r, ...), custom_call_target="tpu_custom_call" | custom-call | flops 8000000000 | bytes 20000000 | tf_op jit(solution)/shard_map/interior/pallas_call | solution.py:341
  68.2 0.0 collective-permute-done.left_ref
  68.3 0.0 collective-permute-done.1
  68.3 3.8 %edges.1 = (bf16[2112,256]{1,0:T(8,128)(2,1)}, bf16[2112,256]{1,0:T(8,128)(2,1)}, f32[320,128]{1,0:T(8,128)}, f32[2688,256]{1,0:T(8,128)S(1)}, f32[2688,256]{1,0...) custom-call(f32[32,16,128]{2,1,0:T(8,128)S(1)} %collective-permute-d, ...), custom_call_target="tpu_custom_call", output_to_operand_aliasing={{3}: (2, {}), {4}: (3, {}), {5}: (4, {}), {6}: (5, {}), {7}... | custom-call | tf_op jit(solution)/shard_map/edges/pallas_call | solution.py:413
  72.1 8.0 %all-to-all-start.1 = ((f32[160,2,128]{2,1,0:T(2,128)}), f32[160,2,128]{2,1,0:T(2,128)S(1)}, u32[]{:S(2)}, u32[]{:S(2)}) async-start(f32[160,2,128]{2,1,0:T(2,128)} %bitcast.6), calls=%async_computation.1 | async-start | bytes 327680 | tf_op jit(solution)/shard_map/all_to_all | solution.py:603
  80.1 5.6 %moment.1 = f32[320,128]{1,0:T(8,128)S(1)} custom-call(bf16[2112,256]{1,0:T(8,128)(2,1)} %get-tuple-element.32.vh_ref.vh_hbm, bf16[2112,256]{1,0:T(8,128)(2,1)} %get-tuple-element.33.vl_ref.vl_hbm, bf16[21,128,256]{2,1,0:T(8,128)(2,1)} %get-tuple-element.20.ch_hbm.ch_ref, bf16[21,128,256]{2,1,0:T(8,128)(2,1)} %get-tuple-element.21.cl_hbm.cl_ref, ...), custom_call_target="tpu_custom_call" | custom-call | flops 4000000000 | bytes 10000000 | tf_op jit(solution)/shard_map/moment/pallas_call | solution.py:454
  85.8 2.9 %all-to-all-done.1 = f32[160,2,128]{2,1,0:T(2,128)S(1)} async-done(((f32[160,2,128]{2,1,0:T(2,128)}), f32[160,2,128]{2,1,0:T(2,128)S(1)}, u32[]{:S(2)}, u32[]{:S(2)}) %all-to-all-start.1) | async-done | bytes 163872 | tf_op jit(solution)/shard_map/all_to_all | solution.py:603
  88.7 0.1 reduce_sum.18
  88.8 0.1 pad_maximum_fusion
  89.0 14.7 %all_to_all.25 = f32[320,2,128]{2,1,0:T(2,128)S(1)} all-to-all(f32[320,2,128]{2,1,0:T(2,128)S(1)} %bitcast.32), channel_id=1, replica_groups=mesh['blk'=8,'slab'=4] {'blk','slab'}, dimensions={0} | all-to-all | bytes 655360 | tf_op jit(solution)/shard_map/all_to_all | solution.py:603
  103.7 0.1 slice_reduce_fusion
  103.8 0.7 broadcast_in_dim.5
  104.5 2.6 %all-to-all-start.3 = ((f32[160,2,128]{2,1,0:T(2,128)}), f32[160,2,128]{2,1,0:T(2,128)S(1)}, u32[]{:S(2)}, u32[]{:S(2)}) async-start(f32[160,2,128]{2,1,0:T(2,128)} %bitcast.12), calls=%async_computation.3 | async-start | bytes 327680 | tf_op jit(solution)/shard_map/all_to_all | solution.py:603
  107.0 11.6 %basis.1 = (f32[256,256]{1,0:T(8,128)S(1)}, f32[32,128,128]{2,1,0:T(8,128)}) custom-call(f32[640,128]{1,0:T(8,128)S(1)} %bitcast.26, bf16[2112,256]{1,0:T(8,128)(2,1)} %get-tuple-element.32.vh_ref.vh_hbm, bf16[2112,256]{1,0:T(8,128)(2,1)} %get-tuple-element.33.vl_ref.vl_hbm), custom_call_target="tpu_custom_call" | custom-call | flops 4000000000 | bytes 20000000 | tf_op jit(solution)/shard_map/basis/pallas_call | solution.py:573
  118.6 0.0 all-to-all-done.3
  118.6 5.8 %all-to-all-start.4 = ((f32[32,128,128]{2,1,0:T(8,128)}), f32[32,128,128]{2,1,0:T(8,128)S(1)}, u32[]{:S(2)}, u32[]{:S(2)}) async-start(f32[32,128,128]{2,1,0:T(8,128)} %get-tuple-element.35), calls=%async_computation.4 | async-start | bytes 4194304 | tf_op jit(solution)/shard_map/all_to_all | solution.py:603
  124.5 1.5 project.1
  126.0 47.3 %all-to-all-done.4 = f32[32,128,128]{2,1,0:T(8,128)S(1)} async-done(((f32[32,128,128]{2,1,0:T(8,128)}), f32[32,128,128]{2,1,0:T(8,128)S(1)}, u32[]{:S(2)}, u32[]{:S(2)}) %all-to-all-start.4) | async-done | bytes 2097184 | tf_op jit(solution)/shard_map/all_to_all | solution.py:603
  173.3 2.5 %unpack.1 = f32[32,128,128]{2,1,0:T(8,128)} custom-call(f32[4096,128]{1,0:T(8,128)S(1)} %bitcast.23), custom_call_target="tpu_custom_call" | custom-call | tf_op jit(solution)/shard_map/unpack/pallas_call | solution.py:132
  (10 shorter events, 0.1 us)
Async XLA Ops:
  4.0 7.4 %copy-start.4 = (s32[2,1024]{1,0:T(2,128)S(1)}, s32[2,1024]{1,0:T(2,128)}, u32[]{:S(2)}) copy-start(s32[2,1024]{1,0:T(2,128)} %param.7) | copy-start | bytes 24580
  4.0 14.7 %copy-start = (f32[4,8,8]{2,1,0:T(8,128)S(1)}, f32[4,8,8]{2,1,0:T(8,128)}, u32[]{:S(2)}) copy-start(f32[4,8,8]{2,1,0:T(8,128)} %onsite_ref.1) | copy-start | bytes 3076
  4.1 14.7 %copy-start.1 = (f32[8,8]{1,0:T(8,128)S(1)}, f32[8,8]{1,0:T(8,128)}, u32[]{:S(2)}) copy-start(f32[8,8]{1,0:T(8,128)} %kx_ref.1) | copy-start | bytes 772
  4.1 14.7 %copy-start.2 = (f32[8,8]{1,0:T(8,128)S(1)}, f32[8,8]{1,0:T(8,128)}, u32[]{:S(2)}) copy-start(f32[8,8]{1,0:T(8,128)} %ky_ref.1) | copy-start | bytes 772
  4.1 14.7 %copy-start.3 = (f32[4,8]{1,0:T(4,128)S(1)}, f32[4,8]{1,0:T(4,128)}, u32[]{:S(2)}) copy-start(f32[4,8]{1,0:T(4,128)} %hop_ref.1) | copy-start | bytes 388
  4.1 56.1 %all-to-all-start = ((f32[32,128,128]{2,1,0:T(8,128)}), f32[32,128,128]{2,1,0:T(8,128)S(1)}, u32[]{:S(2)}, u32[]{:S(2)}) async-start(f32[32,128,128]{2,1,0:T(8,128)} %pack.1), calls=%async_computation | async-start | bytes 4194304 | tf_op jit(solution)/shard_map/all_to_all | solution.py:603
  60.2 8.1 %collective-permute-start = (f32[32,16,128]{2,1,0:T(8,128)S(1)}, f32[32,16,128]{2,1,0:T(8,128)S(1)}, u32[]{:S(2)}, u32[]{:S(2)}) collective-permute-start(f32[32,16,128]{2,1,0:T(8,128)S(1)} %slice.12), channel_id=1, source_target_pairs={{0,1},{1,2},{2,3},{3,4},{4,5},{5,6},{6,7},{7,8},{8,9},{9,10},{10,1... | collective-permute-start | bytes 786440 | tf_op jit(solution)/shard_map/ppermute | solution.py:409
  61.8 6.5 %collective-permute-start.1 = (f32[32,5,4,128]{3,2,1,0:T(4,128)S(1)}, f32[32,5,4,128]{3,2,1,0:T(4,128)S(1)}, u32[]{:S(2)}, u32[]{:S(2)}) collective-permute-start(f32[32,5,4,128]{3,2,1,0:T(4,128)S(1)} %slice.13), channel_id=1, source_target_pairs={{1,0},{2,1},{3,2},{4,3},{5,4},{6,5},{7,6},{8,7},{9,8},{10,9},{11,1... | collective-permute-start | bytes 983048 | tf_op jit(solution)/shard_map/ppermute | solution.py:408
  72.1 16.6 %all-to-all-start.1 = ((f32[160,2,128]{2,1,0:T(2,128)}), f32[160,2,128]{2,1,0:T(2,128)S(1)}, u32[]{:S(2)}, u32[]{:S(2)}) async-start(f32[160,2,128]{2,1,0:T(2,128)} %bitcast.6), calls=%async_computation.1 | async-start | bytes 327680 | tf_op jit(solution)/shard_map/all_to_all | solution.py:603
  104.5 14.2 %all-to-all-start.3 = ((f32[160,2,128]{2,1,0:T(2,128)}), f32[160,2,128]{2,1,0:T(2,128)S(1)}, u32[]{:S(2)}, u32[]{:S(2)}) async-start(f32[160,2,128]{2,1,0:T(2,128)} %bitcast.12), calls=%async_computation.3 | async-start | bytes 327680 | tf_op jit(solution)/shard_map/all_to_all | solution.py:603
  118.6 54.6 %all-to-all-start.4 = ((f32[32,128,128]{2,1,0:T(8,128)}), f32[32,128,128]{2,1,0:T(8,128)S(1)}, u32[]{:S(2)}, u32[]{:S(2)}) async-start(f32[32,128,128]{2,1,0:T(8,128)} %get-tuple-element.35), calls=%async_computation.4 | async-start | bytes 4194304 | tf_op jit(solution)/shard_map/all_to_all | solution.py:603
